TPU v7x, 32 devices: a whole 2x2x4 slice. The times are simulated.
32 devices in a mesh: group: 8 (over y, x, core), expert: 4 (over z).
Axes of the slice: x: 2, y: 2, z: 4, core: 2. Of those that a mesh axis runs over, the one named last changes fastest.
Arguments:
- tokens: bfloat16 [8192, 1024], P(('group', 'expert')), may hold values from -6 to 6
- lengths: int32 [8], P('group'), may hold values from 256 to 1024, as said below
- routes: int32 [8192, 8], P(('group', 'expert')), may hold values from 0 to 31, all different within a row; in each aligned block of 256 rows (0 to 255, 256 to 511, ...) at most 96 rows name the same one
- norm_gain1: bfloat16 [1024], P('expert'), may hold values from 0.5 to 1.5
- w_query: bfloat16 [1024, 1024], P('expert'), may hold values from -0.375 to 0.375
- key_projection: bfloat16 [1024, 512], P('expert'), may hold values from -0.1875 to 0.1875
- value_projection: bfloat16 [1024, 512], P('expert'), may hold values from -0.1875 to 0.1875
- w_out: bfloat16 [1024, 1024], P('expert'), may hold values from -1.5 to 1.5
- norm_gain2: bfloat16 [1024], P('expert'), may hold values from 0.5 to 1.5
- w_router: bfloat16 [1024, 32], P('expert'), may hold values from -0.09375 to 0.09375
- w_gate: bfloat16 [32, 1024, 512], P('expert'), may hold values from -0.1875 to 0.1875
- w_up: bfloat16 [32, 1024, 512], P('expert'), may hold values from -0.1875 to 0.1875
- w_down: bfloat16 [32, 512, 1024], P('expert'), may hold values from -1 to 1
- cotangent: bfloat16 [8192, 1024], P(('group', 'expert')), may hold values from -6 to 6
Outputs:
- mixed: bfloat16 [8192, 1024], P(('group', 'expert'))
- grad_tokens: float32 [8192, 1024], P(('group', 'expert'))
- grad_gain1: float32 [1024], P('expert')
- grad_query: float32 [1024, 1024], P('expert')
- grad_key: float32 [1024, 512], P('expert')
- grad_value: float32 [1024, 512], P('expert')
- grad_out: float32 [1024, 1024], P('expert')
- grad_gain2: float32 [1024], P('expert')
- grad_router: float32 [1024, 32], P('expert')
- grad_gate: float32 [32, 1024, 512], P('expert')
- grad_up: float32 [32, 1024, 512], P('expert')
- grad_down: float32 [32, 512, 1024], P('expert')
Inputs may be any that keep to these rules, and one draw needn't show every extreme that they name: The first lengths[s] slots of sequence s are valid; one sequence fills all 1024 slots and one holds 256. `routes`: a slot's 8 experts differ; among the rows of one device at most 96 name one expert, and in every draw some expert is named by exactly 96 of them.
All inputs are finite; a program needn't handle non-finite values.
Results may differ from a plain program's by a relative error of at most 0.028.
Values may be sent and summed in bfloat16 or wider, within the bound.
A program may use at most 256 MiB of HBM per device.

v0:
```python
import functools

import jax
import jax.numpy as jnp
from jax import lax
from jax.experimental import pallas as pl
from jax.experimental.pallas import tpu as pltpu
from jax.sharding import PartitionSpec as P

D = 1024
QUERY_HEADS = 16
KEY_VALUE_HEADS = 8
HEAD_DIMENSION = 64
EXPERTS = 32
TOP = 8
FF = 512
LANES = 128
STAGES = 4

EPSILON = 1e-05
NEGATIVE_LARGE = -1e30
BF = jnp.bfloat16
F32 = jnp.float32


def rotary_tables(positions, head_size):
    half_width = head_size // 2
    frequency = 10000.0 ** (-2.0 * jnp.arange(half_width).astype(F32) / head_size)
    angles = positions.astype(F32)[:, None] * frequency[None, :]
    return (jnp.cos(angles)[:, None, :], jnp.sin(angles)[:, None, :])


def apply_rotation(tensor_in, cosine_lookup, sine_lookup):
    half_width = tensor_in.shape[-1] // 2
    first_half = tensor_in[..., :half_width]
    second_half = tensor_in[..., half_width:]
    return jnp.concatenate(
        [
            first_half * cosine_lookup - second_half * sine_lookup,
            second_half * cosine_lookup + first_half * sine_lookup,
        ],
        axis=-1,
    )


def dot(a, b):
    return jnp.dot(a, b, preferred_element_type=F32)


def dot_nt(a, b):
    return lax.dot_general(a, b, (((1,), (1,)), ((), ())), preferred_element_type=F32)


def dot_tn(a, b):
    return lax.dot_general(a, b, (((0,), (0,)), ((), ())), preferred_element_type=F32)


MESH = pl.DeviceIdType.MESH
ANY = pl.BlockSpec(memory_space=pl.ANY)
IN_VMEM = pl.BlockSpec(memory_space=pltpu.VMEM)


def remote(source, target, send, receive, device):
    return pltpu.make_async_remote_copy(
        src_ref=source,
        dst_ref=target,
        send_sem=send,
        recv_sem=receive,
        device_id=device,
        device_id_type=MESH,
    )


def greet(devices):
    barrier = pltpu.get_barrier_semaphore()
    count = 0
    for condition, device in devices:
        if condition is None:
            pl.semaphore_signal(barrier, inc=1, device_id=device, device_id_type=MESH)
            count = count + 1
        else:

            @pl.when(condition)
            def _():
                pl.semaphore_signal(barrier, inc=1, device_id=device, device_id_type=MESH)

            count = count + jnp.where(condition, 1, 0)
    pl.semaphore_wait(barrier, count)


def line_gather_kernel(n, count, *refs):
    ins, outs = refs[:count], refs[count : 2 * count]
    local, send, receive = refs[2 * count :]
    group, me = lax.axis_index("group"), lax.axis_index("expert")
    left, right = (group, me - 1), (group, me + 1)
    own = [
        pltpu.make_async_copy(ins[i], outs[i].at[me], local.at[i]) for i in range(count)
    ]
    for copy in own:
        copy.start()
    greet([(me > 0, left), (me < n - 1, right)])

    def hop(i, step, side):
        block = me - step if side == 0 else me + step
        source = ins[i] if step == 0 else outs[i].at[block]
        index = (side, step, i)
        return remote(
            source, outs[i].at[block], send.at[index], receive.at[index], right if side == 0 else left
        )

    def arrival(i, step, side):
        block = me - 1 - step if side == 0 else me + 1 + step
        index = (side, step, i)
        return remote(
            outs[i].at[block], outs[i].at[block], send.at[index], receive.at[index], left if side == 0 else right
        )

    def sends(step, side):
        return (me - step >= 0) & (me < n - 1) if side == 0 else (me + step < n) & (me > 0)

    def arrives(step, side):
        return me - 1 - step >= 0 if side == 0 else me + 1 + step < n

    for step in range(n - 1):
        for side in (0, 1):

            @pl.when(sends(step, side))
            def _():
                for i in range(count):
                    hop(i, step, side).start()

        for side in (0, 1):

            @pl.when(arrives(step, side))
            def _():
                for i in range(count):
                    arrival(i, step, side).wait_recv()

    for step in range(n - 1):
        for side in (0, 1):

            @pl.when(sends(step, side))
            def _():
                for i in range(count):
                    hop(i, step, side).wait_send()

    for copy in own:
        copy.wait()


def line_gather(values, n, collective_id, name):
    count = len(values)
    outs = pl.pallas_call(
        functools.partial(line_gather_kernel, n, count),
        out_shape=[jax.ShapeDtypeStruct((n,) + v.shape, v.dtype) for v in values],
        in_specs=[IN_VMEM] * count,
        out_specs=[ANY] * count,
        scratch_shapes=[
            pltpu.SemaphoreType.DMA((count,)),
            pltpu.SemaphoreType.DMA((2, n - 1, count)),
            pltpu.SemaphoreType.DMA((2, n - 1, count)),
        ],
        compiler_params=pltpu.CompilerParams(collective_id=collective_id, has_side_effects=True),
        cost_estimate=pl.CostEstimate(flops=0, bytes_accessed=100000000, transcendentals=0),
        name=name,
    )(*values)
    return [o.reshape((n * v.shape[0],) + v.shape[1:]) for o, v in zip(outs, values)]


class LineSum:
    def __init__(self, n, part, landing, staging, send, receive):
        self.n, self.part, self.landing, self.staging = n, part, landing, staging
        self.send, self.receive = send, receive
        self.group, self.me = lax.axis_index("group"), lax.axis_index("expert")
        self.rows = part.shape[1]
        self.tile = min(32, self.rows)

    def neighbours(self):
        left, right = (self.group, self.me - 1), (self.group, self.me + 1)
        return [(self.me > 0, left), (self.me < self.n - 1, right)]

    def copy(self, source, step, side):
        index = (side, step)
        device = (self.group, self.me + 1 if side == 0 else self.me - 1)
        return remote(
            source, self.landing.at[index], self.send.at[index], self.receive.at[index], device
        )

    def places(self):
        me, n = self.me, self.n
        for step in range(n - 1):
            for side in (0, 1):
                owner = n - 1 - step if side == 0 else step
                beyond = me < owner if side == 0 else me > owner
                edge = me == 0 if side == 0 else me == n - 1
                yield step, side, owner, beyond, edge

    def start(self):
        for step, side, owner, beyond, edge in self.places():

            @pl.when(beyond & edge)
            def _():
                self.copy(self.part.at[owner], step, side).start()

    def spans(self, body):
        def tile_body(t, carry):
            body(pl.ds(pl.multiple_of(t * self.tile, self.tile), self.tile))
            return carry

        lax.fori_loop(0, self.rows // self.tile, tile_body, 0)

    def forward(self, hop):
        me, n = self.me, self.n
        for side in (0, 1):
            step = hop - me if side == 0 else hop - (n - 1 - me)
            owner = n - 1 - step if side == 0 else step
            inner = me > 0 if side == 0 else me < n - 1
            beyond = me < owner if side == 0 else me > owner

            @pl.when(inner & (step >= 0) & beyond)
            def _():
                self.copy(self.part.at[owner], step, side).wait_recv()

                def add(span):
                    total = self.part[owner, span, :].astype(F32)
                    total = total + self.landing[side, step, span, :].astype(F32)
                    self.staging[side, step, span, :] = total.astype(BF)

                self.spans(add)
                self.copy(self.staging.at[side, step], step, side).start()

    def finish(self, out_ref):
        me, n = self.me, self.n

        @pl.when(me > 0)
        def _():
            self.copy(self.part.at[me], n - 1 - me, 0).wait_recv()

        @pl.when(me < n - 1)
        def _():
            self.copy(self.part.at[me], me, 1).wait_recv()

        def total(span):
            value = self.part[me, span, :].astype(F32)
            from_left = self.landing[0, jnp.minimum(n - 1 - me, n - 2), span, :].astype(F32)
            from_right = self.landing[1, jnp.minimum(me, n - 2), span, :].astype(F32)
            value = value + jnp.where(me > 0, from_left, 0.0)
            value = value + jnp.where(me < n - 1, from_right, 0.0)
            out_ref[span, :] = value.astype(out_ref.dtype)

        self.spans(total)
        for step, side, owner, beyond, edge in self.places():

            @pl.when(beyond)
            def _():
                self.copy(self.part.at[owner], step, side).wait_send()


def line_sum_scratch(n, rows, width):
    return [
        pltpu.VMEM((2, n - 1, rows, width), BF),
        pltpu.VMEM((2, n - 2, rows, width), BF),
        pltpu.SemaphoreType.DMA((2, n - 1)),
        pltpu.SemaphoreType.DMA((2, n - 1)),
    ]


def line_scatter_kernel(n, part_ref, out_ref, *scratch):
    line = LineSum(n, part_ref, *scratch)
    greet(line.neighbours())
    line.start()
    for hop in range(1, n - 1):
        line.forward(hop)
    line.finish(out_ref)


def line_scatter(value, n, dtype, collective_id, name):
    total, width = value.shape
    rows = total // n
    return pl.pallas_call(
        functools.partial(line_scatter_kernel, n),
        out_shape=jax.ShapeDtypeStruct((rows, width), dtype),
        in_specs=[IN_VMEM],
        out_specs=IN_VMEM,
        scratch_shapes=line_sum_scratch(n, rows, width),
        compiler_params=pltpu.CompilerParams(collective_id=collective_id, has_side_effects=True),
        cost_estimate=pl.CostEstimate(flops=0, bytes_accessed=100000000, transcendentals=0),
        name=name,
    )(value.reshape(n, rows, width))


def plane_position():
    group, me = lax.axis_index("group"), lax.axis_index("expert")
    c, x, y = group % 2, (group // 2) % 2, (group // 4) % 2
    by_c, by_x, by_y = (group + 1 - 2 * c, me), (group + 2 - 4 * x, me), (group + 4 - 8 * y, me)
    return group, me, (y, x, c), (by_y, by_x, by_c)


def weights_kernel(n, pieces, widths, *refs):
    wq, wk, wv, wo, small, extra = refs[:6]
    outs, extra_out, owns = refs[6:9], refs[9], refs[10:13]
    load, store, zsend, zrecv, psend, precv, csend, crecv, xsend, xrecv = refs[13:]
    group, me, (y, x, c), (by_y, by_x, by_c) = plane_position()
    left, right = (group, me - 1), (group, me + 1)
    eighth = owns[0].shape[0]
    span = pl.ds(pl.multiple_of((y * 4 + x * 2 + c) * eighth, eighth), eighth)
    query_width, key_width = wq.shape[1], wk.shape[1]
    targets = (
        owns[0].at[:, :query_width],
        owns[0].at[:, query_width : query_width + key_width],
        owns[0].at[:, query_width + key_width :],
        owns[1],
        owns[2],
    )
    loads = [
        pltpu.make_async_copy(source.at[span, :], target, load.at[i])
        for i, (source, target) in enumerate(zip((wq, wk, wv, wo, small), targets))
    ]
    for copy in loads:
        copy.start()
    for copy in loads:
        copy.wait()
    stores = [
        pltpu.make_async_copy(owns[i], outs[i].at[me, y, x, c], store.at[i]) for i in range(3)
    ]
    stores.append(pltpu.make_async_copy(extra, extra_out.at[me], store.at[3]))
    for copy in stores:
        copy.start()
    greet(
        [(me > 0, left), (me < n - 1, right), (None, by_c), (None, by_x), (None, by_y)]
    )

    def hop(i, step, side):
        block = me - step if side == 0 else me + step
        source = owns[i] if step == 0 else outs[i].at[block, y, x, c]
        index = (side, step, i)
        return remote(
            source,
            outs[i].at[block, y, x, c],
            zsend.at[index],
            zrecv.at[index],
            right if side == 0 else left,
        )

    def sends(step, side):
        return (me - step >= 0) & (me < n - 1) if side == 0 else (me + step < n) & (me > 0)

    def extra_hop(step, side):
        block = me - step if side == 0 else me + step
        source = extra if step == 0 else extra_out.at[block]
        return remote(
            source,
            extra_out.at[block],
            xsend.at[side, step],
            xrecv.at[side, step],
            right if side == 0 else left,
        )

    def first(slot, block, p):
        i, start, width, along_x = pieces[p]
        spot = outs[i].at[block, y, x, c, :, start : start + width]
        source = owns[i].at[:, start : start + width] if slot == 0 else spot
        index = (0, slot, p)
        return remote(source, spot, psend.at[index], precv.at[index], by_x if along_x else by_y)

    def second(slot, block, p):
        i, start, width, along_x = pieces[p]
        columns = slice(start, start + width)
        if along_x:
            spot = outs[i].at[block, y, :, c, :, columns]
        else:
            spot = outs[i].at[block, :, x, c, :, columns]
        index = (1, slot, p)
        return remote(spot, spot, psend.at[index], precv.at[index], by_y if along_x else by_x)

    def third(slot, block, i):
        spot = outs[i].at[block, :, :, c]
        index = (slot, i)
        return remote(spot, spot, csend.at[index], crecv.at[index], by_c)

    def held(step):
        if step == 0:
            return [(0, me, me >= 0)]
        return [(step, me - step, me - step >= 0), (n - 1 + step, me + step, me + step < n)]

    count = len(pieces)
    for step in range(n + 2):
        if step < n:
            for slot, block, there in held(step):

                @pl.when(there)
                def _():
                    if step > 0:
                        side = 0 if slot < n else 1
                        for i in range(3):
                            hop(i, step - 1, side).wait_recv()
                    for p in range(count):
                        first(slot, block, p).start()

            if step < n - 1:
                for side in (0, 1):

                    @pl.when(sends(step, side))
                    def _():
                        for i in range(3):
                            hop(i, step, side).start()

        if 1 <= step < n + 1:
            if step == 1:
                for copy in stores:
                    copy.wait()
            for slot, block, there in held(step - 1):

                @pl.when(there)
                def _():
                    for p in range(count):
                        first(slot, block, p).wait_recv()
                    for p in range(count):
                        second(slot, block, p).start()

        if step >= 2:
            for slot, block, there in held(step - 2):

                @pl.when(there)
                def _():
                    for p in range(count):
                        second(slot, block, p).wait_recv()
                    for i in range(3):
                        third(slot, block, i).start()

            for side in (0, 1):
                if step > 2:

                    @pl.when(me - step + 2 >= 0 if side == 0 else me + step - 2 < n)
                    def _():
                        extra_hop(step - 3, side).wait_recv()

                if step < n + 1:

                    @pl.when(sends(step - 2, side))
                    def _():
                        extra_hop(step - 2, side).start()

    for step in range(n):
        for slot, block, there in held(step):

            @pl.when(there)
            def _():
                for p in range(count):
                    first(slot, block, p).wait_send()
                    second(slot, block, p).wait_send()
                for i in range(3):
                    third(slot, block, i).wait()

        if step < n - 1:
            for side in (0, 1):

                @pl.when(sends(step, side))
                def _():
                    for i in range(3):
                        hop(i, step, side).wait_send()
                    extra_hop(step, side).wait_send()


def path_pieces(query_width, key_width, out_width, small_width):
    half = (query_width + 2 * key_width + out_width) // 2
    return (
        (0, 0, half, True),
        (0, half, query_width + 2 * key_width - half, False),
        (1, 0, out_width, False),
        (2, 0, small_width, True),
    )


def gather_weights(wq, wk, wv, wo, small, extra, n, collective_id):
    rows = wq.shape[0]
    eighth = rows // 8
    widths = (wq.shape[1] + wk.shape[1] + wv.shape[1], wo.shape[1], small.shape[1])
    pieces = path_pieces(wq.shape[1], wk.shape[1], wo.shape[1], small.shape[1])
    outs = pl.pallas_call(
        functools.partial(weights_kernel, n, pieces, widths),
        out_shape=[jax.ShapeDtypeStruct((n, 2, 2, 2, eighth, w), BF) for w in widths]
        + [jax.ShapeDtypeStruct((n,) + extra.shape, BF)],
        in_specs=[ANY] * 5 + [IN_VMEM],
        out_specs=[ANY] * 4,
        scratch_shapes=[pltpu.VMEM((eighth, w), BF) for w in widths]
        + [
            pltpu.SemaphoreType.DMA((5,)),
            pltpu.SemaphoreType.DMA((4,)),
            pltpu.SemaphoreType.DMA((2, n - 1, 3)),
            pltpu.SemaphoreType.DMA((2, n - 1, 3)),
            pltpu.SemaphoreType.DMA((2, 2 * n - 1, 4)),
            pltpu.SemaphoreType.DMA((2, 2 * n - 1, 4)),
            pltpu.SemaphoreType.DMA((2 * n - 1, 3)),
            pltpu.SemaphoreType.DMA((2 * n - 1, 3)),
            pltpu.SemaphoreType.DMA((2, n - 1)),
            pltpu.SemaphoreType.DMA((2, n - 1)),
        ],
        compiler_params=pltpu.CompilerParams(collective_id=collective_id, has_side_effects=True),
        cost_estimate=pl.CostEstimate(flops=0, bytes_accessed=100000000, transcendentals=0),
        name="gather_weights",
    )(wq, wk, wv, wo, small, extra)
    weights = [o.reshape(n * rows, w) for o, w in zip(outs, widths)]
    return weights + [outs[3].reshape(-1, extra.shape[1])]


def reduce_kernel(n, pieces, *refs):
    (
        grad_q_ref,
        grad_kv_ref,
        tokens_ref,
        gain_ref,
        weight_ref,
        cosine_ref,
        sine_ref,
        mixed_ref,
        grad_attn_ref,
        grad_residual_ref,
        router_ref,
        gain_two_ref,
        y_part,
    ) = refs[:13]
    outs, y_out, grad_tokens_ref = refs[13:15], refs[15], refs[16]
    ins, grad_pre_ref = refs[17:20], refs[20]
    refs = refs[21:]
    pair, one, two, landing, staging = refs[:2], refs[2:4], refs[4:6], refs[6:8], refs[8:10]
    csend, crecv, psend, precv, zsend, zrecv, gsend, grecv = refs[10:18]
    line = LineSum(n, y_part, *refs[18:])
    group, me, (y, x, c), (by_y, by_x, by_c) = plane_position()
    left, right = (group, me - 1), (group, me + 1)
    eighth = pair[0].shape[3]
    greet(
        [(me > 0, left), (me < n - 1, right), (None, by_c), (None, by_x), (None, by_y)]
    )

    places, ends = [], [0, 0]
    for array, start, width, along_x in pieces:
        path = 0 if along_x else 1
        places.append((array, start, width, path, ends[path]))
        ends[path] += width

    def swap(p):
        array, start, width, path, at = places[p]
        return remote(
            ins[array].at[:, :, :, 1 - c, :, start : start + width],
            pair[path].at[:, :, :, :, at : at + width],
            csend.at[p],
            crecv.at[p],
            by_c,
        )

    line.start()
    D_rows = weight_ref.shape[0]
    query_width = grad_q_ref.shape[1]
    key_width = (weight_ref.shape[1] - query_width) // 2

    def put(array, columns, value):
        ins[array][:, :, :, :, :, columns] = value.astype(BF).reshape(
            ins[array].shape[:5] + (value.shape[1],)
        )

    tile = 4 * LANES
    for start in range(0, grad_attn_ref.shape[1], tile):
        columns = slice(start, start + tile)
        put(1, columns, dot_tn(mixed_ref[...], grad_attn_ref[:, columns]))
    swap(2).start()
    unit, inverse = normed(tokens_ref)
    gain = gain_ref[...]
    first_norm = (unit * gain).astype(BF)
    cosine, sine = cosine_ref[...], -sine_ref[...]
    for j in range(query_width // LANES):
        columns = slice(j * LANES, (j + 1) * LANES)
        grad_pre_ref[:, columns] = rotate(grad_q_ref[:, columns], cosine, sine).astype(BF)
    for j in range(key_width // LANES):
        start = 2 * j * LANES
        key = grad_kv_ref[:, start : start + LANES].astype(F32)
        at = query_width + j * LANES
        grad_pre_ref[:, at : at + LANES] = rotate(key, cosine, sine).astype(BF)
        at = at + key_width
        grad_pre_ref[:, at : at + LANES] = grad_kv_ref[:, start + LANES : start + 2 * LANES]
    for start in range(0, weight_ref.shape[1], tile):
        columns = slice(start, start + tile)
        put(0, columns, dot_tn(first_norm, grad_pre_ref[:, columns]))
    swap(0).start()
    swap(1).start()
    grad_first = dot_nt(grad_pre_ref[...], weight_ref[...])
    gain_one_row = jnp.sum(grad_first * unit, axis=0, keepdims=True)
    lane = lax.broadcasted_iota(jnp.int32, (LANES, D_rows), 0)
    gains = jnp.where(lane == EXPERTS, gain_one_row, 0.0)
    gains = jnp.where(lane == EXPERTS + 1, gain_two_ref[...], gains)
    put(2, slice(0, LANES), router_ref[...] + gains.T)
    swap(3).start()
    scaled = grad_first * gain
    mean = jnp.mean(scaled * unit, axis=-1, keepdims=True)
    grad_tokens_ref[...] = grad_residual_ref[...] + inverse * (scaled - unit * mean)
    for p in range(len(places)):
        swap(p).wait_recv()
        array, start, width, path, at = places[p]

        def pair_sum(t, carry):
            z, a, b = t // 4, (t // 2) % 2, t % 2
            mine = ins[array][z, a, b, c, :, start : start + width].astype(F32)
            theirs = pair[path][z, a, b, :, at : at + width].astype(F32)
            pair[path][z, a, b, :, at : at + width] = (mine + theirs).astype(BF)
            return carry

        lax.fori_loop(0, 4 * n, pair_sum, 0)

    def first(path):
        source = pair[0].at[:, :, 1 - x] if path == 0 else pair[1].at[:, 1 - y]
        return remote(
            source, one[path], psend.at[0, path], precv.at[0, path], by_x if path == 0 else by_y
        )

    def second(path):
        source = one[path].at[:, 1 - y] if path == 0 else one[path].at[:, 1 - x]
        return remote(
            source, two[path], psend.at[1, path], precv.at[1, path], by_y if path == 0 else by_x
        )

    for path in (0, 1):
        first(path).start()
    line.forward(1)
    for path in (0, 1):
        first(path).wait_recv()

        def first_sum(t, carry):
            z, a = t // 2, t % 2
            mine = pair[0][z, a, x] if path == 0 else pair[1][z, y, a]
            one[path][z, a] = (mine.astype(F32) + one[path][z, a].astype(F32)).astype(BF)
            return carry

        lax.fori_loop(0, 2 * n, first_sum, 0)
        second(path).start()
    for far in range(2, n - 1):
        line.forward(far)
    for path in (0, 1):
        second(path).wait_recv()

        def second_sum(z, carry):
            mine = one[0][z, y] if path == 0 else one[1][z, x]
            two[path][z] = (mine.astype(F32) + two[path][z].astype(F32)).astype(BF)
            return carry

        lax.fori_loop(0, n, second_sum, 0)

    def hop(source, path, step, side):
        index = (path, side, step)
        return remote(
            source,
            landing[path].at[side, step],
            zsend.at[index],
            zrecv.at[index],
            right if side == 0 else left,
        )

    for step in range(n - 1):
        for side in (0, 1):
            owner = n - 1 - step if side == 0 else step
            beyond = me < owner if side == 0 else me > owner
            edge = me == 0 if side == 0 else me == n - 1

            @pl.when(beyond & edge)
            def _():
                for path in (0, 1):
                    hop(two[path].at[owner], path, step, side).start()

    for far in range(1, n - 1):
        for side in (0, 1):
            step = far - me if side == 0 else far - (n - 1 - me)
            owner = n - 1 - step if side == 0 else step
            inner = me > 0 if side == 0 else me < n - 1
            beyond = me < owner if side == 0 else me > owner

            @pl.when(inner & (step >= 0) & beyond)
            def _():
                for path in (0, 1):
                    hop(two[path].at[owner], path, step, side).wait_recv()
                    staging[path][side, step] = (
                        two[path][owner].astype(F32) + landing[path][side, step].astype(F32)
                    ).astype(BF)
                    hop(staging[path].at[side, step], path, step, side).start()

    @pl.when(me > 0)
    def _():
        for path in (0, 1):
            hop(two[path].at[me], path, n - 1 - me, 0).wait_recv()

    @pl.when(me < n - 1)
    def _():
        for path in (0, 1):
            hop(two[path].at[me], path, me, 1).wait_recv()

    for path in (0, 1):
        total = two[path][me].astype(F32)
        from_left = landing[path][0, jnp.minimum(n - 1 - me, n - 2)].astype(F32)
        from_right = landing[path][1, jnp.minimum(me, n - 2)].astype(F32)
        total = total + jnp.where(me > 0, from_left, 0.0)
        total = total + jnp.where(me < n - 1, from_right, 0.0)
        outs[path][y, x, c] = total.astype(BF)

    def spread(path, stage):
        out = outs[path]
        if stage == 2:
            spot, device = out.at[:, :, c], by_c
        elif stage == 0:
            spot, device = out.at[y, x, c], by_x if path == 0 else by_y
        elif path == 0:
            spot, device = out.at[y, :, c], by_y
        else:
            spot, device = out.at[:, x, c], by_x
        return remote(spot, spot, gsend.at[path, stage], grecv.at[path, stage], device)

    for stage in range(3):
        for path in (0, 1):
            spread(path, stage).start()
        if stage == 0:
            line.finish(y_out)
        for path in (0, 1):
            spread(path, stage).wait_recv()

    for path in (0, 1):
        for stage in range(3):
            spread(path, stage).wait_send()
        first(path).wait_send()
        second(path).wait_send()
    for p in range(len(places)):
        swap(p).wait_send()
    for step in range(n - 1):
        for side in (0, 1):
            owner = n - 1 - step if side == 0 else step
            beyond = me < owner if side == 0 else me > owner

            @pl.when(beyond)
            def _():
                for path in (0, 1):
                    hop(two[path].at[owner], path, step, side).wait_send()


def reduce_weights(
    grad_q,
    grad_kv,
    tokens,
    gain,
    weight,
    cosine,
    sine,
    mixed_low,
    grad_attn,
    grad_residual,
    grad_router,
    gain_two_row,
    y_part,
    n,
    collective_id,
):
    rows_all, width_all = weight.shape
    query_width = grad_q.shape[1]
    key_width = (width_all - query_width) // 2
    array_widths = (width_all, grad_attn.shape[1], LANES)
    rows = rows_all // n
    eighth = rows // 8
    pieces = path_pieces(query_width, key_width, grad_attn.shape[1], LANES)
    widths = [sum(p[2] for p in pieces if p[3]), sum(p[2] for p in pieces if not p[3])]
    scratch = [pltpu.VMEM((n, 2, 2, 2, eighth, w), BF) for w in array_widths]
    scratch += [pltpu.VMEM((grad_q.shape[0], width_all), BF)]
    scratch += [pltpu.VMEM((n, 2, 2, eighth, w), BF) for w in widths]
    scratch += [pltpu.VMEM((n, 2, eighth, w), BF) for w in widths]
    scratch += [pltpu.VMEM((n, eighth, w), BF) for w in widths]
    scratch += [pltpu.VMEM((2, n - 1, eighth, w), BF) for w in widths] * 2
    sems = [(4,), (4,), (2, 2), (2, 2), (2, 2, n - 1), (2, 2, n - 1), (2, 3), (2, 3)]
    y_rows = y_part.shape[0] // n
    outs = pl.pallas_call(
        functools.partial(reduce_kernel, n, pieces),
        out_shape=[jax.ShapeDtypeStruct((2, 2, 2, eighth, w), BF) for w in widths]
        + [jax.ShapeDtypeStruct((y_rows, y_part.shape[1]), F32)]
        + [jax.ShapeDtypeStruct(tokens.shape, F32)],
        in_specs=[IN_VMEM] * 13,
        out_specs=[IN_VMEM] * 4,
        scratch_shapes=scratch
        + [pltpu.SemaphoreType.DMA(s) for s in sems]
        + line_sum_scratch(n, y_rows, y_part.shape[1]),
        compiler_params=pltpu.CompilerParams(
            collective_id=collective_id, has_side_effects=True, vmem_limit_bytes=60 * 1024 * 1024
        ),
        cost_estimate=pl.CostEstimate(flops=0, bytes_accessed=100000000, transcendentals=0),
        name="reduce_weights",
    )(
        grad_q,
        grad_kv,
        tokens,
        gain,
        weight,
        cosine,
        sine,
        mixed_low,
        grad_attn,
        grad_residual,
        grad_router,
        gain_two_row,
        y_part.reshape(n, y_rows, y_part.shape[1]),
    )
    first, second = [o.reshape(rows, w) for o, w in zip(outs, widths)]
    cut = pieces[0][2]
    rest = pieces[1][2]
    qkv = jnp.concatenate([first[:, :cut], second[:, :rest]], axis=1)
    return qkv, second[:, rest:], first[:, cut:], outs[2], outs[3]


def plane_tick(step, local):
    tick = jnp.where(step <= 2, step, jnp.where(step < local, (step + 2) // 2, step - 3))
    runs = (step <= 2) | (step >= local) | (step % 2 == 0)
    return tick, runs


def expert_kernel(sizes, plane, *refs):
    blocks, rows, local, capacity = sizes
    x_ref, ct_low_ref, ct_high_ref, router_t_ref, rank_row_ref, rank_col_ref = refs[:6]
    w_gate_ref, w_up_ref, w_down_ref = refs[6:9]
    y_ref, gs_ref, out_gate_ref, out_up_ref, out_down_ref = refs[9:14]
    xs_ref, g_ref, rank_ref, gate_ref, dots_ref, y_sem = refs[14:20]
    refs = refs[20:]
    slots = local * capacity
    step = pl.program_id(0)
    tick, ticks = plane_tick(step, local)
    base = lax.axis_index("expert") * local
    if plane:
        stage_refs, pair_refs, one_refs, two_refs = refs[:3], refs[3:6], refs[6:10], refs[10:14]
        csend, crecv, psend, precv, qsend, qrecv = refs[14:20]
        gs_part = refs[20]
        line = LineSum(blocks, gs_part, *refs[21:])
        _, _, (y, x, c), (by_y, by_x, by_c) = plane_position()
        half = stage_refs[2].shape[4] // 2

        @pl.when(step == 0)
        def _():
            greet([(None, by_c), (None, by_x), (None, by_y)] + line.neighbours())

    @pl.when(step == 0)
    def _():
        logits = dot_nt(router_t_ref[...], x_ref[...])
        hot = rank_row_ref[...] < 200.0
        top = jnp.max(jnp.where(hot, logits, NEGATIVE_LARGE), axis=0, keepdims=True)
        weight = jnp.where(hot, jnp.exp(jnp.minimum(logits - top, 0.0)), 0.0)
        gates = weight / jnp.sum(weight, axis=0, keepdims=True)
        expert_id = lax.broadcasted_iota(jnp.int32, gates.shape, 0)
        slot_id = lax.broadcasted_iota(jnp.int32, (capacity, rows), 0).astype(F32)
        rank_rows = []
        for e in range(local):
            mine = expert_id == base + e
            rank_rows.append(jnp.sum(jnp.where(mine, rank_row_ref[...], 0.0), 0, keepdims=True))
            rank_ref[e : e + 1, :] = rank_rows[e]
            gate_ref[e : e + 1, :] = jnp.sum(jnp.where(mine, gates, 0.0), 0, keepdims=True)
        for b in range(blocks):
            here = slice(b * rows, (b + 1) * rows)
            pieces = []
            for e in range(local):
                taken = jnp.broadcast_to(rank_rows[e][:, here], (capacity, rows)) == slot_id
                pieces.append(jnp.where(taken, 1.0, 0.0).astype(BF))
            pick = jnp.concatenate(pieces, axis=0)
            xs_ref[b] = dot(pick, x_ref[here, :]).astype(BF)
            middle = ct_low_ref.shape[1]
            g_ref[b, :, :middle] = dot(pick, ct_low_ref[here, :]).astype(BF)
            g_ref[b, :, middle:] = dot(pick, ct_high_ref[here, :]).astype(BF)

    @pl.when(step < local)
    def _():
        here = pl.ds(pl.multiple_of(step * capacity, capacity), capacity)
        xs = jnp.concatenate([xs_ref[b, here, :] for b in range(blocks)], axis=0)
        g = jnp.concatenate([g_ref[b, here, :] for b in range(blocks)], axis=0).astype(F32)
        slot_id = lax.broadcasted_iota(jnp.int32, (capacity, rows), 0).astype(F32)
        rank_row, gate_row = rank_ref[pl.ds(step, 1), :], gate_ref[pl.ds(step, 1), :]
        gates = []
        for b in range(blocks):
            taken = rank_row[:, b * rows : (b + 1) * rows] == slot_id
            gate = jnp.where(taken, gate_row[:, b * rows : (b + 1) * rows], 0.0)
            gates.append(jnp.sum(gate, axis=1, keepdims=True))
        gate_slot = jnp.concatenate(gates, axis=0)
        w_gate, w_up, w_down = w_gate_ref[0], w_up_ref[0], w_down_ref[0]
        gate_pre = dot(xs, w_gate)
        up_pre = dot(xs, w_up)
        sigmoid = jax.nn.sigmoid(gate_pre)
        silu = gate_pre * sigmoid
        activation = (silu * up_pre).astype(BF)
        expert_out = dot(activation, w_down).astype(BF).astype(F32)
        slot_dot = jnp.sum(g * expert_out, axis=1, keepdims=True)
        grad_out = (gate_slot * g).astype(BF)
        scaled_out = (gate_slot * expert_out).astype(BF)
        grad_down = dot_tn(activation, grad_out).astype(BF)
        grad_activation = dot_nt(grad_out, w_down)
        grad_gate_pre = (
            grad_activation * up_pre * sigmoid * (1.0 + gate_pre * (1.0 - sigmoid))
        ).astype(BF)
        grad_up_pre = (grad_activation * silu).astype(BF)
        grad_gate = dot_tn(xs, grad_gate_pre).astype(BF)
        grad_up = dot_tn(xs, grad_up_pre).astype(BF)
        if plane:
            for ref, value in zip(stage_refs, (grad_gate, grad_up, grad_down)):
                ref[step % STAGES] = value.reshape(ref.shape[1:])
        else:
            out_gate_ref[0], out_up_ref[0], out_down_ref[0] = grad_gate, grad_up, grad_down
        grad_in = (dot_nt(grad_gate_pre, w_gate) + dot_nt(grad_up_pre, w_up)).astype(BF)
        lane = lax.broadcasted_iota(jnp.int32, (blocks * capacity, LANES), 1)
        high = slot_dot.astype(BF).astype(F32)
        middle = (slot_dot - high).astype(BF).astype(F32)
        low = slot_dot - high - middle
        mine = base + step
        dots = jnp.where(lane == mine, high, 0.0)
        dots = jnp.where(lane == mine + EXPERTS, middle, dots)
        dots = jnp.where(lane == mine + 2 * EXPERTS, low, dots).astype(BF)
        for b in range(blocks):
            part = slice(b * capacity, (b + 1) * capacity)
            xs_ref[b, here, :] = grad_in[part]
            g_ref[b, here, :] = scaled_out[part]
            dots_ref[b, here, :] = dots[part]

    def store_y(b):
        there = pl.ds(b * rows, rows)
        return pltpu.make_async_copy(g_ref.at[b, :rows, :], y_ref.at[there, :], y_sem.at[b])

    @pl.when(step == local - 1)
    def _():
        slot_expert = lax.broadcasted_iota(jnp.int32, (EXPERTS, slots), 1) // capacity
        spread_row = lax.broadcasted_iota(jnp.int32, (EXPERTS, slots), 0)
        spread = jnp.where(spread_row == slot_expert + base, 1.0, 0.0).astype(BF)
        slot_rank = (lax.broadcasted_iota(jnp.int32, (rows, slots), 1) % capacity).astype(F32)
        for b in range(blocks):
            there = slice(b * rows, (b + 1) * rows)
            ranks = dot(rank_col_ref[there, :], spread)
            put = jnp.where(ranks == slot_rank, 1.0, 0.0).astype(BF)
            g_ref[b, :rows, :] = dot(put, g_ref[b]).astype(BF)
            store_y(b).start()
            back = dot(put, xs_ref[b]).astype(BF), dot(put, dots_ref[b]).astype(BF)
            if plane:
                gs_part[b, :, :D], gs_part[b, :, D:] = back
            else:
                gs_ref[there, :D], gs_ref[there, D:] = back
        if plane:
            line.start()

    @pl.when(step == pl.num_programs(0) - 1)
    def _():
        for b in range(blocks):
            store_y(b).wait()

    if not plane:
        return

    gate, up, low_down, high_down = range(4)
    low_rows, high_rows = slice(0, half), slice(half, 2 * half)

    def swap(e, i):
        return remote(
            stage_refs[i].at[e % STAGES, :, :, 1 - c],
            pair_refs[i].at[e % 3],
            csend.at[e % 2, i],
            crecv.at[e % 3, i],
            by_c,
        )

    def first(e, k):
        slot = e % 3
        source = {
            gate: lambda: pair_refs[0].at[slot, :, 1 - x],
            up: lambda: pair_refs[1].at[slot, 1 - y],
            low_down: lambda: pair_refs[2].at[slot, :, 1 - x, low_rows],
            high_down: lambda: pair_refs[2].at[slot, 1 - y, :, high_rows],
        }[k]()
        device = by_x if k in (gate, low_down) else by_y
        return remote(source, one_refs[k].at[slot], psend.at[slot, k], precv.at[slot, k], device)

    def second(e, k):
        along_x = k in (gate, low_down)
        source = one_refs[k].at[e % 3, 1 - y] if along_x else one_refs[k].at[e % 3, 1 - x]
        slot = e % 2
        return remote(
            source,
            two_refs[k].at[slot],
            qsend.at[slot, k],
            qrecv.at[slot, k],
            by_y if along_x else by_x,
        )

    def add(first_value, second_value):
        return (first_value.astype(F32) + second_value.astype(F32)).astype(BF)

    @pl.when(ticks & (tick >= 3))
    def _():
        e = tick - 3
        for k in range(4):
            second(e, k).wait()
        own = [one_refs[k][e % 3, y if k in (gate, low_down) else x] for k in range(4)]
        out_gate_ref[0] = add(own[gate], two_refs[gate][e % 2])
        out_up_ref[0] = add(own[up], two_refs[up][e % 2])
        out_down_ref[0, low_rows] = add(own[low_down], two_refs[low_down][e % 2])
        out_down_ref[0, high_rows] = add(own[high_down], two_refs[high_down][e % 2])

    @pl.when(ticks & (tick >= 2) & (tick < local + 2))
    def _():
        e = tick - 2
        slot = e % 3
        for k in range(4):
            first(e, k).wait()
            for t in (0, 1):
                mine = {
                    gate: lambda: pair_refs[0][slot, t, x],
                    up: lambda: pair_refs[1][slot, y, t],
                    low_down: lambda: pair_refs[2][slot, t, x, low_rows],
                    high_down: lambda: pair_refs[2][slot, y, t, high_rows],
                }[k]()
                one_refs[k][slot, t] = add(mine, one_refs[k][slot, t])
            second(e, k).start()

    @pl.when(ticks & (tick >= 1) & (tick < local + 1))
    def _():
        e = tick - 1
        slot = e % 3
        for i in range(3):
            swap(e, i).wait()

            def pair_sum(t, carry):
                a, b = t // 2, t % 2
                pair_refs[i][slot, a, b] = add(
                    stage_refs[i][e % STAGES, a, b, c], pair_refs[i][slot, a, b]
                )
                return carry

            lax.fori_loop(0, 4, pair_sum, 0)
        for k in range(4):
            first(e, k).start()

    @pl.when(ticks & (tick < local))
    def _():
        for i in range(3):
            swap(tick, i).start()

    for hop in range(1, blocks - 1):

        @pl.when(step == local + hop)
        def _():
            line.forward(hop)

    @pl.when(step == local + blocks - 1)
    def _():
        line.finish(gs_ref)


def run_experts(
    x_all,
    ct_low,
    ct_high,
    router_t,
    rank_row,
    rank_col,
    w_gate,
    w_up,
    w_down,
    rows,
    capacity,
    plane,
    collective_id,
):
    total = x_all.shape[0]
    blocks, local = total // rows, w_gate.shape[0]
    slots = local * capacity
    sizes = (blocks, rows, local, capacity)
    whole = lambda shape: pl.BlockSpec(
        shape, lambda e: (0,) * len(shape), pipeline_mode=pl.Buffered(1)
    )
    per = lambda shape: pl.BlockSpec((1,) + shape, lambda e: (jnp.minimum(e, local - 1), 0, 0))
    shapes = ((D, FF), (D, FF), (FF, D))
    scratch = [
        pltpu.VMEM((blocks, slots, D), BF),
        pltpu.VMEM((blocks, slots, D), BF),
        pltpu.VMEM((local, total), F32),
        pltpu.VMEM((local, total), F32),
        pltpu.VMEM((blocks, slots, LANES), BF),
        pltpu.SemaphoreType.DMA((blocks,)),
    ]
    params = dict(dimension_semantics=("arbitrary",), vmem_limit_bytes=63 * 1024 * 1024)
    if plane:
        eighths = [(a // 8, b) for a, b in shapes]
        out = lambda shape: pl.BlockSpec(
            (1,) + shape, lambda e: (jnp.maximum(plane_tick(e, local)[0] - 3, 0), 0, 0)
        )
        grad_shapes, grad_specs = eighths, [out(shape) for shape in eighths]
        low = (eighths[2][0] // 2, eighths[2][1])
        passed = (eighths[0], eighths[1], low, low)
        scratch += [pltpu.VMEM((STAGES, 2, 2, 2) + shape, BF) for shape in eighths]
        scratch += [pltpu.VMEM((3, 2, 2) + shape, BF) for shape in eighths]
        scratch += [pltpu.VMEM((3, 2) + shape, BF) for shape in passed]
        scratch += [pltpu.VMEM((2,) + shape, BF) for shape in passed]
        sems = [(2, 3), (3, 3), (3, 4), (3, 4), (2, 4), (2, 4)]
        scratch += [pltpu.SemaphoreType.DMA(shape) for shape in sems]
        scratch += [pltpu.VMEM((blocks, rows, D + LANES), BF)]
        scratch += line_sum_scratch(blocks, rows, D + LANES)
        gs_shape, gs_type = (rows, D + LANES), F32
        params |= dict(collective_id=collective_id, has_side_effects=True)
    else:
        grad_shapes, grad_specs = shapes, [per(shape) for shape in shapes]
        gs_shape, gs_type = (total, D + LANES), BF
    flops = 2 * total * D * slots * 4 // blocks + 18 * blocks * slots * D * FF
    return pl.pallas_call(
        functools.partial(expert_kernel, sizes, plane),
        grid=(local + 6 if plane else local,),
        out_shape=[
            jax.ShapeDtypeStruct((total, D), BF),
            jax.ShapeDtypeStruct(gs_shape, gs_type),
        ]
        + [jax.ShapeDtypeStruct((local,) + shape, BF) for shape in grad_shapes],
        in_specs=[
            whole((total, D)),
            whole(ct_low.shape),
            whole(ct_high.shape),
            whole((EXPERTS, D)),
            whole((EXPERTS, total)),
            whole((total, EXPERTS)),
        ]
        + [per(shape) for shape in shapes],
        out_specs=[ANY, whole(gs_shape)] + grad_specs,
        scratch_shapes=scratch,
        compiler_params=pltpu.CompilerParams(**params),
        cost_estimate=pl.CostEstimate(
            flops=flops, bytes_accessed=2 * (6 * local * D * FF + 4 * total * D), transcendentals=0
        ),
        name="experts",
    )(x_all, ct_low, ct_high, router_t, rank_row, rank_col, w_gate, w_up, w_down)


def rotate(tile, cosine, sine):
    half = HEAD_DIMENSION // 2
    lane = lax.broadcasted_iota(jnp.int32, tile.shape, 1) % HEAD_DIMENSION
    other = jnp.where(lane < half, pltpu.roll(tile, LANES - half, 1), pltpu.roll(tile, half, 1))
    return tile * cosine + other * sine


def normed(tokens_ref):
    value = tokens_ref[...].astype(F32)
    inverse = lax.rsqrt(jnp.mean(value * value, axis=-1, keepdims=True) + EPSILON)
    return value * inverse, inverse


def mask_bias(bias_ref, length_ref, rows):
    base = lax.axis_index("expert") * rows
    key = lax.broadcasted_iota(jnp.int32, bias_ref.shape, 0)
    query = lax.broadcasted_iota(jnp.int32, bias_ref.shape, 1) + base
    allowed = (key <= query) & (key < length_ref[0])
    bias_ref[...] = jnp.where(allowed, 0.0, NEGATIVE_LARGE)


def head_columns(ref, head):
    start = 2 * HEAD_DIMENSION * head
    middle = start + HEAD_DIMENSION
    return jnp.concatenate([ref[:, start:middle], ref[:, middle : middle + HEAD_DIMENSION]], 0)


def put_heads(ref, head, transposed):
    rows = ref.shape[0]
    value = transposed.T
    start = 2 * HEAD_DIMENSION * head
    middle = start + HEAD_DIMENSION
    ref[:, start:middle] = value[:rows].astype(ref.dtype)
    ref[:, middle : middle + HEAD_DIMENSION] = value[rows:].astype(ref.dtype)


def attention_kernel(
    n,
    length_ref,
    tokens_ref,
    gain_ref,
    weight_ref,
    cosine_ref,
    sine_ref,
    rank_ref,
    mixed_ref,
    log_total_ref,
    kv_all_ref,
    query_out_ref,
    rank_all_ref,
    *scratch,
):
    bias_ref, query_ref, kv_ref, chunk_ref, rank_buffer, send, recv, rank_send, rank_recv = scratch
    pair, pairs = pl.program_id(0), pl.num_programs(0)
    group, me = lax.axis_index("group"), lax.axis_index("expert")
    left, right = (group, me - 1), (group, me + 1)
    rows, width = kv_ref.shape[1:]

    def hop(j, step, side):
        block = me - step if side == 0 else me + step
        source = kv_ref.at[j] if step == 0 else chunk_ref.at[j, block]
        index = (j, side, step)
        return remote(
            source,
            chunk_ref.at[j, block],
            send.at[index],
            recv.at[index],
            right if side == 0 else left,
        )

    def rank_hop(step, side):
        block = me - step if side == 0 else me + step
        source = rank_ref if step == 0 else rank_buffer.at[block]
        index = (side, step)
        return remote(
            source,
            rank_buffer.at[block],
            rank_send.at[index],
            rank_recv.at[index],
            right if side == 0 else left,
        )

    def sends(step, side):
        return (me - step >= 0) & (me < n - 1) if side == 0 else (me + step < n) & (me > 0)

    def arrives(step, side):
        return me - 1 - step >= 0 if side == 0 else me + 1 + step < n

    def launch(make, step):
        for side in (0, 1):

            @pl.when(sends(step, side))
            def _():
                make(step, side).start()

    def await_hop(make, step):
        for side in (0, 1):

            @pl.when(arrives(step, side))
            def _():
                make(step, side).wait_recv()

    def drain(make):
        for step in range(n - 1):
            for side in (0, 1):

                @pl.when(sends(step, side))
                def _():
                    make(step, side).wait_send()

    def chunk(j):
        return lambda step, side: hop(j, step, side)

    @pl.when(pair == 0)
    def _():
        unit, _ = normed(tokens_ref)
        first_norm = (unit * gain_ref[...]).astype(BF)
        cosine, sine = cosine_ref[...], sine_ref[...]
        count = kv_ref.shape[0]
        query_width = count * width
        key_width = query_width // 2
        keys = dot(first_norm, weight_ref[:, query_width : query_width + key_width])
        values = dot(first_norm, weight_ref[:, query_width + key_width :])
        for j in range(count):
            columns = slice(j * LANES, (j + 1) * LANES)
            kv_ref[j, :, :LANES] = rotate(keys[:, columns], cosine, sine).astype(BF)
            kv_ref[j, :, LANES:] = values[:, columns].astype(BF)
        rank_buffer[me] = rank_ref[...]
        greet([(me > 0, left), (me < n - 1, right)])
        launch(chunk(0), 0)
        launch(chunk(1), 0)
        queries = dot(first_norm, weight_ref[:, :query_width])
        for j in range(2 * count):
            start = (j % 2) * LANES
            tile = queries[:, j * LANES : (j + 1) * LANES]
            query_ref[j // 2, :, start : start + LANES] = rotate(tile, cosine, sine).astype(BF)
        mask_bias(bias_ref, length_ref, rows)
        await_hop(chunk(0), 0)
        launch(chunk(0), 1)

    for step in range(1, n - 1):
        await_hop(chunk(pair), step)
        if step < n - 2:
            launch(chunk(pair), step + 1)

    @pl.when(pair + 1 < pairs)
    def _():
        await_hop(chunk(pair + 1), 0)
        launch(chunk(pair + 1), 1)

    @pl.when(pair + 2 < pairs)
    def _():
        launch(chunk(pair + 2), 0)

    @pl.when(pair == 1)
    def _():
        launch(rank_hop, 0)

    for step in range(n - 1):

        @pl.when(pair == jnp.minimum(2 + step, pairs - 1))
        def _():
            await_hop(rank_hop, step)
            if step < n - 2:
                launch(rank_hop, step + 1)

    chunk_ref[pair, me] = kv_ref[pair]
    kv = chunk_ref[pair].reshape(n * rows, width)
    kv_all_ref[...] = kv
    query_out_ref[0] = query_ref[pair]
    bias = jnp.concatenate([bias_ref[...]] * 2, axis=1)
    for head in (0, 1):
        start = head * HEAD_DIMENSION
        key = kv[:, start : start + HEAD_DIMENSION]
        value = kv[:, LANES + start : LANES + start + HEAD_DIMENSION]
        query = head_columns(query_ref.at[pair], head) * jnp.asarray(HEAD_DIMENSION**-0.5, BF)
        scores = dot_nt(key, query) + bias
        top = jnp.max(scores, axis=0, keepdims=True)
        weights = jnp.exp(scores - top)
        total = jnp.sum(weights, axis=0, keepdims=True)
        put_heads(mixed_ref, head, dot_tn(value, weights.astype(BF)) / total)
        log_total_ref[0, head : head + 1, :] = top + jnp.log(total)

    @pl.when(pair == pairs - 1)
    def _():
        drain(rank_hop)
        rank_all_ref[...] = rank_buffer[...]
        for j in range(KEY_VALUE_HEADS // 2):
            drain(chunk(j))


def attention(length, tokens, gain, weight, cosine, sine, rank, n, collective_id):
    rows = tokens.shape[0]
    keys, width = n * rows, 2 * LANES
    pairs = KEY_VALUE_HEADS // 2
    return pl.pallas_call(
        functools.partial(attention_kernel, n),
        grid=(pairs,),
        out_shape=(
            jax.ShapeDtypeStruct((rows, pairs * width), BF),
            jax.ShapeDtypeStruct((pairs, 2, 2 * rows), F32),
            jax.ShapeDtypeStruct((keys, pairs * width), BF),
            jax.ShapeDtypeStruct((pairs, rows, width), BF),
            jax.ShapeDtypeStruct((n,) + rank.shape, rank.dtype),
        ),
        in_specs=[pl.BlockSpec(memory_space=pltpu.SMEM)] + [IN_VMEM] * 6,
        out_specs=(
            pl.BlockSpec((rows, width), lambda j: (0, j)),
            pl.BlockSpec((1, 2, 2 * rows), lambda j: (j, 0, 0)),
            pl.BlockSpec((keys, width), lambda j: (0, j)),
            pl.BlockSpec((1, rows, width), lambda j: (j, 0, 0)),
            IN_VMEM,
        ),
        scratch_shapes=[
            pltpu.VMEM((keys, rows), F32),
            pltpu.VMEM((pairs, rows, width), BF),
            pltpu.VMEM((pairs, rows, width), BF),
            pltpu.VMEM((pairs, n, rows, width), BF),
            pltpu.VMEM((n,) + rank.shape, rank.dtype),
            pltpu.SemaphoreType.DMA((pairs, 2, n - 1)),
            pltpu.SemaphoreType.DMA((pairs, 2, n - 1)),
            pltpu.SemaphoreType.DMA((2, n - 1)),
            pltpu.SemaphoreType.DMA((2, n - 1)),
        ],
        compiler_params=pltpu.CompilerParams(
            dimension_semantics=("arbitrary",),
            vmem_limit_bytes=56 * 1024 * 1024,
            collective_id=collective_id,
            has_side_effects=True,
        ),
        cost_estimate=pl.CostEstimate(
            flops=16 * rows * keys * D, bytes_accessed=100000000, transcendentals=0
        ),
        name="attention",
    )(length, tokens, gain, weight, cosine, sine, rank)


def attention_back_kernel(
    n,
    length_ref,
    q_ref,
    kv_ref,
    grad_ref,
    log_total_ref,
    grad_q_ref,
    grad_kv_ref,
    bias_ref,
    terms_ref,
    landing,
    staging,
    send,
    recv,
):
    step, pairs = pl.program_id(0), pl.num_programs(0) - 1

    def line(j):
        return LineSum(
            n, terms_ref.at[j], landing.at[j], staging.at[j], send.at[j], recv.at[j]
        )

    @pl.when(step == 0)
    def _():
        greet(line(0).neighbours())
        mask_bias(bias_ref, length_ref, q_ref.shape[1])

    @pl.when(step < pairs)
    def _():
        attention_back_pair(
            q_ref, kv_ref, grad_ref, log_total_ref, grad_q_ref, terms_ref.at[step], bias_ref
        )
        line(step).start()

    @pl.when(step > 0)
    def _():
        for hop in range(1, n - 1):
            line(step - 1).forward(hop)
        line(step - 1).finish(grad_kv_ref)


def attention_back_pair(q_ref, kv_ref, grad_ref, log_total_ref, grad_q_ref, grad_kv_ref, bias_ref):
    scale = HEAD_DIMENSION**-0.5
    blocks, rows, _ = grad_kv_ref.shape
    q_ref = q_ref.at[0]
    bias = jnp.concatenate([bias_ref[...]] * 2, axis=1)
    for head in (0, 1):
        columns = slice(head * HEAD_DIMENSION, (head + 1) * HEAD_DIMENSION)
        key, value = kv_ref[:, :LANES][:, columns], kv_ref[:, LANES:][:, columns]
        query = head_columns(q_ref, head) * jnp.asarray(scale, BF)
        grad = head_columns(grad_ref, head)
        scores = dot_nt(key, query) + bias
        probs = jnp.exp(scores - log_total_ref[0, head : head + 1, :])
        grad_probs = dot_nt(value, grad)
        delta = jnp.sum(probs * grad_probs, axis=0, keepdims=True)
        grad_scores = (probs * (grad_probs - delta)).astype(BF)
        grad_key = dot(grad_scores, query).astype(BF).reshape(blocks, rows, HEAD_DIMENSION)
        grad_kv_ref[:, :, columns] = grad_key
        grad_value = dot(probs.astype(BF), grad).astype(BF).reshape(blocks, rows, HEAD_DIMENSION)
        start = LANES + head * HEAD_DIMENSION
        grad_kv_ref[:, :, start : start + HEAD_DIMENSION] = grad_value
        put_heads(grad_q_ref, head, dot_tn(key, grad_scores) * scale)


def attention_back(length, query, kv_all, grad_mixed, log_total, n, collective_id):
    rows, keys = query.shape[1], kv_all.shape[0]
    pairs, width = KEY_VALUE_HEADS // 2, 2 * LANES
    now = lambda j: jnp.minimum(j, pairs - 1)
    row_spec = pl.BlockSpec((rows, width), lambda j: (0, now(j)))
    return pl.pallas_call(
        functools.partial(attention_back_kernel, n),
        grid=(pairs + 1,),
        out_shape=(
            jax.ShapeDtypeStruct((rows, pairs * width), F32),
            jax.ShapeDtypeStruct((rows, pairs * width), BF),
        ),
        in_specs=[
            pl.BlockSpec(memory_space=pltpu.SMEM),
            pl.BlockSpec((1, rows, width), lambda j: (now(j), 0, 0)),
            pl.BlockSpec((keys, width), lambda j: (0, now(j))),
            row_spec,
            pl.BlockSpec((1, 2, 2 * rows), lambda j: (now(j), 0, 0)),
        ],
        out_specs=(
            row_spec,
            pl.BlockSpec((rows, width), lambda j: (0, jnp.maximum(j - 1, 0))),
        ),
        scratch_shapes=[
            pltpu.VMEM((keys, rows), F32),
            pltpu.VMEM((pairs, n, rows, width), BF),
            pltpu.VMEM((pairs, 2, n - 1, rows, width), BF),
            pltpu.VMEM((pairs, 2, n - 2, rows, width), BF),
            pltpu.SemaphoreType.DMA((pairs, 2, n - 1)),
            pltpu.SemaphoreType.DMA((pairs, 2, n - 1)),
        ],
        compiler_params=pltpu.CompilerParams(
            dimension_semantics=("arbitrary",),
            vmem_limit_bytes=60 * 1024 * 1024,
            collective_id=collective_id,
            has_side_effects=True,
        ),
        cost_estimate=pl.CostEstimate(
            flops=40 * rows * keys * D, bytes_accessed=100000000, transcendentals=0
        ),
        name="attention_back",
    )(length, query, kv_all, grad_mixed, log_total)


def widen_kernel(value_ref, out_ref):
    out_ref[...] = value_ref[...].astype(F32)


def widen(value):
    block = (1,) + value.shape[1:]
    spec = pl.BlockSpec(block, lambda e: (e, 0, 0))
    return pl.pallas_call(
        widen_kernel,
        grid=(value.shape[0],),
        out_shape=jax.ShapeDtypeStruct(value.shape, F32),
        in_specs=[spec],
        out_specs=spec,
        compiler_params=pltpu.CompilerParams(dimension_semantics=("arbitrary",)),
        cost_estimate=pl.CostEstimate(flops=0, bytes_accessed=6 * value.size, transcendentals=0),
        name="widen",
    )(value)


def unpair_columns(value):
    rows = value.shape[0]
    value = value.reshape(rows, -1, 2, LANES)
    return value[:, :, 0].reshape(rows, -1), value[:, :, 1].reshape(rows, -1)


def gather_rows(value):
    return lax.all_gather(value, "expert", axis=0, tiled=True)


def scatter_rows(value):
    return lax.psum_scatter(value, "expert", scatter_dimension=0, tiled=True)


def per_device(
    tokens,
    lengths,
    routes,
    norm_gain1,
    w_query,
    key_projection,
    value_projection,
    w_out,
    norm_gain2,
    w_router,
    w_gate,
    w_up,
    w_down,
    cotangent,
):
    rows = tokens.shape[0]
    n, groups = lax.axis_size("expert"), lax.axis_size("group")
    plane = groups == 8 and w_gate.shape[0] == 8
    my_index = lax.axis_index("expert")
    capacity = 3 * rows * TOP // (2 * EXPERTS)
    query_width, key_width = w_query.shape[1], key_projection.shape[1]
    length = lengths[0]
    positions = my_index * rows + jnp.arange(rows, dtype=jnp.int32)
    valid_rows = (positions < length)[:, None]
    grad_output = jnp.where(valid_rows, cotangent, jnp.zeros_like(cotangent))

    small = jnp.concatenate(
        [w_router, norm_gain1[:, None], norm_gain2[:, None]]
        + [jnp.zeros((w_router.shape[0], LANES - EXPERTS - 2), BF)],
        axis=1,
    )
    middle = D // 2
    qkv_weight, out_weight, small, ct_low = gather_weights(
        w_query, key_projection, value_projection, w_out, small, grad_output[:, :middle], n, 1
    )
    qkv_weight, ct_high = lax.optimization_barrier((qkv_weight, grad_output[:, middle:]))
    ct_high = gather_rows(ct_high)
    router_weight = small[:, :EXPERTS]
    gain_one = small[:, EXPERTS].astype(F32)
    gain_two = small[:, EXPERTS + 1].astype(F32)

    expert_ids = jnp.arange(EXPERTS, dtype=jnp.int32)
    hot = jnp.any(routes[:, :, None] == expert_ids, axis=1)
    row_id = jnp.arange(rows, dtype=jnp.int32)
    earlier = (row_id[:, None] < row_id[None, :]).astype(BF)
    rank = jnp.where(hot.T, dot(hot.T.astype(BF), earlier), 255.0).astype(BF)

    cosine_lookup, sine_lookup = [table[:, 0] for table in rotary_tables(positions, HEAD_DIMENSION)]
    cosine = jnp.tile(cosine_lookup, (1, 4))
    sine = jnp.tile(jnp.concatenate([-sine_lookup, sine_lookup], axis=1), (1, 2))
    token_f32 = tokens.astype(F32)
    gain_one_row = gain_one[None, :]
    mixed_low, log_total, kv_all, query_pairs, rank_all = attention(
        lengths, tokens, gain_one_row, qkv_weight, cosine, sine, rank, n, 2
    )
    rank_row = jnp.transpose(rank_all, (1, 0, 2)).reshape(EXPERTS, n * rows).astype(F32)
    rank_col = jnp.transpose(rank_all, (0, 2, 1)).reshape(n * rows, EXPERTS)
    residual = token_f32 + dot(mixed_low, out_weight)
    inverse_two = lax.rsqrt(jnp.mean(residual * residual, axis=-1, keepdims=True) + EPSILON)
    unit_two = residual * inverse_two
    second_norm = (unit_two * gain_two).astype(BF)
    (x_all,) = line_gather([second_norm], n, 3, "gather_rows")

    y_part, gs, grad_gate, grad_up, grad_down = run_experts(
        x_all,
        ct_low,
        ct_high,
        router_weight.T,
        rank_row,
        rank_col,
        w_gate,
        w_up,
        w_down,
        rows,
        capacity,
        plane,
        7,
    )
    if not plane:
        gs = line_scatter(gs, n, F32, 4, "scatter_grads")

    logits = dot(second_norm, router_weight)
    chosen = jnp.where(hot, logits, NEGATIVE_LARGE)
    gate_weights = jnp.where(hot, jnp.exp(chosen - jnp.max(chosen, axis=-1, keepdims=True)), 0.0)
    gate_weights = gate_weights / jnp.sum(gate_weights, axis=-1, keepdims=True)
    grad_gates = gs[:, D : D + EXPERTS] + gs[:, D + EXPERTS : D + 2 * EXPERTS]
    grad_gates = grad_gates + gs[:, D + 2 * EXPERTS : D + 3 * EXPERTS]
    grad_logits = (
        gate_weights * (grad_gates - jnp.sum(gate_weights * grad_gates, axis=-1, keepdims=True))
    ).astype(BF)
    grad_second = gs[:, :D] + dot_nt(grad_logits, router_weight)
    grad_router = dot_tn(second_norm, grad_logits)
    scaled_two = grad_second * gain_two
    grad_gain2 = jnp.sum(grad_second * unit_two, axis=0)
    grad_residual = grad_output.astype(F32) + inverse_two * (
        scaled_two - unit_two * jnp.mean(scaled_two * unit_two, axis=-1, keepdims=True)
    )
    grad_attn = grad_residual.astype(BF)
    mixed_gradient = dot_nt(grad_attn, out_weight).astype(BF)
    grad_query_acc, kv_gradient = attention_back(
        lengths, query_pairs, kv_all, mixed_gradient, log_total, n, 5
    )
    pad = jnp.zeros((D, LANES - EXPERTS), F32)
    if plane:
        *shares, expert_sum, grad_tokens = reduce_weights(
            grad_query_acc,
            kv_gradient,
            tokens,
            gain_one_row,
            qkv_weight,
            cosine,
            sine,
            mixed_low,
            grad_attn,
            grad_residual,
            jnp.concatenate([grad_router, pad], axis=1),
            grad_gain2[None, :],
            y_part,
            n,
            6,
        )
    else:
        inverse_one = lax.rsqrt(jnp.mean(token_f32 * token_f32, axis=-1, keepdims=True) + EPSILON)
        unit_one = token_f32 * inverse_one
        first_norm = (unit_one * gain_one).astype(BF)
        own_key_gradient, own_value_gradient = unpair_columns(kv_gradient)
        back = lambda value: apply_rotation(
            value.astype(F32).reshape(rows, -1, HEAD_DIMENSION),
            cosine_lookup[:, None],
            -sine_lookup[:, None],
        )
        grad_query_pre = back(grad_query_acc).reshape(rows, query_width).astype(BF)
        grad_key_pre = back(own_key_gradient).reshape(rows, key_width).astype(BF)
        grad_qkv_pre = jnp.concatenate([grad_query_pre, grad_key_pre, own_value_gradient], axis=1)
        grad_first = dot_nt(grad_qkv_pre, qkv_weight)
        scaled_one = grad_first * gain_one
        grad_gain1 = jnp.sum(grad_first * unit_one, axis=0)
        grad_tokens = grad_residual + inverse_one * (
            scaled_one - unit_one * jnp.mean(scaled_one * unit_one, axis=-1, keepdims=True)
        )
        grad_small = jnp.concatenate(
            [grad_router, grad_gain1[:, None], grad_gain2[:, None], pad[:, 2:]], axis=1
        )
        shares = (dot_tn(first_norm, grad_qkv_pre), dot_tn(mixed_low, grad_attn), grad_small)
        shares = [lax.psum(scatter_rows(share.astype(BF)), "group") for share in shares]
        expert_sum = line_scatter(y_part, n, F32, 8, "scatter_outputs")
    mixed = (residual + expert_sum).astype(BF)
    share_qkv, share_out, share_small = [share.astype(F32) for share in shares]

    def sum_over_groups(value):
        if not plane:
            value = lax.psum_scatter(value, "group", scatter_dimension=1, tiled=True)
        return widen(lax.all_gather(value, "group", axis=1, tiled=True))

    return (
        mixed,
        grad_tokens,
        share_small[:, EXPERTS],
        share_qkv[:, :query_width],
        share_qkv[:, query_width : query_width + key_width],
        share_qkv[:, query_width + key_width :],
        share_out,
        share_small[:, EXPERTS + 1],
        share_small[:, :EXPERTS],
        sum_over_groups(grad_gate),
        sum_over_groups(grad_up),
        sum_over_groups(grad_down),
    )


def solution(mesh):
    rows = P(("group", "expert"), None)
    vector, matrix, stack = P("expert"), P("expert", None), P("expert", None, None)
    return jax.shard_map(
        per_device,
        mesh=mesh,
        in_specs=(
            rows,
            P("group"),
            rows,
            vector,
            matrix,
            matrix,
            matrix,
            matrix,
            vector,
            matrix,
            stack,
            stack,
            stack,
            rows,
        ),
        out_specs=(
            rows,
            rows,
            vector,
            matrix,
            matrix,
            matrix,
            matrix,
            vector,
            matrix,
            stack,
            stack,
            stack,
        ),
        check_vma=False,
    )
```

profile of v0, /device:TPU:0, one launch (start us, length us, event | category | flops | bytes accessed | tf_op | source)
XLA Modules:
  0.0 507.4 jit_solution(15015255944209130662)
XLA Ops:
  10.3 1.2 broadcast_select_fusion
  13.1 48.1 %gather_weights.1 = (bf16[4,2,2,2,32,2048]{5,4,3,2,1,0:T(8,128)(2,1)}, bf16[4,2,2,2,32,1024]{5,4,3,2,1,0:T(8,128)(2,1)}, bf16[4,2,2,2,32,128]{5,4,3,2,1,0:T(8,128)(2,1)}, bf16[4,256,512]{2,1,0:T(8,128)(2,1)}) custom-call(bf16[256,1024]{1,0:T(8,128)(2,1)} %refs_0_.1, bf16[256,512]{1,0:T(8,128)(2,1)} %refs_1_.1, bf16[256,512]{1,0:T(8,128)(2,1)} %refs_2_.2, ...), custom_call_target="tpu_custom_call" | custom-call | bytes 100000000 | tf_op jit(solution)/shard_map/gather_weights/pallas_call | solution.py:480
  63.9 1.7 copy.85
  65.6 1.0 convert_reduce_fusion
  66.6 60.6 %attention.1 = (bf16[256,1024]{1,0:T(8,128)(2,1)}, f32[4,2,512]{2,1,0:T(2,128)}, bf16[1024,1024]{1,0:T(8,128)(2,1)}, bf16[4,256,256]{2,1,0:T(8,128)(2,1)}, bf16[4,32,256]{2,1,0:T(8,128)(2,1)}) custom-call(s32[1]{0:T(128)} %copy.93.length_ref, bf16[256,1024]{1,0:T(8,128)(2,1)} %refs_2_.3, f32[1,1024]{1,0:T(1,128)} %bitcast.55, bf16[1024,2048]{1,0:T(8,128)(2,1)} %bitcast.39, ...), custom_call_target="tpu_custom_call" | custom-call | flops 4294967296 | bytes 100000000 | tf_op jit(solution)/shard_map/attention/pallas_call | solution.py:1325
  128.7 1.7 copy.75
  130.4 1.8 multiply_reduce_fusion.2
  134.1 36.2 %gather_rows.1 = bf16[4,256,1024]{2,1,0:T(8,128)(2,1)} custom-call(bf16[256,1024]{1,0:T(8,128)(2,1)} %multiply_convert_fusion.refs_0_), custom_call_target="tpu_custom_call" | custom-call | bytes 100000000 | tf_op jit(solution)/shard_map/gather_rows/pallas_call | solution.py:153
  170.4 124.9 %experts.1 = (bf16[1024,1024]{1,0:T(8,128)(2,1)}, f32[256,1152]{1,0:T(8,128)}, bf16[8,128,512]{2,1,0:T(8,128)(2,1)}, bf16[8,128,512]{2,1,0:T(8,128)(2,1)}, bf16[8,64,1024]{2,1,0:T(8,128)(2,1)}) custom-call(bf16[1024,1024]{1,0:T(8,128)(2,1)} %bitcast.44, bf16[1024,512]{1,0:T(8,128)(2,1)} %bitcast.60, bf16[1024,512]{1,0:T(8,128)(2,1)} %all-gather.5.cloned.1.call-done.refs_2_, ...), custom_call_target="tpu_custom_call" | custom-call | flops 30601641984 | bytes 58720256 | tf_op jit(solution)/shard_map/experts/pallas_call | solution.py:1103
  297.4 1.4 multiply_reduce_fusion.3
  298.8 1.3 multiply_convert_fusion.1
  301.3 1.0 multiply_reduce_fusion
  302.3 1.3 fusion.9
  304.5 1.6 convolution_convert_fusion.grad_ref
  306.1 50.8 %attention_back.1 = (f32[256,1024]{1,0:T(8,128)}, bf16[256,1024]{1,0:T(8,128)(2,1)}) custom-call(s32[1]{0:T(128)} %copy.93.length_ref, bf16[4,256,256]{2,1,0:T(8,128)(2,1)} %get-tuple-element.39.q_ref, bf16[1024,1024]{1,0:T(8,128)(2,1)} %get-tuple-element.40.kv_ref, bf16[256,1024]{1,0:T(8,128)(2,1)} %convolution_convert_fusion.grad_ref, ...), custom_call_target="tpu_custom_call" | custom-call | flops 10737418240 | bytes 100000000 | tf_op jit(solution)/shard_map/attention_back/pallas_call | solution.py:1437
  356.9 103.0 %reduce_weights.1 = (bf16[2,2,2,32,1664]{4,3,2,1,0:T(8,128)(2,1)}, bf16[2,2,2,32,1536]{4,3,2,1,0:T(8,128)(2,1)}, f32[256,1024]{1,0:T(8,128)}, f32[256,1024]{1,0:T(8,128)}) custom-call(f32[256,1024]{1,0:T(8,128)} %get-tuple-element.46.refs_0_, bf16[256,1024]{1,0:T(8,128)(2,1)} %get-tuple-element.47.refs_1_, bf16[256,1024]{1,0:T(8,128)(2,1)} %refs_2_.3, ...), custom_call_target="tpu_custom_call" | custom-call | bytes 100000000 | tf_op jit(solution)/shard_map/reduce_weights/pallas_call | solution.py:773
  460.8 1.4 slice.83
  464.2 1.1 slice.85
  465.3 1.1 maximum_convert_fusion.1
  466.9 1.1 slice_convert_fusion
  468.9 10.3 %widen.5 = f32[8,512,1024]{2,1,0:T(8,128)} custom-call(bf16[8,512,1024]{2,1,0:T(8,128)(2,1)} %all-gather.11.cloned.1.call-done.value_ref), custom_call_target="tpu_custom_call" | custom-call | bytes 25165824 | tf_op jit(solution)/shard_map/widen/pallas_call | solution.py:1483
  479.2 10.3 %widen.4 = f32[8,1024,512]{2,1,0:T(8,128)} custom-call(bf16[8,1024,512]{2,1,0:T(8,128)(2,1)} %all-gather.9.cloned.1.call-done.value_ref), custom_call_target="tpu_custom_call" | custom-call | bytes 25165824 | tf_op jit(solution)/shard_map/widen/pallas_call | solution.py:1483
  489.6 10.4 %widen.3 = f32[8,1024,512]{2,1,0:T(8,128)} custom-call(bf16[8,1024,512]{2,1,0:T(8,128)(2,1)} %all-gather.7.cloned.1.call-done.value_ref), custom_call_target="tpu_custom_call" | custom-call | bytes 25165824 | tf_op jit(solution)/shard_map/widen/pallas_call | solution.py:1483
  499.9 1.0 copy.94
  (75 shorter events, 18.4 us)
Async XLA Ops:
  7.2 163.2 %all-gather.5.cloned.1.call-start = ((), (), s32[]{:S(2)}) async-start(), calls=%async_computation | async-start | bytes 1310720 | tf_op jit(solution)/shard_map/all_gather | solution.py:1502
  10.2 51.1 %copy-start.13 = (s32[256,8]{0,1:T(8,128)S(1)}, s32[256,8]{0,1:T(8,128)}, u32[]{:S(2)}) copy-start(s32[256,8]{0,1:T(8,128)} %param.16) | copy-start | bytes 24580
  61.2 4.4 copy-start.3
  61.3 407.7 %all-gather.11.cloned.1.call-start = ((), (), s32[]{:S(2)}) async-start(), calls=%async_computation.3 | async-start | bytes 9437184 | tf_op jit(solution)/shard_map/all_gather | solution.py:1662
  66.6 63.8 %copy-start.5 = (bf16[256,1024]{1,0:T(8,128)(2,1)S(1)}, bf16[256,1024]{1,0:T(8,128)(2,1)}, u32[]{:S(2)}) copy-start(bf16[256,1024]{1,0:T(8,128)(2,1)} %refs_2_.3) | copy-start | bytes 1572868
  66.6 63.8 %copy-start.7 = (bf16[4,2,2,2,32,1024]{5,4,3,2,1,0:T(8,128)(2,1)S(1)}, bf16[4,2,2,2,32,1024]{5,4,3,2,1,0:T(8,128)(2,1)}, u32[]{:S(2)}) copy-start(bf16[4,2,2,2,32,1024]{5,4,3,2,1,0:T(8,128)(2,1)} %get-tuple-element.38) | copy-start | bytes 6291460
  132.2 1.0 copy-start
  295.3 1.5 copy-start.2
  295.4 183.9 %all-gather.9.cloned.1.call-start = ((), (), s32[]{:S(2)}) async-start(), calls=%async_computation.2 | async-start | bytes 9437184 | tf_op jit(solution)/shard_map/all_gather | solution.py:1662
  296.1 193.5 %all-gather.7.cloned.1.call-start = ((), (), s32[]{:S(2)}) async-start(), calls=%async_computation.1 | async-start | bytes 9437184 | tf_op jit(solution)/shard_map/all_gather | solution.py:1662
  296.8 4.5 copy-start.1
  296.8 4.5 copy-start.4
  300.5 1.9 copy-start.9
  302.3 2.1 copy-start.8
  303.7 53.2 %copy-start.6 = (bf16[256,1024]{1,0:T(8,128)(2,1)}, bf16[256,1024]{1,0:T(8,128)(2,1)S(1)}, u32[]{:S(2)}) copy-start(bf16[256,1024]{1,0:T(8,128)(2,1)S(1)} %get-tuple-element.60.refs_8_) | copy-start | bytes 1572868
  464.2 2.8 copy-start.12
  465.2 2.8 copy-start.11
  489.6 10.4 %copy-start.10 = (f32[256,1024]{1,0:T(8,128)S(1)}, f32[256,1024]{1,0:T(8,128)}, u32[]{:S(2)}) copy-start(f32[256,1024]{1,0:T(8,128)} %get-tuple-element.89) | copy-start | bytes 3145732
Sparse Core Ops, SparseCore 0:
  61.4 35.0 all-gather.4
  295.5 53.0 all-gather.10
  350.5 75.8 all-gather.8
  428.1 59.3 all-gather.6
where the time goes:
time: 509 us; the launch traced here: 507 us
  Pallas kernels  455 us (89%)
  local copies, waits for them, and re-layouts  18.1 us (4%)
  between operations  14.7 us (3%)
  other arithmetic  12.5 us (2%)
  matrix products  5.94 us (1%)
    pallas_call x1, Pallas kernels, run_experts(): pl.pallas_call(functools.partial(expert_kernel, sizes, plane), grid=(loca...  125 us
    pallas_call x1, Pallas kernels, reduce_weights(): pl.pallas_call(functools.partial(reduce_kernel, n, pieces), out_shape=[ja...  103 us
    pallas_call x1, Pallas kernels, attention(): pl.pallas_call(functools.partial(attention_kernel, n), grid=(pairs,), out...  60.6 us
    pallas_call x1, Pallas kernels, attention_back(): pl.pallas_call(functools.partial(attention_back_kernel, n), grid=(pairs +...  50.8 us
    pallas_call x1, Pallas kernels, gather_weights(): pl.pallas_call(functools.partial(weights_kernel, n, pieces, widths), out_...  48.1 us
    pallas_call x1, Pallas kernels, line_gather(): pl.pallas_call(functools.partial(line_gather_kernel, n, count), out_shape...  36.2 us
    pallas_call x3, Pallas kernels, widen(): pl.pallas_call(widen_kernel, grid=(value.shape[0],), out_shape=jax.ShapeD...  31 us
  transfers between devices with their start and end apart: 4, of which 0 were waited for; matrix products, arithmetic and copies ran while one was open for 6% of the time, Pallas kernels for 53%

commit v1 on v0

--- a/solution.py
+++ b/solution.py
@@ -815,53 +815,161 @@
 
 def expert_kernel(sizes, plane, *refs):
     blocks, rows, local, capacity = sizes
-    x_ref, ct_low_ref, ct_high_ref, router_t_ref, rank_row_ref, rank_col_ref = refs[:6]
-    w_gate_ref, w_up_ref, w_down_ref = refs[6:9]
-    y_ref, gs_ref, out_gate_ref, out_up_ref, out_down_ref = refs[9:14]
-    xs_ref, g_ref, rank_ref, gate_ref, dots_ref, y_sem = refs[14:20]
-    refs = refs[20:]
+    if plane:
+        mixed_in, tokens_in, out_weight_in, gain_ref = refs[:4]
+        refs = refs[4:]
+    else:
+        x_ref = refs[0]
+        refs = refs[1:]
+    ct_low_ref, ct_high_ref, router_t_ref, rank_all_ref = refs[:4]
+    w_gate_ref, w_up_ref, w_down_ref = refs[4:7]
+    y_ref, gs_ref, out_gate_ref, out_up_ref, out_down_ref = refs[7:12]
+    refs = refs[12:]
+    if plane:
+        second_ref, residual_ref = refs[:2]
+        refs = refs[2:]
+    xs_ref, g_ref, rank_ref, gate_ref, dots_ref, y_sem = refs[:6]
+    refs = refs[6:]
     slots = local * capacity
     step = pl.program_id(0)
     tick, ticks = plane_tick(step, local)
-    base = lax.axis_index("expert") * local
+    me = lax.axis_index("expert")
+    base = me * local
     if plane:
         stage_refs, pair_refs, one_refs, two_refs = refs[:3], refs[3:6], refs[6:10], refs[10:14]
         csend, crecv, psend, precv, qsend, qrecv = refs[14:20]
         gs_part = refs[20]
-        line = LineSum(blocks, gs_part, *refs[21:])
-        _, _, (y, x, c), (by_y, by_x, by_c) = plane_position()
+        line = LineSum(blocks, gs_part, *refs[21:25])
+        x_ref, xsend, xrecv, in_sem, out_sem = refs[25:]
+        group, _, (y, x, c), (by_y, by_x, by_c) = plane_position()
         half = stage_refs[2].shape[4] // 2
 
-        @pl.when(step == 0)
-        def _():
-            greet([(None, by_c), (None, by_x), (None, by_y)] + line.neighbours())
-
-    @pl.when(step == 0)
-    def _():
-        logits = dot_nt(router_t_ref[...], x_ref[...])
-        hot = rank_row_ref[...] < 200.0
+    def expert_id():
+        return lax.broadcasted_iota(jnp.int32, (EXPERTS, rows), 0)
+
+    def note_ranks(b):
+        ranks = rank_all_ref[b].astype(F32)
+        for e in range(local):
+            mine = jnp.where(expert_id() == base + e, ranks, 0.0)
+            rank_ref[b, e : e + 1, :] = jnp.sum(mine, axis=0, keepdims=True)
+
+    def pick(b):
+        slot_id = lax.broadcasted_iota(jnp.int32, (capacity, rows), 0).astype(F32)
+        pieces = [
+            jnp.where(rank_ref[b, e : e + 1, :] == slot_id, 1.0, 0.0).astype(BF)
+            for e in range(local)
+        ]
+        return jnp.concatenate(pieces, axis=0)
+
+    def dispatch_grads(b):
+        picked = pick(b)
+        middle = ct_low_ref.shape[2]
+        g_ref[b, :, :middle] = dot(picked, ct_low_ref[b]).astype(BF)
+        g_ref[b, :, middle:] = dot(picked, ct_high_ref[b]).astype(BF)
+
+    def dispatch_rows(b):
+        logits = dot_nt(router_t_ref[...], x_ref[b])
+        hot = rank_all_ref[b].astype(F32) < 200.0
         top = jnp.max(jnp.where(hot, logits, NEGATIVE_LARGE), axis=0, keepdims=True)
         weight = jnp.where(hot, jnp.exp(jnp.minimum(logits - top, 0.0)), 0.0)
         gates = weight / jnp.sum(weight, axis=0, keepdims=True)
-        expert_id = lax.broadcasted_iota(jnp.int32, gates.shape, 0)
-        slot_id = lax.broadcasted_iota(jnp.int32, (capacity, rows), 0).astype(F32)
-        rank_rows = []
         for e in range(local):
-            mine = expert_id == base + e
-            rank_rows.append(jnp.sum(jnp.where(mine, rank_row_ref[...], 0.0), 0, keepdims=True))
-            rank_ref[e : e + 1, :] = rank_rows[e]
-            gate_ref[e : e + 1, :] = jnp.sum(jnp.where(mine, gates, 0.0), 0, keepdims=True)
-        for b in range(blocks):
-            here = slice(b * rows, (b + 1) * rows)
-            pieces = []
-            for e in range(local):
-                taken = jnp.broadcast_to(rank_rows[e][:, here], (capacity, rows)) == slot_id
-                pieces.append(jnp.where(taken, 1.0, 0.0).astype(BF))
-            pick = jnp.concatenate(pieces, axis=0)
-            xs_ref[b] = dot(pick, x_ref[here, :]).astype(BF)
-            middle = ct_low_ref.shape[1]
-            g_ref[b, :, :middle] = dot(pick, ct_low_ref[here, :]).astype(BF)
-            g_ref[b, :, middle:] = dot(pick, ct_high_ref[here, :]).astype(BF)
+            mine = jnp.where(expert_id() == base + e, gates, 0.0)
+            gate_ref[b, e : e + 1, :] = jnp.sum(mine, axis=0, keepdims=True)
+        xs_ref[b] = dot(pick(b), x_ref[b]).astype(BF)
+
+    if plane:
+        n = blocks
+        leave_second = pltpu.make_async_copy(x_ref.at[me], second_ref, out_sem.at[0])
+        leave_residual = pltpu.make_async_copy(gs_ref.at[:, :D], residual_ref, out_sem.at[1])
+
+        def hop(far, side):
+            block = me - far if side == 0 else me + far
+            device = (group, me + 1 if side == 0 else me - 1)
+            index = (side, far)
+            return remote(
+                x_ref.at[block], x_ref.at[block], xsend.at[index], xrecv.at[index], device
+            )
+
+        def sends(far, side):
+            if side == 0:
+                return (far < n - 1) & (me - far >= 0) & (me < n - 1)
+            return (far < n - 1) & (me + far < n) & (me > 0)
+
+        def arrives(far, side):
+            return me - 1 - far >= 0 if side == 0 else me + 1 + far < n
+
+        @pl.when(step == 0)
+        def _():
+            loads = [
+                pltpu.make_async_copy(out_weight_in, stage_refs[2].at[2:4], in_sem.at[0]),
+                pltpu.make_async_copy(tokens_in, xs_ref.at[0, :rows, :], in_sem.at[1]),
+                pltpu.make_async_copy(mixed_in, xs_ref.at[1, :rows, :], in_sem.at[2]),
+            ]
+            for copy in loads:
+                copy.start()
+            for b in range(blocks):
+                note_ranks(b)
+            for copy in loads:
+                copy.wait()
+            out_weight = stage_refs[2][2:4].reshape(D, D)
+            residual = xs_ref[0, :rows, :].astype(F32) + dot(xs_ref[1, :rows, :], out_weight)
+            inverse = lax.rsqrt(jnp.mean(residual * residual, axis=-1, keepdims=True) + EPSILON)
+            x_ref[me] = (residual * inverse * gain_ref[...]).astype(BF)
+            gs_ref[:, :D] = residual
+            greet([(None, by_c), (None, by_x), (None, by_y)] + line.neighbours())
+            for side in (0, 1):
+
+                @pl.when(sends(0, side))
+                def _():
+                    hop(0, side).start()
+
+            leave_second.start()
+            leave_residual.start()
+            for b in range(blocks):
+                dispatch_grads(b)
+            dispatch_rows(me)
+
+            def arrived(far, carry):
+                for side in (0, 1):
+
+                    @pl.when(arrives(far, side))
+                    def _():
+                        hop(far, side).wait_recv()
+
+                    @pl.when(sends(far + 1, side))
+                    def _():
+                        hop(far + 1, side).start()
+
+                for side in (0, 1):
+
+                    @pl.when(arrives(far, side))
+                    def _():
+                        dispatch_rows(me - 1 - far if side == 0 else me + 1 + far)
+
+                return carry
+
+            lax.fori_loop(0, n - 1, arrived, 0)
+
+        @pl.when(step == 1)
+        def _():
+            leave_second.wait()
+            leave_residual.wait()
+            for far in range(n - 1):
+                for side in (0, 1):
+
+                    @pl.when(sends(far, side))
+                    def _():
+                        hop(far, side).wait_send()
+
+    else:
+
+        @pl.when(step == 0)
+        def _():
+            for b in range(blocks):
+                note_ranks(b)
+                dispatch_grads(b)
+                dispatch_rows(b)
 
     @pl.when(step < local)
     def _():
@@ -869,11 +977,10 @@
         xs = jnp.concatenate([xs_ref[b, here, :] for b in range(blocks)], axis=0)
         g = jnp.concatenate([g_ref[b, here, :] for b in range(blocks)], axis=0).astype(F32)
         slot_id = lax.broadcasted_iota(jnp.int32, (capacity, rows), 0).astype(F32)
-        rank_row, gate_row = rank_ref[pl.ds(step, 1), :], gate_ref[pl.ds(step, 1), :]
         gates = []
         for b in range(blocks):
-            taken = rank_row[:, b * rows : (b + 1) * rows] == slot_id
-            gate = jnp.where(taken, gate_row[:, b * rows : (b + 1) * rows], 0.0)
+            taken = rank_ref[b, pl.ds(step, 1), :] == slot_id
+            gate = jnp.where(taken, gate_ref[b, pl.ds(step, 1), :], 0.0)
             gates.append(jnp.sum(gate, axis=1, keepdims=True))
         gate_slot = jnp.concatenate(gates, axis=0)
         w_gate, w_up, w_down = w_gate_ref[0], w_up_ref[0], w_down_ref[0]
@@ -926,7 +1033,7 @@
         slot_rank = (lax.broadcasted_iota(jnp.int32, (rows, slots), 1) % capacity).astype(F32)
         for b in range(blocks):
             there = slice(b * rows, (b + 1) * rows)
-            ranks = dot(rank_col_ref[there, :], spread)
+            ranks = dot_tn(rank_all_ref[b], spread)
             put = jnp.where(ranks == slot_rank, 1.0, 0.0).astype(BF)
             g_ref[b, :rows, :] = dot(put, g_ref[b]).astype(BF)
             store_y(b).start()
@@ -1046,22 +1153,10 @@
 
 
 def run_experts(
-    x_all,
-    ct_low,
-    ct_high,
-    router_t,
-    rank_row,
-    rank_col,
-    w_gate,
-    w_up,
-    w_down,
-    rows,
-    capacity,
-    plane,
-    collective_id,
+    sources, ct_low, ct_high, router_t, rank_all, w_gate, w_up, w_down, capacity, plane, collective_id
 ):
-    total = x_all.shape[0]
-    blocks, local = total // rows, w_gate.shape[0]
+    blocks, _, rows = rank_all.shape
+    total, local = blocks * rows, w_gate.shape[0]
     slots = local * capacity
     sizes = (blocks, rows, local, capacity)
     whole = lambda shape: pl.BlockSpec(
@@ -1069,11 +1164,12 @@
     )
     per = lambda shape: pl.BlockSpec((1,) + shape, lambda e: (jnp.minimum(e, local - 1), 0, 0))
     shapes = ((D, FF), (D, FF), (FF, D))
+    ct_low, ct_high = [ct.reshape(blocks, rows, -1) for ct in (ct_low, ct_high)]
     scratch = [
         pltpu.VMEM((blocks, slots, D), BF),
         pltpu.VMEM((blocks, slots, D), BF),
-        pltpu.VMEM((local, total), F32),
-        pltpu.VMEM((local, total), F32),
+        pltpu.VMEM((blocks, local, rows), F32),
+        pltpu.VMEM((blocks, local, rows), F32),
         pltpu.VMEM((blocks, slots, LANES), BF),
         pltpu.SemaphoreType.DMA((blocks,)),
     ]
@@ -1094,11 +1190,24 @@
         scratch += [pltpu.SemaphoreType.DMA(shape) for shape in sems]
         scratch += [pltpu.VMEM((blocks, rows, D + LANES), BF)]
         scratch += line_sum_scratch(blocks, rows, D + LANES)
+        scratch += [pltpu.VMEM((blocks, rows, D), BF)]
+        sems = [(2, blocks - 1), (2, blocks - 1), (3,), (2,)]
+        scratch += [pltpu.SemaphoreType.DMA(shape) for shape in sems]
+        mixed_low, tokens, out_weight, gain = sources
+        sources = [mixed_low, tokens, out_weight.reshape((2, 2, 2, 2) + eighths[2]), gain]
+        source_specs = [ANY] * 3 + [whole(gain.shape)]
+        more_shapes = [
+            jax.ShapeDtypeStruct((rows, D), BF),
+            jax.ShapeDtypeStruct((rows, D), F32),
+        ]
         gs_shape, gs_type = (rows, D + LANES), F32
         params |= dict(collective_id=collective_id, has_side_effects=True)
     else:
         grad_shapes, grad_specs = shapes, [per(shape) for shape in shapes]
         gs_shape, gs_type = (total, D + LANES), BF
+        sources = [sources[0].reshape(blocks, rows, D)]
+        source_specs = [whole(sources[0].shape)]
+        more_shapes = []
     flops = 2 * total * D * slots * 4 // blocks + 18 * blocks * slots * D * FF
     return pl.pallas_call(
         functools.partial(expert_kernel, sizes, plane),
@@ -1107,24 +1216,24 @@
             jax.ShapeDtypeStruct((total, D), BF),
             jax.ShapeDtypeStruct(gs_shape, gs_type),
         ]
-        + [jax.ShapeDtypeStruct((local,) + shape, BF) for shape in grad_shapes],
-        in_specs=[
-            whole((total, D)),
+        + [jax.ShapeDtypeStruct((local,) + shape, BF) for shape in grad_shapes]
+        + more_shapes,
+        in_specs=source_specs
+        + [
             whole(ct_low.shape),
             whole(ct_high.shape),
             whole((EXPERTS, D)),
-            whole((EXPERTS, total)),
-            whole((total, EXPERTS)),
+            whole(rank_all.shape),
         ]
         + [per(shape) for shape in shapes],
-        out_specs=[ANY, whole(gs_shape)] + grad_specs,
+        out_specs=[ANY, whole(gs_shape)] + grad_specs + [ANY] * len(more_shapes),
         scratch_shapes=scratch,
         compiler_params=pltpu.CompilerParams(**params),
         cost_estimate=pl.CostEstimate(
             flops=flops, bytes_accessed=2 * (6 * local * D * FF + 4 * total * D), transcendentals=0
         ),
         name="experts",
-    )(x_all, ct_low, ct_high, router_t, rank_row, rank_col, w_gate, w_up, w_down)
+    )(*sources, ct_low, ct_high, router_t, rank_all, w_gate, w_up, w_down)
 
 
 def rotate(tile, cosine, sine):
@@ -1562,30 +1671,20 @@
     mixed_low, log_total, kv_all, query_pairs, rank_all = attention(
         lengths, tokens, gain_one_row, qkv_weight, cosine, sine, rank, n, 2
     )
-    rank_row = jnp.transpose(rank_all, (1, 0, 2)).reshape(EXPERTS, n * rows).astype(F32)
-    rank_col = jnp.transpose(rank_all, (0, 2, 1)).reshape(n * rows, EXPERTS)
-    residual = token_f32 + dot(mixed_low, out_weight)
+    expert_args = (ct_low, ct_high, router_weight.T, rank_all, w_gate, w_up, w_down, capacity)
+    if plane:
+        sources = (mixed_low, tokens, out_weight, gain_two[None, :])
+        y_part, gs, grad_gate, grad_up, grad_down, second_norm, residual = run_experts(
+            sources, *expert_args, plane, 7
+        )
+    else:
+        residual = token_f32 + dot(mixed_low, out_weight)
     inverse_two = lax.rsqrt(jnp.mean(residual * residual, axis=-1, keepdims=True) + EPSILON)
     unit_two = residual * inverse_two
-    second_norm = (unit_two * gain_two).astype(BF)
-    (x_all,) = line_gather([second_norm], n, 3, "gather_rows")
-
-    y_part, gs, grad_gate, grad_up, grad_down = run_experts(
-        x_all,
-        ct_low,
-        ct_high,
-        router_weight.T,
-        rank_row,
-        rank_col,
-        w_gate,
-        w_up,
-        w_down,
-        rows,
-        capacity,
-        plane,
-        7,
-    )
     if not plane:
+        second_norm = (unit_two * gain_two).astype(BF)
+        sources = line_gather([second_norm], n, 3, "gather_rows")
+        y_part, gs, grad_gate, grad_up, grad_down = run_experts(sources, *expert_args, plane, 7)
         gs = line_scatter(gs, n, F32, 4, "scatter_grads")
 
     logits = dot(second_norm, router_weight)

time: 509 us -> 499 us (0.980)
    pallas_call x1 -> x0, Pallas kernels: 36.2 us -> none  [line_gather(): pl.pallas_call(functools.partial(line_gather_kernel, n, count), out_shape...]
    pallas_call x1, Pallas kernels: 125 us -> 159 us  [run_experts(): pl.pallas_call(functools.partial(expert_kernel, sizes, plane), grid=(loca...]
  transfers between devices with their start and end apart: 4 -> 4, of which waited for: 0 -> 0; matrix products, arithmetic and copies ran while one was open for 6% -> 4% of each run, Pallas kernels for 53% -> 48%
where the time goes in v1:
time: 499 us; the launch traced here: 498 us
  Pallas kernels  454 us (91%)
  local copies, waits for them, and re-layouts  14.8 us (3%)
  between operations  14.7 us (3%)
  other arithmetic  8.7 us (2%)
    pallas_call x1, Pallas kernels, run_experts(): pl.pallas_call(functools.partial(expert_kernel, sizes, plane), grid=(loca...  159 us
    pallas_call x1, Pallas kernels, reduce_weights(): pl.pallas_call(functools.partial(reduce_kernel, n, pieces), out_shape=[ja...  104 us
    pallas_call x1, Pallas kernels, attention(): pl.pallas_call(functools.partial(attention_kernel, n), grid=(pairs,), out...  60.6 us
    pallas_call x1, Pallas kernels, attention_back(): pl.pallas_call(functools.partial(attention_back_kernel, n), grid=(pairs +...  50.9 us
    pallas_call x1, Pallas kernels, gather_weights(): pl.pallas_call(functools.partial(weights_kernel, n, pieces, widths), out_...  48.1 us
    pallas_call x3, Pallas kernels, widen(): pl.pallas_call(widen_kernel, grid=(value.shape[0],), out_shape=jax.ShapeD...  31.4 us
  transfers between devices with their start and end apart: 4, of which 0 were waited for; matrix products, arithmetic and copies ran while one was open for 4% of the time, Pallas kernels for 48%

profile of v1, /device:TPU:0, one launch (start us, length us, event | category | flops | bytes accessed | tf_op | source)
XLA Modules:
  0.0 497.8 jit_solution(13585110443626828197)
XLA Ops:
  9.4 0.8 copy.62
  10.2 1.1 broadcast_select_fusion
  13.1 48.1 %gather_weights.1 = (bf16[4,2,2,2,32,2048]{5,4,3,2,1,0:T(8,128)(2,1)}, bf16[4,2,2,2,32,1024]{5,4,3,2,1,0:T(8,128)(2,1)}, bf16[4,2,2,2,32,128]{5,4,3,2,1,0:T(8,128)(2,1)}, bf16[4,256,512]{2,1,0:T(8,128)(2,1)}) custom-call(bf16[256,1024]{1,0:T(8,128)(2,1)} %refs_0_.1, bf16[256,512]{1,0:T(8,128)(2,1)} %refs_1_.2, bf16[256,512]{1,0:T(8,128)(2,1)} %refs_2_.2, ...), custom_call_target="tpu_custom_call" | custom-call | bytes 100000000 | tf_op jit(solution)/shard_map/gather_weights/pallas_call | solution.py:480
  63.1 1.7 copy.77
  64.8 1.0 convert_reduce_fusion
  66.6 60.6 %attention.1 = (bf16[256,1024]{1,0:T(8,128)(2,1)}, f32[4,2,512]{2,1,0:T(2,128)}, bf16[1024,1024]{1,0:T(8,128)(2,1)}, bf16[4,256,256]{2,1,0:T(8,128)(2,1)}, bf16[4,32,256]{2,1,0:T(8,128)(2,1)}) custom-call(s32[1]{0:T(128)} %copy.84.length_ref, bf16[256,1024]{1,0:T(8,128)(2,1)} %refs_2_.3, f32[1,1024]{1,0:T(1,128)} %bitcast.43, bf16[1024,2048]{1,0:T(8,128)(2,1)} %bitcast.32, ...), custom_call_target="tpu_custom_call" | custom-call | flops 4294967296 | bytes 100000000 | tf_op jit(solution)/shard_map/attention/pallas_call | solution.py:1434
  127.2 158.9 %experts.1 = (bf16[1024,1024]{1,0:T(8,128)(2,1)}, f32[256,1152]{1,0:T(8,128)}, bf16[8,128,512]{2,1,0:T(8,128)(2,1)}, bf16[8,128,512]{2,1,0:T(8,128)(2,1)}, bf16[...) custom-call(bf16[256,1024]{1,0:T(8,128)(2,1)} %get-tuple-element.39.refs_0_.refs_7_, ...), custom_call_target="tpu_custom_call" | custom-call | flops 30601641984 | bytes 58720256 | tf_op jit(solution)/shard_map/experts/pallas_call | solution.py:1212
  289.1 0.8 concatenate.14.refs_10_
  290.1 1.0 multiply_reduce_fusion
  291.1 1.3 fusion.9
  293.2 1.6 convolution_convert_fusion.grad_ref
  294.8 50.9 %attention_back.1 = (f32[256,1024]{1,0:T(8,128)}, bf16[256,1024]{1,0:T(8,128)(2,1)}) custom-call(s32[1]{0:T(128)} %copy.84.length_ref, bf16[4,256,256]{2,1,0:T(8,128)(2,1)} %get-tuple-element.45.q_ref, bf16[1024,1024]{1,0:T(8,128)(2,1)} %get-tuple-element.46.kv_ref, bf16[256,1024]{1,0:T(8,128)(2,1)} %convolution_convert_fusion.grad_ref, ...), custom_call_target="tpu_custom_call" | custom-call | flops 10737418240 | bytes 100000000 | tf_op jit(solution)/shard_map/attention_back/pallas_call | solution.py:1546
  345.8 104.1 %reduce_weights.1 = (bf16[2,2,2,32,1664]{4,3,2,1,0:T(8,128)(2,1)}, bf16[2,2,2,32,1536]{4,3,2,1,0:T(8,128)(2,1)}, f32[256,1024]{1,0:T(8,128)}, f32[256,1024]{1,0:T(8,128)}) custom-call(f32[256,1024]{1,0:T(8,128)} %get-tuple-element.50.refs_0_, bf16[256,1024]{1,0:T(8,128)(2,1)} %get-tuple-element.51.refs_1_, bf16[256,1024]{1,0:T(8,128)(2,1)} %refs_2_.3, ...), custom_call_target="tpu_custom_call" | custom-call | bytes 100000000 | tf_op jit(solution)/shard_map/reduce_weights/pallas_call | solution.py:773
  449.9 0.9 slice.81
  450.8 1.4 slice.83
  452.9 1.0 slice.84
  454.2 1.1 slice.85
  455.2 1.1 maximum_convert_fusion.1
  456.9 1.1 slice_convert_fusion
  458.0 0.9 add_convert_fusion
  458.9 10.7 %widen.5 = f32[8,512,1024]{2,1,0:T(8,128)} custom-call(bf16[8,512,1024]{2,1,0:T(8,128)(2,1)} %all-gather.11.cloned.1.call-done.value_ref), custom_call_target="tpu_custom_call" | custom-call | bytes 25165824 | tf_op jit(solution)/shard_map/widen/pallas_call | solution.py:1592
  469.7 10.3 %widen.4 = f32[8,1024,512]{2,1,0:T(8,128)} custom-call(bf16[8,1024,512]{2,1,0:T(8,128)(2,1)} %all-gather.9.cloned.1.call-done.value_ref), custom_call_target="tpu_custom_call" | custom-call | bytes 25165824 | tf_op jit(solution)/shard_map/widen/pallas_call | solution.py:1592
  480.0 10.4 %widen.3 = f32[8,1024,512]{2,1,0:T(8,128)} custom-call(bf16[8,1024,512]{2,1,0:T(8,128)(2,1)} %all-gather.7.cloned.1.call-done.value_ref), custom_call_target="tpu_custom_call" | custom-call | bytes 25165824 | tf_op jit(solution)/shard_map/widen/pallas_call | solution.py:1592
  490.3 1.0 copy.85
  (68 shorter events, 11.2 us)
Async XLA Ops:
  7.2 120.0 %all-gather.5.cloned.1.call-start = ((), (), s32[]{:S(2)}) async-start(), calls=%async_computation | async-start | bytes 1310720 | tf_op jit(solution)/shard_map/all_gather | solution.py:1611
  12.2 52.5 %copy-start.11 = (s32[256,8]{0,1:T(8,128)S(1)}, s32[256,8]{0,1:T(8,128)}, u32[]{:S(2)}) copy-start(s32[256,8]{0,1:T(8,128)} %param.16) | copy-start | bytes 24580
  61.2 3.6 copy-start.1
  61.2 397.7 %all-gather.11.cloned.1.call-start = ((), (), s32[]{:S(2)}) async-start(), calls=%async_computation.3 | async-start | bytes 9437184 | tf_op jit(solution)/shard_map/all_gather | solution.py:1761
  286.1 1.5 copy-start.6
  286.1 2.0 copy-start.2
  286.2 183.5 %all-gather.9.cloned.1.call-start = ((), (), s32[]{:S(2)}) async-start(), calls=%async_computation.2 | async-start | bytes 9437184 | tf_op jit(solution)/shard_map/all_gather | solution.py:1761
  286.9 193.1 %all-gather.7.cloned.1.call-start = ((), (), s32[]{:S(2)}) async-start(), calls=%async_computation.1 | async-start | bytes 9437184 | tf_op jit(solution)/shard_map/all_gather | solution.py:1761
  287.6 2.3 copy-start
  288.2 1.9 copy-start.3
  288.2 1.9 copy-start.10
  289.9 1.2 copy-start.5
  291.1 2.1 copy-start.12
  292.5 53.3 %copy-start.4 = (bf16[256,1024]{1,0:T(8,128)(2,1)}, bf16[256,1024]{1,0:T(8,128)(2,1)S(1)}, u32[]{:S(2)}) copy-start(bf16[256,1024]{1,0:T(8,128)(2,1)S(1)} %get-tuple-element.64.refs_8_) | copy-start | bytes 1572868
  454.1 2.8 copy-start.9
  455.2 2.8 copy-start.8
  480.0 10.4 %copy-start.7 = (f32[256,1024]{1,0:T(8,128)S(1)}, f32[256,1024]{1,0:T(8,128)}, u32[]{:S(2)}) copy-start(f32[256,1024]{1,0:T(8,128)} %get-tuple-element.91) | copy-start | bytes 3145732
Sparse Core Ops, SparseCore 0:
  61.4 35.0 all-gather.4
  286.3 53.8 all-gather.10
  342.1 73.0 all-gather.8
  416.9 60.1 all-gather.6

commit v2 on v1

--- a/solution.py
+++ b/solution.py
@@ -1,4 +1,5 @@
 import functools
+import itertools
 
 import jax
 import jax.numpy as jnp
@@ -428,18 +429,19 @@
                     for i in range(3):
                         third(slot, block, i).start()
 
-            for side in (0, 1):
-                if step > 2:
-
-                    @pl.when(me - step + 2 >= 0 if side == 0 else me + step - 2 < n)
-                    def _():
-                        extra_hop(step - 3, side).wait_recv()
-
-                if step < n + 1:
-
-                    @pl.when(sends(step - 2, side))
-                    def _():
-                        extra_hop(step - 2, side).start()
+        for side in (0, 1):
+            if 2 <= step < n + 1:
+
+                @pl.when(me - step + 1 >= 0 if side == 0 else me + step - 1 < n)
+                def _():
+                    extra_hop(step - 2, side).wait_recv()
+
+        for side in (0, 1):
+            if 1 <= step < n:
+
+                @pl.when(sends(step - 1, side))
+                def _():
+                    extra_hop(step - 1, side).start()
 
     for step in range(n):
         for slot, block, there in held(step):
@@ -463,7 +465,7 @@
 
 
 def path_pieces(query_width, key_width, out_width, small_width):
-    half = (query_width + 2 * key_width + out_width) // 2
+    half = query_width + key_width
     return (
         (0, 0, half, True),
         (0, half, query_width + 2 * key_width - half, False),
@@ -518,11 +520,12 @@
         grad_residual_ref,
         router_ref,
         gain_two_ref,
+        residual_ref,
         y_part,
-    ) = refs[:13]
-    outs, y_out, grad_tokens_ref = refs[13:15], refs[15], refs[16]
-    ins, grad_pre_ref = refs[17:20], refs[20]
-    refs = refs[21:]
+    ) = refs[:14]
+    q_out, k_out, v_out, o_out, small_out, mixed_out, grad_tokens_ref = refs[14:21]
+    ins, grad_pre_ref, outs, y_out = refs[21:24], refs[24], refs[25:27], refs[27]
+    refs = refs[28:]
     pair, one, two, landing, staging = refs[:2], refs[2:4], refs[4:6], refs[6:8], refs[8:10]
     csend, crecv, psend, precv, zsend, zrecv, gsend, grecv = refs[10:18]
     line = LineSum(n, y_part, *refs[18:])
@@ -716,8 +719,17 @@
             spread(path, stage).start()
         if stage == 0:
             line.finish(y_out)
+            mixed_out[...] = (residual_ref[...] + y_out[...]).astype(BF)
         for path in (0, 1):
             spread(path, stage).wait_recv()
+
+    flat = [out[...].reshape(-1, out.shape[4]).astype(F32) for out in outs]
+    columns = ([(0, q_out), (0, k_out)], [(1, v_out), (1, o_out)], [(0, small_out)])
+    starts = [0, 0]
+    for path, target in itertools.chain(*columns):
+        width = target.shape[1]
+        target[...] = flat[path][:, starts[path] : starts[path] + width]
+        starts[path] += width
 
     for path in (0, 1):
         for stage in range(3):
@@ -750,6 +762,7 @@
     grad_residual,
     grad_router,
     gain_two_row,
+    residual,
     y_part,
     n,
     collective_id,
@@ -764,19 +777,21 @@
     widths = [sum(p[2] for p in pieces if p[3]), sum(p[2] for p in pieces if not p[3])]
     scratch = [pltpu.VMEM((n, 2, 2, 2, eighth, w), BF) for w in array_widths]
     scratch += [pltpu.VMEM((grad_q.shape[0], width_all), BF)]
+    scratch += [pltpu.VMEM((2, 2, 2, eighth, w), BF) for w in widths]
+    scratch += [pltpu.VMEM((y_part.shape[0] // n, y_part.shape[1]), F32)]
     scratch += [pltpu.VMEM((n, 2, 2, eighth, w), BF) for w in widths]
     scratch += [pltpu.VMEM((n, 2, eighth, w), BF) for w in widths]
     scratch += [pltpu.VMEM((n, eighth, w), BF) for w in widths]
     scratch += [pltpu.VMEM((2, n - 1, eighth, w), BF) for w in widths] * 2
     sems = [(4,), (4,), (2, 2), (2, 2), (2, 2, n - 1), (2, 2, n - 1), (2, 3), (2, 3)]
     y_rows = y_part.shape[0] // n
-    outs = pl.pallas_call(
+    out_widths = (query_width, key_width, key_width, grad_attn.shape[1], LANES)
+    return pl.pallas_call(
         functools.partial(reduce_kernel, n, pieces),
-        out_shape=[jax.ShapeDtypeStruct((2, 2, 2, eighth, w), BF) for w in widths]
-        + [jax.ShapeDtypeStruct((y_rows, y_part.shape[1]), F32)]
-        + [jax.ShapeDtypeStruct(tokens.shape, F32)],
-        in_specs=[IN_VMEM] * 13,
-        out_specs=[IN_VMEM] * 4,
+        out_shape=[jax.ShapeDtypeStruct((rows, w), F32) for w in out_widths]
+        + [jax.ShapeDtypeStruct(tokens.shape, BF), jax.ShapeDtypeStruct(tokens.shape, F32)],
+        in_specs=[IN_VMEM] * 14,
+        out_specs=[IN_VMEM] * 7,
         scratch_shapes=scratch
         + [pltpu.SemaphoreType.DMA(s) for s in sems]
         + line_sum_scratch(n, y_rows, y_part.shape[1]),
@@ -798,13 +813,9 @@
         grad_residual,
         grad_router,
         gain_two_row,
+        residual,
         y_part.reshape(n, y_rows, y_part.shape[1]),
     )
-    first, second = [o.reshape(rows, w) for o, w in zip(outs, widths)]
-    cut = pieces[0][2]
-    rest = pieces[1][2]
-    qkv = jnp.concatenate([first[:, :cut], second[:, :rest]], axis=1)
-    return qkv, second[:, rest:], first[:, cut:], outs[2], outs[3]
 
 
 def plane_tick(step, local):
@@ -821,10 +832,10 @@
     else:
         x_ref = refs[0]
         refs = refs[1:]
-    ct_low_ref, ct_high_ref, router_t_ref, rank_all_ref = refs[:4]
-    w_gate_ref, w_up_ref, w_down_ref = refs[4:7]
-    y_ref, gs_ref, out_gate_ref, out_up_ref, out_down_ref = refs[7:12]
-    refs = refs[12:]
+    ct_ref, router_t_ref, rank_all_ref = refs[:3]
+    w_gate_ref, w_up_ref, w_down_ref = refs[3:6]
+    y_ref, gs_ref, out_gate_ref, out_up_ref, out_down_ref = refs[6:11]
+    refs = refs[11:]
     if plane:
         second_ref, residual_ref = refs[:2]
         refs = refs[2:]
@@ -862,10 +873,7 @@
         return jnp.concatenate(pieces, axis=0)
 
     def dispatch_grads(b):
-        picked = pick(b)
-        middle = ct_low_ref.shape[2]
-        g_ref[b, :, :middle] = dot(picked, ct_low_ref[b]).astype(BF)
-        g_ref[b, :, middle:] = dot(picked, ct_high_ref[b]).astype(BF)
+        g_ref[b] = dot(pick(b), ct_ref[b]).astype(BF)
 
     def dispatch_rows(b):
         logits = dot_nt(router_t_ref[...], x_ref[b])
@@ -1153,7 +1161,7 @@
 
 
 def run_experts(
-    sources, ct_low, ct_high, router_t, rank_all, w_gate, w_up, w_down, capacity, plane, collective_id
+    sources, ct_all, router_t, rank_all, w_gate, w_up, w_down, capacity, plane, collective_id
 ):
     blocks, _, rows = rank_all.shape
     total, local = blocks * rows, w_gate.shape[0]
@@ -1164,7 +1172,7 @@
     )
     per = lambda shape: pl.BlockSpec((1,) + shape, lambda e: (jnp.minimum(e, local - 1), 0, 0))
     shapes = ((D, FF), (D, FF), (FF, D))
-    ct_low, ct_high = [ct.reshape(blocks, rows, -1) for ct in (ct_low, ct_high)]
+    ct_all = ct_all.reshape(blocks, rows, D)
     scratch = [
         pltpu.VMEM((blocks, slots, D), BF),
         pltpu.VMEM((blocks, slots, D), BF),
@@ -1220,8 +1228,7 @@
         + more_shapes,
         in_specs=source_specs
         + [
-            whole(ct_low.shape),
-            whole(ct_high.shape),
+            whole(ct_all.shape),
             whole((EXPERTS, D)),
             whole(rank_all.shape),
         ]
@@ -1233,7 +1240,7 @@
             flops=flops, bytes_accessed=2 * (6 * local * D * FF + 4 * total * D), transcendentals=0
         ),
         name="experts",
-    )(*sources, ct_low, ct_high, router_t, rank_all, w_gate, w_up, w_down)
+    )(*sources, ct_all, router_t, rank_all, w_gate, w_up, w_down)
 
 
 def rotate(tile, cosine, sine):
@@ -1478,11 +1485,23 @@
     length_ref,
     q_ref,
     kv_ref,
-    grad_ref,
     log_total_ref,
+    gs_ref,
+    residual_ref,
+    second_ref,
+    ct_ref,
+    hot_ref,
+    gain_ref,
+    router_ref,
+    out_weight_ref,
     grad_q_ref,
     grad_kv_ref,
+    grad_residual_ref,
+    grad_attn_ref,
+    grad_router_ref,
+    grad_gain_ref,
     bias_ref,
+    grad_ref,
     terms_ref,
     landing,
     staging,
@@ -1500,11 +1519,35 @@
     def _():
         greet(line(0).neighbours())
         mask_bias(bias_ref, length_ref, q_ref.shape[1])
+        hot = hot_ref[...] > 0.5
+        second, router = second_ref[...], router_ref[...]
+        logits = dot(second, router)
+        top = jnp.max(jnp.where(hot, logits, NEGATIVE_LARGE), axis=-1, keepdims=True)
+        weight = jnp.where(hot, jnp.exp(jnp.minimum(logits - top, 0.0)), 0.0)
+        gates = weight / jnp.sum(weight, axis=-1, keepdims=True)
+        grad_gates = gs_ref[:, D : D + EXPERTS] + gs_ref[:, D + EXPERTS : D + 2 * EXPERTS]
+        grad_gates = grad_gates + gs_ref[:, D + 2 * EXPERTS : D + 3 * EXPERTS]
+        mean = jnp.sum(gates * grad_gates, axis=-1, keepdims=True)
+        grad_logits = (gates * (grad_gates - mean)).astype(BF)
+        grad_second = gs_ref[:, :D] + dot_nt(grad_logits, router)
+        grad_router_ref[...] = jnp.zeros_like(grad_router_ref)
+        grad_router_ref[:, :EXPERTS] = dot_tn(second, grad_logits)
+        unit, inverse = normed(residual_ref)
+        grad_gain_ref[...] = jnp.sum(grad_second * unit, axis=0, keepdims=True)
+        scaled = grad_second * gain_ref[...]
+        mean = jnp.mean(scaled * unit, axis=-1, keepdims=True)
+        grad_residual = ct_ref[...].astype(F32) + inverse * (scaled - unit * mean)
+        grad_residual_ref[...] = grad_residual
+        grad_attn_ref[...] = grad_residual.astype(BF)
+        grad_mixed = dot_nt(grad_residual.astype(BF), out_weight_ref[...]).astype(BF)
+        width = grad_ref.shape[2]
+        for j in range(grad_ref.shape[0]):
+            grad_ref[j] = grad_mixed[:, j * width : (j + 1) * width]
 
     @pl.when(step < pairs)
     def _():
         attention_back_pair(
-            q_ref, kv_ref, grad_ref, log_total_ref, grad_q_ref, terms_ref.at[step], bias_ref
+            q_ref, kv_ref, grad_ref.at[step], log_total_ref, grad_q_ref, terms_ref.at[step], bias_ref
         )
         line(step).start()
 
@@ -1538,7 +1581,7 @@
         put_heads(grad_q_ref, head, dot_tn(key, grad_scores) * scale)
 
 
-def attention_back(length, query, kv_all, grad_mixed, log_total, n, collective_id):
+def attention_back(length, query, kv_all, log_total, sources, n, collective_id):
     rows, keys = query.shape[1], kv_all.shape[0]
     pairs, width = KEY_VALUE_HEADS // 2, 2 * LANES
     now = lambda j: jnp.minimum(j, pairs - 1)
@@ -1549,20 +1592,26 @@
         out_shape=(
             jax.ShapeDtypeStruct((rows, pairs * width), F32),
             jax.ShapeDtypeStruct((rows, pairs * width), BF),
+            jax.ShapeDtypeStruct((rows, D), F32),
+            jax.ShapeDtypeStruct((rows, D), BF),
+            jax.ShapeDtypeStruct((D, LANES), F32),
+            jax.ShapeDtypeStruct((1, D), F32),
         ),
         in_specs=[
             pl.BlockSpec(memory_space=pltpu.SMEM),
             pl.BlockSpec((1, rows, width), lambda j: (now(j), 0, 0)),
             pl.BlockSpec((keys, width), lambda j: (0, now(j))),
-            row_spec,
             pl.BlockSpec((1, 2, 2 * rows), lambda j: (now(j), 0, 0)),
-        ],
+        ]
+        + [IN_VMEM] * len(sources),
         out_specs=(
             row_spec,
             pl.BlockSpec((rows, width), lambda j: (0, jnp.maximum(j - 1, 0))),
-        ),
+        )
+        + (IN_VMEM,) * 4,
         scratch_shapes=[
             pltpu.VMEM((keys, rows), F32),
+            pltpu.VMEM((pairs, rows, width), BF),
             pltpu.VMEM((pairs, n, rows, width), BF),
             pltpu.VMEM((pairs, 2, n - 1, rows, width), BF),
             pltpu.VMEM((pairs, 2, n - 2, rows, width), BF),
@@ -1579,7 +1628,7 @@
             flops=40 * rows * keys * D, bytes_accessed=100000000, transcendentals=0
         ),
         name="attention_back",
-    )(length, query, kv_all, grad_mixed, log_total)
+    )(length, query, kv_all, log_total, *sources)
 
 
 def widen_kernel(value_ref, out_ref):
@@ -1647,12 +1696,9 @@
         + [jnp.zeros((w_router.shape[0], LANES - EXPERTS - 2), BF)],
         axis=1,
     )
-    middle = D // 2
-    qkv_weight, out_weight, small, ct_low = gather_weights(
-        w_query, key_projection, value_projection, w_out, small, grad_output[:, :middle], n, 1
+    qkv_weight, out_weight, small, ct_all = gather_weights(
+        w_query, key_projection, value_projection, w_out, small, grad_output, n, 1
     )
-    qkv_weight, ct_high = lax.optimization_barrier((qkv_weight, grad_output[:, middle:]))
-    ct_high = gather_rows(ct_high)
     router_weight = small[:, :EXPERTS]
     gain_one = small[:, EXPERTS].astype(F32)
     gain_two = small[:, EXPERTS + 1].astype(F32)
@@ -1671,7 +1717,7 @@
     mixed_low, log_total, kv_all, query_pairs, rank_all = attention(
         lengths, tokens, gain_one_row, qkv_weight, cosine, sine, rank, n, 2
     )
-    expert_args = (ct_low, ct_high, router_weight.T, rank_all, w_gate, w_up, w_down, capacity)
+    expert_args = (ct_all, router_weight.T, rank_all, w_gate, w_up, w_down, capacity)
     if plane:
         sources = (mixed_low, tokens, out_weight, gain_two[None, :])
         y_part, gs, grad_gate, grad_up, grad_down, second_norm, residual = run_experts(
@@ -1679,38 +1725,27 @@
         )
     else:
         residual = token_f32 + dot(mixed_low, out_weight)
-    inverse_two = lax.rsqrt(jnp.mean(residual * residual, axis=-1, keepdims=True) + EPSILON)
-    unit_two = residual * inverse_two
-    if not plane:
-        second_norm = (unit_two * gain_two).astype(BF)
+        inverse_two = lax.rsqrt(jnp.mean(residual * residual, axis=-1, keepdims=True) + EPSILON)
+        second_norm = (residual * inverse_two * gain_two).astype(BF)
         sources = line_gather([second_norm], n, 3, "gather_rows")
         y_part, gs, grad_gate, grad_up, grad_down = run_experts(sources, *expert_args, plane, 7)
         gs = line_scatter(gs, n, F32, 4, "scatter_grads")
 
-    logits = dot(second_norm, router_weight)
-    chosen = jnp.where(hot, logits, NEGATIVE_LARGE)
-    gate_weights = jnp.where(hot, jnp.exp(chosen - jnp.max(chosen, axis=-1, keepdims=True)), 0.0)
-    gate_weights = gate_weights / jnp.sum(gate_weights, axis=-1, keepdims=True)
-    grad_gates = gs[:, D : D + EXPERTS] + gs[:, D + EXPERTS : D + 2 * EXPERTS]
-    grad_gates = grad_gates + gs[:, D + 2 * EXPERTS : D + 3 * EXPERTS]
-    grad_logits = (
-        gate_weights * (grad_gates - jnp.sum(gate_weights * grad_gates, axis=-1, keepdims=True))
-    ).astype(BF)
-    grad_second = gs[:, :D] + dot_nt(grad_logits, router_weight)
-    grad_router = dot_tn(second_norm, grad_logits)
-    scaled_two = grad_second * gain_two
-    grad_gain2 = jnp.sum(grad_second * unit_two, axis=0)
-    grad_residual = grad_output.astype(F32) + inverse_two * (
-        scaled_two - unit_two * jnp.mean(scaled_two * unit_two, axis=-1, keepdims=True)
+    sources = (
+        gs,
+        residual,
+        second_norm,
+        grad_output,
+        hot.astype(F32),
+        gain_two[None, :],
+        router_weight,
+        out_weight,
     )
-    grad_attn = grad_residual.astype(BF)
-    mixed_gradient = dot_nt(grad_attn, out_weight).astype(BF)
-    grad_query_acc, kv_gradient = attention_back(
-        lengths, query_pairs, kv_all, mixed_gradient, log_total, n, 5
+    grad_query_acc, kv_gradient, grad_residual, grad_attn, grad_router, gain_two_row = (
+        attention_back(lengths, query_pairs, kv_all, log_total, sources, n, 5)
     )
-    pad = jnp.zeros((D, LANES - EXPERTS), F32)
     if plane:
-        *shares, expert_sum, grad_tokens = reduce_weights(
+        *shares, mixed, grad_tokens = reduce_weights(
             grad_query_acc,
             kv_gradient,
             tokens,
@@ -1721,8 +1756,9 @@
             mixed_low,
             grad_attn,
             grad_residual,
-            jnp.concatenate([grad_router, pad], axis=1),
-            grad_gain2[None, :],
+            grad_router,
+            gain_two_row,
+            residual,
             y_part,
             n,
             6,
@@ -1746,14 +1782,17 @@
         grad_tokens = grad_residual + inverse_one * (
             scaled_one - unit_one * jnp.mean(scaled_one * unit_one, axis=-1, keepdims=True)
         )
-        grad_small = jnp.concatenate(
-            [grad_router, grad_gain1[:, None], grad_gain2[:, None], pad[:, 2:]], axis=1
-        )
+        gains = [grad_gain1[:, None], gain_two_row.T]
+        rest = grad_router[:, EXPERTS + 2 :]
+        grad_small = jnp.concatenate([grad_router[:, :EXPERTS]] + gains + [rest], axis=1)
         shares = (dot_tn(first_norm, grad_qkv_pre), dot_tn(mixed_low, grad_attn), grad_small)
         shares = [lax.psum(scatter_rows(share.astype(BF)), "group") for share in shares]
+        share_qkv, share_out, share_small = [share.astype(F32) for share in shares]
+        split = (query_width, query_width + key_width)
+        shares = jnp.split(share_qkv, split, axis=1) + [share_out, share_small]
         expert_sum = line_scatter(y_part, n, F32, 8, "scatter_outputs")
-    mixed = (residual + expert_sum).astype(BF)
-    share_qkv, share_out, share_small = [share.astype(F32) for share in shares]
+        mixed = (residual + expert_sum).astype(BF)
+    share_query, share_key, share_value, share_out, share_small = shares
 
     def sum_over_groups(value):
         if not plane:
@@ -1764,9 +1803,9 @@
         mixed,
         grad_tokens,
         share_small[:, EXPERTS],
-        share_qkv[:, :query_width],
-        share_qkv[:, query_width : query_width + key_width],
-        share_qkv[:, query_width + key_width :],
+        share_query,
+        share_key,
+        share_value,
         share_out,
         share_small[:, EXPERTS + 1],
         share_small[:, :EXPERTS],

time: 499 us -> 503 us (level)
    pallas_call x1, Pallas kernels: 60.6 us -> 46.5 us  [attention(): pl.pallas_call(functools.partial(attention_kernel, n), grid=(pairs,), out...]
    pallas_call x1, Pallas kernels: 48.1 us -> 59.9 us  [gather_weights(): pl.pallas_call(functools.partial(weights_kernel, n, pieces, widths), out_...]
    unnamed x30 -> x14, local copies, waits for them, and re-layouts: 4.42 us -> 11 us
    pallas_call x1, Pallas kernels: 50.9 us -> 56.4 us  [attention_back(): pl.pallas_call(functools.partial(attention_back_kernel, n), grid=(pairs +...]
  transfers between devices with their start and end apart: 4 -> 3, of which waited for: 0 -> 1; matrix products, arithmetic and copies ran while one was open for 4% -> 1% of each run, Pallas kernels for 48% -> 36%
where the time goes in v2:
time: 503 us; the launch traced here: 502 us
  Pallas kernels  457 us (91%)
  local copies, waits for them, and re-layouts  19.1 us (4%)
  between operations  14.5 us (3%)
  other arithmetic  5.65 us (1%)
    pallas_call x1, Pallas kernels, run_experts(): pl.pallas_call(functools.partial(expert_kernel, sizes, plane), grid=(loca...  160 us
    pallas_call x1, Pallas kernels, reduce_weights(): pl.pallas_call(functools.partial(reduce_kernel, n, pieces), out_shape=[ja...  104 us
    pallas_call x1, Pallas kernels, gather_weights(): pl.pallas_call(functools.partial(weights_kernel, n, pieces, widths), out_...  59.9 us
    pallas_call x1, Pallas kernels, attention_back(): pl.pallas_call(functools.partial(attention_back_kernel, n), grid=(pairs +...  56.4 us
    pallas_call x1, Pallas kernels, attention(): pl.pallas_call(functools.partial(attention_kernel, n), grid=(pairs,), out...  46.5 us
    pallas_call x3, Pallas kernels, widen(): pl.pallas_call(widen_kernel, grid=(value.shape[0],), out_shape=jax.ShapeD...  30.8 us
    unnamed x14, local copies, waits for them, and re-layouts  11 us
  transfers between devices with their start and end apart: 3, of which 1 were waited for; matrix products, arithmetic and copies ran while one was open for 1% of the time, Pallas kernels for 36%

profile of v2, /device:TPU:0, one launch (start us, length us, event | category | flops | bytes accessed | tf_op | source)
XLA Modules:
  0.0 501.7 jit_solution(13653512942209813677)
XLA Ops:
  9.4 0.8 copy.54
  10.4 1.9 broadcast_select_fusion.refs_5_.ct_ref
  13.0 59.9 %gather_weights.1 = (bf16[4,2,2,2,32,2048]{5,4,3,2,1,0:T(8,128)(2,1)}, bf16[4,2,2,2,32,1024]{5,4,3,2,1,0:T(8,128)(2,1)}, bf16[4,2,2,2,32,128]{5,4,3,2,1,0:T(8,128)(2,1)}, bf16[4,256,1024]{2,1,0:T(8,128)(2,1)}) custom-call(bf16[256,1024]{1,0:T(8,128)(2,1)} %refs_0_.1, bf16[256,512]{1,0:T(8,128)(2,1)} %refs_1_.2, bf16[256,512]{1,0:T(8,128)(2,1)} %refs_2_.2, ...), custom_call_target="tpu_custom_call" | custom-call | bytes 100000000 | tf_op jit(solution)/shard_map/gather_weights/pallas_call | solution.py:482
  73.0 2.0 convert_reduce_fusion
  75.0 1.7 fusion.5
  77.4 0.8 fusion.rank_ref
  78.4 0.8 copy.58.sine_ref.refs_6_
  79.2 0.8 copy.57.cosine_ref.refs_5_
  80.7 46.5 %attention.1 = (bf16[256,1024]{1,0:T(8,128)(2,1)}, f32[4,2,512]{2,1,0:T(2,128)}, bf16[1024,1024]{1,0:T(8,128)(2,1)}, bf16[4,256,256]{2,1,0:T(8,128)(2,1)}, bf16[4,32,256]{2,1,0:T(8,128)(2,1)}) custom-call(s32[1]{0:T(128)} %copy.70.length_ref, bf16[256,1024]{1,0:T(8,128)(2,1)} %refs_2_.3, f32[1,1024]{1,0:T(1,128)} %bitcast.25, bf16[1024,2048]{1,0:T(8,128)(2,1)} %bitcast.17, ...), custom_call_target="tpu_custom_call" | custom-call | flops 4294967296 | bytes 100000000 | tf_op jit(solution)/shard_map/attention/pallas_call | solution.py:1441
  127.2 160.0 %experts.1 = (bf16[1024,1024]{1,0:T(8,128)(2,1)}, f32[256,1152]{1,0:T(8,128)}, bf16[8,128,512]{2,1,0:T(8,128)(2,1)}, bf16[8,128,512]{2,1,0:T(8,128)(2,1)}, bf16[...) custom-call(bf16[256,1024]{1,0:T(8,128)(2,1)} %get-tuple-element.46.refs_0_.refs_7_, ...), custom_call_target="tpu_custom_call" | custom-call | flops 30601641984 | bytes 58720256 | tf_op jit(solution)/shard_map/experts/pallas_call | solution.py:1220
  289.4 56.4 %attention_back.1 = (f32[256,1024]{1,0:T(8,128)}, bf16[256,1024]{1,0:T(8,128)(2,1)}, f32[256,1024]{1,0:T(8,128)}, bf16[256,1024]{1,0:T(8,128)(2,1)}, f32[1024,128]{1,0:T(8,128)}, /*index=5*/f32[1,1024]{1,0:T(1,128)}) custom-call(s32[1]{0:T(128)} %copy.70.length_ref, bf16[4,256,256]{2,1,0:T(8,128)(2,1)} %get-tuple-element.43.q_ref, ...), custom_call_target="tpu_custom_call" | custom-call | flops 10737418240 | bytes 100000000 | tf_op jit(solution)/shard_map/attention_back/pallas_call | solution.py:1589
  345.8 103.9 %reduce_weights.1 = (f32[256,1024]{1,0:T(8,128)}, f32[256,512]{1,0:T(8,128)}, f32[256,512]{1,0:T(8,128)}, f32[256,1024]{1,0:T(8,128)}, f32[256,128]{1,0:T(8,128)...) custom-call(f32[256,1024]{1,0:T(8,128)} %get-tuple-element.53.refs_0_, bf16[256,1024]{1,0:T(8,128)(2,1)} %get-tuple-element.54.refs_1_, ...), custom_call_target="tpu_custom_call" | custom-call | bytes 100000000 | tf_op jit(solution)/shard_map/reduce_weights/pallas_call | solution.py:789
  449.7 1.7 copy.63
  451.4 1.8 slice_reduce_fusion
  453.2 10.3 %widen.5 = f32[8,512,1024]{2,1,0:T(8,128)} custom-call(bf16[8,512,1024]{2,1,0:T(8,128)(2,1)} %all-gather.8.cloned.1.call-done.value_ref), custom_call_target="tpu_custom_call" | custom-call | bytes 25165824 | tf_op jit(solution)/shard_map/widen/pallas_call | solution.py:1641
  463.5 10.3 %widen.4 = f32[8,1024,512]{2,1,0:T(8,128)} custom-call(bf16[8,1024,512]{2,1,0:T(8,128)(2,1)} %all-gather.6.cloned.1.call-done.value_ref), custom_call_target="tpu_custom_call" | custom-call | bytes 25165824 | tf_op jit(solution)/shard_map/widen/pallas_call | solution.py:1641
  473.8 2.6 all-gather.4.cloned.1.call-done.value_ref
  476.3 10.3 %widen.3 = f32[8,1024,512]{2,1,0:T(8,128)} custom-call(bf16[8,1024,512]{2,1,0:T(8,128)(2,1)} %all-gather.4.cloned.1.call-done.value_ref), custom_call_target="tpu_custom_call" | custom-call | bytes 25165824 | tf_op jit(solution)/shard_map/widen/pallas_call | solution.py:1641
  486.6 1.9 copy.71
  488.5 1.0 copy.72
  489.5 1.0 copy.73
  490.4 1.9 copy.74
  492.3 1.9 copy.75
  494.2 1.0 copy.76
  (30 shorter events, 6.3 us)
Async XLA Ops:
  7.2 446.0 %all-gather.8.cloned.1.call-start = ((), (), s32[]{:S(2)}) async-start(), calls=%async_computation.2 | async-start | bytes 9437184 | tf_op jit(solution)/shard_map/all_gather | solution.py:1800
  287.2 176.3 %all-gather.6.cloned.1.call-start = ((), (), s32[]{:S(2)}) async-start(), calls=%async_computation.1 | async-start | bytes 9437184 | tf_op jit(solution)/shard_map/all_gather | solution.py:1800
  287.9 188.4 %all-gather.4.cloned.1.call-start = ((), (), s32[]{:S(2)}) async-start(), calls=%async_computation | async-start | bytes 9437184 | tf_op jit(solution)/shard_map/all_gather | solution.py:1800
  473.8 14.7 %copy-start.2 = (f32[256,1024]{1,0:T(8,128)S(1)}, f32[256,1024]{1,0:T(8,128)}, u32[]{:S(2)}) copy-start(f32[256,1024]{1,0:T(8,128)} %get-tuple-element.140) | copy-start | bytes 3145732
  473.8 15.7 %copy-start.1 = (f32[256,1024]{1,0:T(8,128)S(1)}, f32[256,1024]{1,0:T(8,128)}, u32[]{:S(2)}) copy-start(f32[256,1024]{1,0:T(8,128)} %get-tuple-element.142) | copy-start | bytes 3145732
  473.8 20.4 %copy-start = (f32[256,1024]{1,0:T(8,128)S(1)}, f32[256,1024]{1,0:T(8,128)}, u32[]{:S(2)}) copy-start(f32[256,1024]{1,0:T(8,128)} %get-tuple-element.145) | copy-start | bytes 3145732
Sparse Core Ops, SparseCore 0:
  287.3 52.5 all-gather.7
  341.8 72.6 all-gather.5
  416.4 59.9 all-gather.3

commit v3 on v2

--- a/solution.py
+++ b/solution.py
@@ -384,6 +384,21 @@
             return [(0, me, me >= 0)]
         return [(step, me - step, me - step >= 0), (n - 1 + step, me + step, me + step < n)]
 
+    def extra_step(far):
+        for side in (0, 1):
+            if far > 0:
+
+                @pl.when(me - far >= 0 if side == 0 else me + far < n)
+                def _():
+                    extra_hop(far - 1, side).wait_recv()
+
+        for side in (0, 1):
+            if far < n - 1:
+
+                @pl.when(sends(far, side))
+                def _():
+                    extra_hop(far, side).start()
+
     count = len(pieces)
     for step in range(n + 2):
         if step < n:
@@ -429,19 +444,12 @@
                     for i in range(3):
                         third(slot, block, i).start()
 
-        for side in (0, 1):
-            if 2 <= step < n + 1:
-
-                @pl.when(me - step + 1 >= 0 if side == 0 else me + step - 1 < n)
-                def _():
-                    extra_hop(step - 2, side).wait_recv()
-
-        for side in (0, 1):
-            if 1 <= step < n:
-
-                @pl.when(sends(step - 1, side))
-                def _():
-                    extra_hop(step - 1, side).start()
+        if step == 1:
+            extra_step(0)
+        elif step >= n:
+            extra_step(step - n + 1)
+    for far in range(3, n):
+        extra_step(far)
 
     for step in range(n):
         for slot, block, there in held(step):
@@ -517,15 +525,13 @@
         sine_ref,
         mixed_ref,
         grad_attn_ref,
-        grad_residual_ref,
         router_ref,
         gain_two_ref,
-        residual_ref,
         y_part,
-    ) = refs[:14]
-    q_out, k_out, v_out, o_out, small_out, mixed_out, grad_tokens_ref = refs[14:21]
-    ins, grad_pre_ref, outs, y_out = refs[21:24], refs[24], refs[25:27], refs[27]
-    refs = refs[28:]
+    ) = refs[:12]
+    outs, y_out, grad_tokens_ref = refs[12:14], refs[14], refs[15]
+    ins, grad_pre_ref = refs[16:19], refs[19]
+    refs = refs[20:]
     pair, one, two, landing, staging = refs[:2], refs[2:4], refs[4:6], refs[6:8], refs[8:10]
     csend, crecv, psend, precv, zsend, zrecv, gsend, grecv = refs[10:18]
     line = LineSum(n, y_part, *refs[18:])
@@ -568,7 +574,7 @@
         put(1, columns, dot_tn(mixed_ref[...], grad_attn_ref[:, columns]))
     swap(2).start()
     unit, inverse = normed(tokens_ref)
-    gain = gain_ref[...]
+    gain = gain_ref[0:1, :]
     first_norm = (unit * gain).astype(BF)
     cosine, sine = cosine_ref[...], -sine_ref[...]
     for j in range(query_width // LANES):
@@ -595,7 +601,7 @@
     swap(3).start()
     scaled = grad_first * gain
     mean = jnp.mean(scaled * unit, axis=-1, keepdims=True)
-    grad_tokens_ref[...] = grad_residual_ref[...] + inverse * (scaled - unit * mean)
+    grad_tokens_ref[...] = inverse * (scaled - unit * mean)
     for p in range(len(places)):
         swap(p).wait_recv()
         array, start, width, path, at = places[p]
@@ -719,17 +725,8 @@
             spread(path, stage).start()
         if stage == 0:
             line.finish(y_out)
-            mixed_out[...] = (residual_ref[...] + y_out[...]).astype(BF)
         for path in (0, 1):
             spread(path, stage).wait_recv()
-
-    flat = [out[...].reshape(-1, out.shape[4]).astype(F32) for out in outs]
-    columns = ([(0, q_out), (0, k_out)], [(1, v_out), (1, o_out)], [(0, small_out)])
-    starts = [0, 0]
-    for path, target in itertools.chain(*columns):
-        width = target.shape[1]
-        target[...] = flat[path][:, starts[path] : starts[path] + width]
-        starts[path] += width
 
     for path in (0, 1):
         for stage in range(3):
@@ -759,10 +756,8 @@
     sine,
     mixed_low,
     grad_attn,
-    grad_residual,
     grad_router,
     gain_two_row,
-    residual,
     y_part,
     n,
     collective_id,
@@ -777,21 +772,18 @@
     widths = [sum(p[2] for p in pieces if p[3]), sum(p[2] for p in pieces if not p[3])]
     scratch = [pltpu.VMEM((n, 2, 2, 2, eighth, w), BF) for w in array_widths]
     scratch += [pltpu.VMEM((grad_q.shape[0], width_all), BF)]
-    scratch += [pltpu.VMEM((2, 2, 2, eighth, w), BF) for w in widths]
-    scratch += [pltpu.VMEM((y_part.shape[0] // n, y_part.shape[1]), F32)]
     scratch += [pltpu.VMEM((n, 2, 2, eighth, w), BF) for w in widths]
     scratch += [pltpu.VMEM((n, 2, eighth, w), BF) for w in widths]
     scratch += [pltpu.VMEM((n, eighth, w), BF) for w in widths]
     scratch += [pltpu.VMEM((2, n - 1, eighth, w), BF) for w in widths] * 2
     sems = [(4,), (4,), (2, 2), (2, 2), (2, 2, n - 1), (2, 2, n - 1), (2, 3), (2, 3)]
     y_rows = y_part.shape[0] // n
-    out_widths = (query_width, key_width, key_width, grad_attn.shape[1], LANES)
-    return pl.pallas_call(
+    first, second, y_sum, grad_rest = pl.pallas_call(
         functools.partial(reduce_kernel, n, pieces),
-        out_shape=[jax.ShapeDtypeStruct((rows, w), F32) for w in out_widths]
-        + [jax.ShapeDtypeStruct(tokens.shape, BF), jax.ShapeDtypeStruct(tokens.shape, F32)],
-        in_specs=[IN_VMEM] * 14,
-        out_specs=[IN_VMEM] * 7,
+        out_shape=[jax.ShapeDtypeStruct((2, 2, 2, eighth, w), BF) for w in widths]
+        + [jax.ShapeDtypeStruct(tokens.shape, F32)] * 2,
+        in_specs=[IN_VMEM] * 12,
+        out_specs=[IN_VMEM] * 4,
         scratch_shapes=scratch
         + [pltpu.SemaphoreType.DMA(s) for s in sems]
         + line_sum_scratch(n, y_rows, y_part.shape[1]),
@@ -810,12 +802,14 @@
         sine,
         mixed_low,
         grad_attn,
-        grad_residual,
         grad_router,
         gain_two_row,
-        residual,
         y_part.reshape(n, y_rows, y_part.shape[1]),
     )
+    first, second = [o.reshape(rows, w) for o, w in zip((first, second), widths)]
+    first = jnp.split(first, (query_width, query_width + key_width), axis=1)
+    second = jnp.split(second, (key_width,), axis=1)
+    return first[0], first[1], second[0], second[1], first[2], y_sum, grad_rest
 
 
 def plane_tick(step, local):
@@ -832,7 +826,7 @@
     else:
         x_ref = refs[0]
         refs = refs[1:]
-    ct_ref, router_t_ref, rank_all_ref = refs[:3]
+    ct_ref, router_ref, rank_all_ref = refs[:3]
     w_gate_ref, w_up_ref, w_down_ref = refs[3:6]
     y_ref, gs_ref, out_gate_ref, out_up_ref, out_down_ref = refs[6:11]
     refs = refs[11:]
@@ -873,10 +867,12 @@
         return jnp.concatenate(pieces, axis=0)
 
     def dispatch_grads(b):
-        g_ref[b] = dot(pick(b), ct_ref[b]).astype(BF)
+        g_ref[b] = dot(pick(b), ct_ref[b, :rows, :]).astype(BF)
 
     def dispatch_rows(b):
-        logits = dot_nt(router_t_ref[...], x_ref[b])
+        logits = lax.dot_general(
+            router_ref[...], x_ref[b], (((0,), (1,)), ((), ())), preferred_element_type=F32
+        )[:EXPERTS]
         hot = rank_all_ref[b].astype(F32) < 200.0
         top = jnp.max(jnp.where(hot, logits, NEGATIVE_LARGE), axis=0, keepdims=True)
         weight = jnp.where(hot, jnp.exp(jnp.minimum(logits - top, 0.0)), 0.0)
@@ -923,7 +919,7 @@
             out_weight = stage_refs[2][2:4].reshape(D, D)
             residual = xs_ref[0, :rows, :].astype(F32) + dot(xs_ref[1, :rows, :], out_weight)
             inverse = lax.rsqrt(jnp.mean(residual * residual, axis=-1, keepdims=True) + EPSILON)
-            x_ref[me] = (residual * inverse * gain_ref[...]).astype(BF)
+            x_ref[me] = (residual * inverse * gain_ref[1:2, :]).astype(BF)
             gs_ref[:, :D] = residual
             greet([(None, by_c), (None, by_x), (None, by_y)] + line.neighbours())
             for side in (0, 1):
@@ -1161,7 +1157,7 @@
 
 
 def run_experts(
-    sources, ct_all, router_t, rank_all, w_gate, w_up, w_down, capacity, plane, collective_id
+    sources, ct_all, router, rank_all, w_gate, w_up, w_down, capacity, plane, collective_id
 ):
     blocks, _, rows = rank_all.shape
     total, local = blocks * rows, w_gate.shape[0]
@@ -1172,7 +1168,6 @@
     )
     per = lambda shape: pl.BlockSpec((1,) + shape, lambda e: (jnp.minimum(e, local - 1), 0, 0))
     shapes = ((D, FF), (D, FF), (FF, D))
-    ct_all = ct_all.reshape(blocks, rows, D)
     scratch = [
         pltpu.VMEM((blocks, slots, D), BF),
         pltpu.VMEM((blocks, slots, D), BF),
@@ -1229,7 +1224,7 @@
         in_specs=source_specs
         + [
             whole(ct_all.shape),
-            whole((EXPERTS, D)),
+            whole(router.shape),
             whole(rank_all.shape),
         ]
         + [per(shape) for shape in shapes],
@@ -1240,7 +1235,7 @@
             flops=flops, bytes_accessed=2 * (6 * local * D * FF + 4 * total * D), transcendentals=0
         ),
         name="experts",
-    )(*sources, ct_all, router_t, rank_all, w_gate, w_up, w_down)
+    )(*sources, ct_all, router, rank_all, w_gate, w_up, w_down)
 
 
 def rotate(tile, cosine, sine):
@@ -1287,7 +1282,7 @@
     weight_ref,
     cosine_ref,
     sine_ref,
-    rank_ref,
+    routes_ref,
     mixed_ref,
     log_total_ref,
     kv_all_ref,
@@ -1315,7 +1310,7 @@
 
     def rank_hop(step, side):
         block = me - step if side == 0 else me + step
-        source = rank_ref if step == 0 else rank_buffer.at[block]
+        source = rank_buffer.at[block]
         index = (side, step)
         return remote(
             source,
@@ -1359,7 +1354,7 @@
     @pl.when(pair == 0)
     def _():
         unit, _ = normed(tokens_ref)
-        first_norm = (unit * gain_ref[...]).astype(BF)
+        first_norm = (unit * gain_ref[0:1, :]).astype(BF)
         cosine, sine = cosine_ref[...], sine_ref[...]
         count = kv_ref.shape[0]
         query_width = count * width
@@ -1370,10 +1365,18 @@
             columns = slice(j * LANES, (j + 1) * LANES)
             kv_ref[j, :, :LANES] = rotate(keys[:, columns], cosine, sine).astype(BF)
             kv_ref[j, :, LANES:] = values[:, columns].astype(BF)
-        rank_buffer[me] = rank_ref[...]
         greet([(me > 0, left), (me < n - 1, right)])
         launch(chunk(0), 0)
         launch(chunk(1), 0)
+        routes = routes_ref[...].astype(F32).T
+        expert_id = lax.broadcasted_iota(jnp.int32, (EXPERTS, rows), 0).astype(F32)
+        hot = jnp.zeros((EXPERTS, rows), F32)
+        for k in range(TOP):
+            hot = jnp.where(routes[k : k + 1, :] == expert_id, 1.0, hot)
+        row_id = lax.broadcasted_iota(jnp.int32, (rows, rows), 0)
+        earlier = jnp.where(row_id < lax.broadcasted_iota(jnp.int32, (rows, rows), 1), 1.0, 0.0)
+        rank = dot(hot.astype(BF), earlier.astype(BF))
+        rank_buffer[me] = jnp.where(hot > 0.5, rank, 255.0).astype(BF)
         queries = dot(first_norm, weight_ref[:, :query_width])
         for j in range(2 * count):
             start = (j % 2) * LANES
@@ -1434,8 +1437,9 @@
             drain(chunk(j))
 
 
-def attention(length, tokens, gain, weight, cosine, sine, rank, n, collective_id):
+def attention(length, tokens, gain, weight, cosine, sine, routes, n, collective_id):
     rows = tokens.shape[0]
+    rank = jax.ShapeDtypeStruct((EXPERTS, rows), BF)
     keys, width = n * rows, 2 * LANES
     pairs = KEY_VALUE_HEADS // 2
     return pl.pallas_call(
@@ -1477,7 +1481,7 @@
             flops=16 * rows * keys * D, bytes_accessed=100000000, transcendentals=0
         ),
         name="attention",
-    )(length, tokens, gain, weight, cosine, sine, rank)
+    )(length, tokens, gain, weight, cosine, sine, routes)
 
 
 def attention_back_kernel(
@@ -1490,7 +1494,7 @@
     residual_ref,
     second_ref,
     ct_ref,
-    hot_ref,
+    routes_ref,
     gain_ref,
     router_ref,
     out_weight_ref,
@@ -1519,8 +1523,12 @@
     def _():
         greet(line(0).neighbours())
         mask_bias(bias_ref, length_ref, q_ref.shape[1])
-        hot = hot_ref[...] > 0.5
-        second, router = second_ref[...], router_ref[...]
+        routes = routes_ref[...]
+        expert_id = lax.broadcasted_iota(jnp.int32, (routes.shape[0], EXPERTS), 1)
+        hot = expert_id == routes[:, 0:1]
+        for k in range(1, TOP):
+            hot = hot | (expert_id == routes[:, k : k + 1])
+        second, router = second_ref[...], router_ref[:, :EXPERTS]
         logits = dot(second, router)
         top = jnp.max(jnp.where(hot, logits, NEGATIVE_LARGE), axis=-1, keepdims=True)
         weight = jnp.where(hot, jnp.exp(jnp.minimum(logits - top, 0.0)), 0.0)
@@ -1534,7 +1542,7 @@
         grad_router_ref[:, :EXPERTS] = dot_tn(second, grad_logits)
         unit, inverse = normed(residual_ref)
         grad_gain_ref[...] = jnp.sum(grad_second * unit, axis=0, keepdims=True)
-        scaled = grad_second * gain_ref[...]
+        scaled = grad_second * gain_ref[1:2, :]
         mean = jnp.mean(scaled * unit, axis=-1, keepdims=True)
         grad_residual = ct_ref[...].astype(F32) + inverse * (scaled - unit * mean)
         grad_residual_ref[...] = grad_residual
@@ -1691,42 +1699,40 @@
     valid_rows = (positions < length)[:, None]
     grad_output = jnp.where(valid_rows, cotangent, jnp.zeros_like(cotangent))
 
-    small = jnp.concatenate(
-        [w_router, norm_gain1[:, None], norm_gain2[:, None]]
-        + [jnp.zeros((w_router.shape[0], LANES - EXPERTS - 2), BF)],
-        axis=1,
+    small = jnp.pad(w_router, ((0, 0), (0, LANES - EXPERTS)))
+    gains = jnp.pad(jnp.concatenate([norm_gain1, norm_gain2]), (0, D - 2 * norm_gain1.shape[0]))
+    below = jnp.broadcast_to(gains, (16, D))
+    qkv_weight, out_weight, router, extra_all = gather_weights(
+        w_query,
+        key_projection,
+        value_projection,
+        w_out,
+        small,
+        jnp.concatenate([grad_output, below], axis=0),
+        n,
+        1,
     )
-    qkv_weight, out_weight, small, ct_all = gather_weights(
-        w_query, key_projection, value_projection, w_out, small, grad_output, n, 1
-    )
-    router_weight = small[:, :EXPERTS]
-    gain_one = small[:, EXPERTS].astype(F32)
-    gain_two = small[:, EXPERTS + 1].astype(F32)
-
-    expert_ids = jnp.arange(EXPERTS, dtype=jnp.int32)
-    hot = jnp.any(routes[:, :, None] == expert_ids, axis=1)
-    row_id = jnp.arange(rows, dtype=jnp.int32)
-    earlier = (row_id[:, None] < row_id[None, :]).astype(BF)
-    rank = jnp.where(hot.T, dot(hot.T.astype(BF), earlier), 255.0).astype(BF)
+    extra_all = extra_all.reshape(n, rows + 16, D)
+    gains = extra_all[:, rows, : 2 * norm_gain1.shape[0]].reshape(n, 2, -1)
+    gains = jnp.transpose(gains, (1, 0, 2)).reshape(2, D).astype(F32)
 
     cosine_lookup, sine_lookup = [table[:, 0] for table in rotary_tables(positions, HEAD_DIMENSION)]
     cosine = jnp.tile(cosine_lookup, (1, 4))
     sine = jnp.tile(jnp.concatenate([-sine_lookup, sine_lookup], axis=1), (1, 2))
     token_f32 = tokens.astype(F32)
-    gain_one_row = gain_one[None, :]
     mixed_low, log_total, kv_all, query_pairs, rank_all = attention(
-        lengths, tokens, gain_one_row, qkv_weight, cosine, sine, rank, n, 2
+        lengths, tokens, gains, qkv_weight, cosine, sine, routes, n, 2
     )
-    expert_args = (ct_all, router_weight.T, rank_all, w_gate, w_up, w_down, capacity)
+    expert_args = (extra_all, router, rank_all, w_gate, w_up, w_down, capacity)
     if plane:
-        sources = (mixed_low, tokens, out_weight, gain_two[None, :])
+        sources = (mixed_low, tokens, out_weight, gains)
         y_part, gs, grad_gate, grad_up, grad_down, second_norm, residual = run_experts(
             sources, *expert_args, plane, 7
         )
     else:
         residual = token_f32 + dot(mixed_low, out_weight)
         inverse_two = lax.rsqrt(jnp.mean(residual * residual, axis=-1, keepdims=True) + EPSILON)
-        second_norm = (residual * inverse_two * gain_two).astype(BF)
+        second_norm = (residual * inverse_two * gains[1]).astype(BF)
         sources = line_gather([second_norm], n, 3, "gather_rows")
         y_part, gs, grad_gate, grad_up, grad_down = run_experts(sources, *expert_args, plane, 7)
         gs = line_scatter(gs, n, F32, 4, "scatter_grads")
@@ -1736,37 +1742,36 @@
         residual,
         second_norm,
         grad_output,
-        hot.astype(F32),
-        gain_two[None, :],
-        router_weight,
+        routes,
+        gains,
+        router,
         out_weight,
     )
     grad_query_acc, kv_gradient, grad_residual, grad_attn, grad_router, gain_two_row = (
         attention_back(lengths, query_pairs, kv_all, log_total, sources, n, 5)
     )
     if plane:
-        *shares, mixed, grad_tokens = reduce_weights(
+        *shares, expert_sum, grad_rest = reduce_weights(
             grad_query_acc,
             kv_gradient,
             tokens,
-            gain_one_row,
+            gains,
             qkv_weight,
             cosine,
             sine,
             mixed_low,
             grad_attn,
-            grad_residual,
             grad_router,
             gain_two_row,
-            residual,
             y_part,
             n,
             6,
         )
+        grad_tokens = grad_residual + grad_rest
     else:
         inverse_one = lax.rsqrt(jnp.mean(token_f32 * token_f32, axis=-1, keepdims=True) + EPSILON)
         unit_one = token_f32 * inverse_one
-        first_norm = (unit_one * gain_one).astype(BF)
+        first_norm = (unit_one * gains[0]).astype(BF)
         own_key_gradient, own_value_gradient = unpair_columns(kv_gradient)
         back = lambda value: apply_rotation(
             value.astype(F32).reshape(rows, -1, HEAD_DIMENSION),
@@ -1777,7 +1782,7 @@
         grad_key_pre = back(own_key_gradient).reshape(rows, key_width).astype(BF)
         grad_qkv_pre = jnp.concatenate([grad_query_pre, grad_key_pre, own_value_gradient], axis=1)
         grad_first = dot_nt(grad_qkv_pre, qkv_weight)
-        scaled_one = grad_first * gain_one
+        scaled_one = grad_first * gains[0]
         grad_gain1 = jnp.sum(grad_first * unit_one, axis=0)
         grad_tokens = grad_residual + inverse_one * (
             scaled_one - unit_one * jnp.mean(scaled_one * unit_one, axis=-1, keepdims=True)
@@ -1787,11 +1792,12 @@
         grad_small = jnp.concatenate([grad_router[:, :EXPERTS]] + gains + [rest], axis=1)
         shares = (dot_tn(first_norm, grad_qkv_pre), dot_tn(mixed_low, grad_attn), grad_small)
         shares = [lax.psum(scatter_rows(share.astype(BF)), "group") for share in shares]
-        share_qkv, share_out, share_small = [share.astype(F32) for share in shares]
+        share_qkv, share_out, share_small = shares
         split = (query_width, query_width + key_width)
         shares = jnp.split(share_qkv, split, axis=1) + [share_out, share_small]
         expert_sum = line_scatter(y_part, n, F32, 8, "scatter_outputs")
-        mixed = (residual + expert_sum).astype(BF)
+    mixed = (residual + expert_sum).astype(BF)
+    shares = [share.astype(F32) for share in shares]
     share_query, share_key, share_value, share_out, share_small = shares
 
     def sum_over_groups(value):

time: 503 us -> 494 us (0.982)
  local copies, waits for them, and re-layouts: 19.1 us -> 7.46 us
  other arithmetic: 5.65 us -> 10.8 us
    unnamed x14 -> x16, local copies, waits for them, and re-layouts: 11 us -> 3.06 us
  transfers between devices with their start and end apart: 3 -> 3, of which waited for: 1 -> 0; matrix products, arithmetic and copies ran while one was open for 1% -> 2% of each run, Pallas kernels for 36% -> 37%
where the time goes in v3:
time: 494 us; the launch traced here: 493 us
  Pallas kernels  459 us (93%)
  between operations  14.6 us (3%)
  other arithmetic  10.8 us (2%)
  local copies, waits for them, and re-layouts  7.46 us (2%)
    pallas_call x1, Pallas kernels, run_experts(): pl.pallas_call(functools.partial(expert_kernel, sizes, plane), grid=(loca...  158 us
    pallas_call x1, Pallas kernels, reduce_weights(): pl.pallas_call(functools.partial(reduce_kernel, n, pieces), out_shape=[ja...  104 us
    pallas_call x1, Pallas kernels, gather_weights(): pl.pallas_call(functools.partial(weights_kernel, n, pieces, widths), out_...  64.2 us
    pallas_call x1, Pallas kernels, attention_back(): pl.pallas_call(functools.partial(attention_back_kernel, n), grid=(pairs +...  56.6 us
    pallas_call x1, Pallas kernels, attention(): pl.pallas_call(functools.partial(attention_kernel, n), grid=(pairs,), out...  44.1 us
    pallas_call x3, Pallas kernels, widen(): pl.pallas_call(widen_kernel, grid=(value.shape[0],), out_shape=jax.ShapeD...  31.2 us
  transfers between devices with their start and end apart: 3, of which 0 were waited for; matrix products, arithmetic and copies ran while one was open for 2% of the time, Pallas kernels for 37%

profile of v3, /device:TPU:0, one launch (start us, length us, event | category | flops | bytes accessed | tf_op | source)
XLA Modules:
  0.0 493.2 jit_solution(17929602839730485631)
XLA Ops:
  7.9 0.8 copy.31
  9.0 0.8 copy.34.sine_ref.refs_6_
  9.7 1.5 copy.35.routes_ref
  11.2 0.8 copy.33.cosine_ref.refs_5_
  12.0 0.7 fusion.3
  12.7 0.6 pad.8.refs_4_
  13.3 1.1 broadcast_select_fusion.ct_ref
  14.5 0.9 pad_maximum_fusion.refs_5_
  15.4 64.2 %gather_weights.1 = (bf16[4,2,2,2,32,2048]{5,4,3,2,1,0:T(8,128)(2,1)}, bf16[4,2,2,2,32,1024]{5,4,3,2,1,0:T(8,128)(2,1)}, bf16[4,2,2,2,32,128]{5,4,3,2,1,0:T(8,128)(2,1)}, bf16[4,272,1024]{2,1,0:T(8,128)(2,1)}) custom-call(bf16[256,1024]{1,0:T(8,128)(2,1)} %refs_0_.1, bf16[256,512]{1,0:T(8,128)(2,1)} %refs_1_.2, bf16[256,512]{1,0:T(8,128)(2,1)} %refs_2_.2, ...), custom_call_target="tpu_custom_call" | custom-call | bytes 100000000 | tf_op jit(solution)/shard_map/gather_weights/pallas_call | solution.py:490
  79.6 0.8 convert_reduce_fusion
  81.0 44.1 %attention.1 = (bf16[256,1024]{1,0:T(8,128)(2,1)}, f32[4,2,512]{2,1,0:T(2,128)}, bf16[1024,1024]{1,0:T(8,128)(2,1)}, bf16[4,256,256]{2,1,0:T(8,128)(2,1)}, bf16[4,32,256]{2,1,0:T(8,128)(2,1)}) custom-call(s32[1]{0:T(128)} %copy.42.length_ref, bf16[256,1024]{1,0:T(8,128)(2,1)} %refs_2_.3, f32[2,1024]{1,0:T(2,128)} %bitcast.29, bf16[1024,2048]{1,0:T(8,128)(2,1)} %bitcast.18, ...), custom_call_target="tpu_custom_call" | custom-call | flops 4294967296 | bytes 100000000 | tf_op jit(solution)/shard_map/attention/pallas_call | solution.py:1445
  125.1 158.4 %experts.1 = (bf16[1024,1024]{1,0:T(8,128)(2,1)}, f32[256,1152]{1,0:T(8,128)}, bf16[8,128,512]{2,1,0:T(8,128)(2,1)}, bf16[8,128,512]{2,1,0:T(8,128)(2,1)}, bf16[...) custom-call(bf16[256,1024]{1,0:T(8,128)(2,1)} %get-tuple-element.40.refs_0_.refs_7_, ...), custom_call_target="tpu_custom_call" | custom-call | flops 30601641984 | bytes 58720256 | tf_op jit(solution)/shard_map/experts/pallas_call | solution.py:1215
  283.6 0.7 all-gather.6.cloned.1.call-update
  284.3 0.7 all-gather.4.cloned.1.call-update
  285.0 56.6 %attention_back.1 = (f32[256,1024]{1,0:T(8,128)}, bf16[256,1024]{1,0:T(8,128)(2,1)}, f32[256,1024]{1,0:T(8,128)}, bf16[256,1024]{1,0:T(8,128)(2,1)}, f32[1024,128]{1,0:T(8,128)}, /*index=5*/f32[1,1024]{1,0:T(1,128)}) custom-call(s32[1]{0:T(128)} %copy.42.length_ref, bf16[4,256,256]{2,1,0:T(8,128)(2,1)} %get-tuple-element.45.q_ref, ...), custom_call_target="tpu_custom_call" | custom-call | flops 10737418240 | bytes 100000000 | tf_op jit(solution)/shard_map/attention_back/pallas_call | solution.py:1597
  341.6 104.4 %reduce_weights.1 = (bf16[2,2,2,32,1664]{4,3,2,1,0:T(8,128)(2,1)}, bf16[2,2,2,32,1536]{4,3,2,1,0:T(8,128)(2,1)}, f32[256,1024]{1,0:T(8,128)}, f32[256,1024]{1,0:T(8,128)}) custom-call(f32[256,1024]{1,0:T(8,128)} %get-tuple-element.50.refs_0_, bf16[256,1024]{1,0:T(8,128)(2,1)} %get-tuple-element.51.refs_1_, bf16[256,1024]{1,0:T(8,128)(2,1)} %refs_2_.3, ...), custom_call_target="tpu_custom_call" | custom-call | bytes 100000000 | tf_op jit(solution)/shard_map/reduce_weights/pallas_call | solution.py:781
  446.0 1.0 split.20
  447.8 2.4 add.26
  450.8 2.1 slice_convert_fusion.2
  452.9 0.9 add_convert_fusion
  453.9 1.6 slice_convert_fusion
  455.4 10.6 %widen.5 = f32[8,512,1024]{2,1,0:T(8,128)} custom-call(bf16[8,512,1024]{2,1,0:T(8,128)(2,1)} %all-gather.8.cloned.1.call-done.value_ref), custom_call_target="tpu_custom_call" | custom-call | bytes 25165824 | tf_op jit(solution)/shard_map/widen/pallas_call | solution.py:1649
  466.0 10.3 %widen.4 = f32[8,1024,512]{2,1,0:T(8,128)} custom-call(bf16[8,1024,512]{2,1,0:T(8,128)(2,1)} %all-gather.6.cloned.1.call-done.value_ref), custom_call_target="tpu_custom_call" | custom-call | bytes 25165824 | tf_op jit(solution)/shard_map/widen/pallas_call | solution.py:1649
  476.4 10.3 %widen.3 = f32[8,1024,512]{2,1,0:T(8,128)} custom-call(bf16[8,1024,512]{2,1,0:T(8,128)(2,1)} %all-gather.4.cloned.1.call-done.value_ref), custom_call_target="tpu_custom_call" | custom-call | bytes 25165824 | tf_op jit(solution)/shard_map/widen/pallas_call | solution.py:1649
  (31 shorter events, 2.3 us)
Async XLA Ops:
  7.2 448.3 %all-gather.8.cloned.1.call-start = ((), (), s32[]{:S(2)}) async-start(), calls=%async_computation.2 | async-start | bytes 9437184 | tf_op jit(solution)/shard_map/all_gather | solution.py:1806
  14.5 110.6 %copy-start = (bf16[256,1024]{1,0:T(8,128)(2,1)}, bf16[256,1024]{1,0:T(8,128)(2,1)S(1)}, u32[]{:S(2)}) copy-start(bf16[256,1024]{1,0:T(8,128)(2,1)S(1)} %broadcast_select_fusion.ct_ref) | copy-start | bytes 1572868
  283.5 182.5 %all-gather.6.cloned.1.call-start = ((), (), s32[]{:S(2)}) async-start(), calls=%async_computation.1 | async-start | bytes 9437184 | tf_op jit(solution)/shard_map/all_gather | solution.py:1806
  284.3 192.1 %all-gather.4.cloned.1.call-start = ((), (), s32[]{:S(2)}) async-start(), calls=%async_computation | async-start | bytes 9437184 | tf_op jit(solution)/shard_map/all_gather | solution.py:1806
  341.6 106.2 %copy-start.1 = (f32[256,1024]{1,0:T(8,128)S(1)}, f32[256,1024]{1,0:T(8,128)}, u32[]{:S(2)}) copy-start(f32[256,1024]{1,0:T(8,128)} %get-tuple-element.57) | copy-start | bytes 3145732
  446.0 6.9 %copy-start.2 = (f32[256,1024]{1,0:T(8,128)S(1)}, f32[256,1024]{1,0:T(8,128)}, u32[]{:S(2)}) copy-start(f32[256,1024]{1,0:T(8,128)} %get-tuple-element.44.residual_ref) | copy-start | bytes 3145732
  446.0 6.9 %copy-start.3 = (f32[256,1024]{1,0:T(8,128)S(1)}, f32[256,1024]{1,0:T(8,128)}, u32[]{:S(2)}) copy-start(f32[256,1024]{1,0:T(8,128)} %get-tuple-element.56) | copy-start | bytes 3145732
  447.1 6.7 %copy-start.4 = (bf16[2,2,2,32,1664]{4,3,2,1,0:T(8,128)(2,1)S(1)}, bf16[2,2,2,32,1664]{4,3,2,1,0:T(8,128)(2,1)}, u32[]{:S(2)}) copy-start(bf16[2,2,2,32,1664]{4,3,2,1,0:T(8,128)(2,1)} %get-tuple-element.59) | copy-start | bytes 2555908
  447.1 6.7 %copy-start.5 = (bf16[2,2,2,32,1536]{4,3,2,1,0:T(8,128)(2,1)S(1)}, bf16[2,2,2,32,1536]{4,3,2,1,0:T(8,128)(2,1)}, u32[]{:S(2)}) copy-start(bf16[2,2,2,32,1536]{4,3,2,1,0:T(8,128)(2,1)} %get-tuple-element.60) | copy-start | bytes 2359300
Sparse Core Ops, SparseCore 0:
  283.6 53.2 all-gather.7
  338.9 72.6 all-gather.5
  413.5 59.0 all-gather.3

commit v4 on v3

--- a/solution.py
+++ b/solution.py
@@ -295,6 +295,76 @@
     c, x, y = group % 2, (group // 2) % 2, (group // 4) % 2
     by_c, by_x, by_y = (group + 1 - 2 * c, me), (group + 2 - 4 * x, me), (group + 4 - 8 * y, me)
     return group, me, (y, x, c), (by_y, by_x, by_c)
+
+
+class PlaneGather:
+    def __init__(self, owns, outs, start, local, send, receive):
+        self.owns, self.outs, self.first_expert = owns, outs, start
+        self.local, self.send, self.receive = local, send, receive
+        _, _, (self.y, self.x, self.c), self.partners = plane_position()
+        self.part = outs[0].shape[0] // 2
+
+    def copy(self, i, path, stage):
+        y, x, c = self.y, self.x, self.c
+        by_y, by_x, by_c = self.partners
+        span = slice(path * self.part, (path + 1) * self.part)
+        out = self.outs[i]
+        near = out.at[span, y, :, c] if path == 0 else out.at[span, :, x, c]
+        far = out.at[span, 1 - y, :, c] if path == 0 else out.at[span, :, 1 - x, c]
+        if stage == 0:
+            start = self.first_expert + path * self.part
+            source, target = self.owns[i].at[start : start + self.part], out.at[span, y, x, c]
+        else:
+            source = far if stage == 3 else near
+            target = source
+        device = (by_x, by_y, by_c, by_c)[stage] if path == 0 else (by_y, by_x, by_c, by_c)[stage]
+        index = (i, path, stage)
+        return remote(source, target, self.send.at[index], self.receive.at[index], device)
+
+    def all(self, stage):
+        return [self.copy(i, path, stage) for i in range(len(self.outs)) for path in (0, 1)]
+
+    def stores(self):
+        span = slice(self.first_expert, self.first_expert + 2 * self.part)
+        return [
+            pltpu.make_async_copy(
+                own.at[span], out.at[:, self.y, self.x, self.c], self.local.at[i]
+            )
+            for i, (own, out) in enumerate(zip(self.owns, self.outs))
+        ]
+
+    def begin(self):
+        for copy in self.all(0) + self.stores():
+            copy.start()
+
+    def second(self):
+        for copy in self.stores():
+            copy.wait()
+        for copy in self.all(0):
+            copy.wait_recv()
+        for copy in self.all(1) + self.all(2):
+            copy.start()
+
+    def third(self):
+        for copy in self.all(1):
+            copy.wait_recv()
+        for copy in self.all(3):
+            copy.start()
+
+    def finish(self):
+        for copy in self.all(0) + self.all(1):
+            copy.wait_send()
+        for copy in self.all(2) + self.all(3):
+            copy.wait()
+
+
+def plane_gather_sems():
+    return [pltpu.SemaphoreType.DMA((3,))] + [pltpu.SemaphoreType.DMA((3, 2, 4))] * 2
+
+
+def plane_gather_shapes(owns):
+    half = owns[0].shape[0] // 2
+    return [jax.ShapeDtypeStruct((half, 2, 2, 2) + own.shape[1:], own.dtype) for own in owns]
 
 
 def weights_kernel(n, pieces, widths, *refs):
@@ -529,9 +599,10 @@
         gain_two_ref,
         y_part,
     ) = refs[:12]
-    outs, y_out, grad_tokens_ref = refs[12:14], refs[14], refs[15]
-    ins, grad_pre_ref = refs[16:19], refs[19]
-    refs = refs[20:]
+    owns, outs, y_out, grad_tokens_ref, wholes = refs[12:15], refs[15:17], refs[17], refs[18], refs[19:22]
+    ins, grad_pre_ref = refs[22:25], refs[25]
+    gather = PlaneGather(owns, wholes, owns[0].shape[0] // 2, *refs[26:29])
+    refs = refs[29:]
     pair, one, two, landing, staging = refs[:2], refs[2:4], refs[4:6], refs[6:8], refs[8:10]
     csend, crecv, psend, precv, zsend, zrecv, gsend, grecv = refs[10:18]
     line = LineSum(n, y_part, *refs[18:])
@@ -559,6 +630,7 @@
         )
 
     line.start()
+    gather.begin()
     D_rows = weight_ref.shape[0]
     query_width = grad_q_ref.shape[1]
     key_width = (weight_ref.shape[1] - query_width) // 2
@@ -632,6 +704,8 @@
     line.forward(1)
     for path in (0, 1):
         first(path).wait_recv()
+        if path == 1:
+            gather.second()
 
         def first_sum(t, carry):
             z, a = t // 2, t % 2
@@ -728,6 +802,8 @@
         for path in (0, 1):
             spread(path, stage).wait_recv()
 
+    gather.third()
+    gather.finish()
     for path in (0, 1):
         for stage in range(3):
             spread(path, stage).wait_send()
@@ -759,6 +835,7 @@
     grad_router,
     gain_two_row,
     y_part,
+    sums,
     n,
     collective_id,
 ):
@@ -772,18 +849,20 @@
     widths = [sum(p[2] for p in pieces if p[3]), sum(p[2] for p in pieces if not p[3])]
     scratch = [pltpu.VMEM((n, 2, 2, 2, eighth, w), BF) for w in array_widths]
     scratch += [pltpu.VMEM((grad_q.shape[0], width_all), BF)]
+    scratch += plane_gather_sems()
     scratch += [pltpu.VMEM((n, 2, 2, eighth, w), BF) for w in widths]
     scratch += [pltpu.VMEM((n, 2, eighth, w), BF) for w in widths]
     scratch += [pltpu.VMEM((n, eighth, w), BF) for w in widths]
     scratch += [pltpu.VMEM((2, n - 1, eighth, w), BF) for w in widths] * 2
     sems = [(4,), (4,), (2, 2), (2, 2), (2, 2, n - 1), (2, 2, n - 1), (2, 3), (2, 3)]
     y_rows = y_part.shape[0] // n
-    first, second, y_sum, grad_rest = pl.pallas_call(
+    first, second, y_sum, grad_rest, *wholes = pl.pallas_call(
         functools.partial(reduce_kernel, n, pieces),
         out_shape=[jax.ShapeDtypeStruct((2, 2, 2, eighth, w), BF) for w in widths]
-        + [jax.ShapeDtypeStruct(tokens.shape, F32)] * 2,
-        in_specs=[IN_VMEM] * 12,
-        out_specs=[IN_VMEM] * 4,
+        + [jax.ShapeDtypeStruct(tokens.shape, F32)] * 2
+        + plane_gather_shapes(sums),
+        in_specs=[IN_VMEM] * 15,
+        out_specs=[IN_VMEM] * 4 + [ANY] * 3,
         scratch_shapes=scratch
         + [pltpu.SemaphoreType.DMA(s) for s in sems]
         + line_sum_scratch(n, y_rows, y_part.shape[1]),
@@ -805,11 +884,12 @@
         grad_router,
         gain_two_row,
         y_part.reshape(n, y_rows, y_part.shape[1]),
+        *sums,
     )
     first, second = [o.reshape(rows, w) for o, w in zip((first, second), widths)]
     first = jnp.split(first, (query_width, query_width + key_width), axis=1)
     second = jnp.split(second, (key_width,), axis=1)
-    return first[0], first[1], second[0], second[1], first[2], y_sum, grad_rest
+    return first[0], first[1], second[0], second[1], first[2], y_sum, grad_rest, wholes
 
 
 def plane_tick(step, local):
@@ -1486,6 +1566,7 @@
 
 def attention_back_kernel(
     n,
+    plane,
     length_ref,
     q_ref,
     kv_ref,
@@ -1498,21 +1579,17 @@
     gain_ref,
     router_ref,
     out_weight_ref,
-    grad_q_ref,
-    grad_kv_ref,
-    grad_residual_ref,
-    grad_attn_ref,
-    grad_router_ref,
-    grad_gain_ref,
-    bias_ref,
-    grad_ref,
-    terms_ref,
-    landing,
-    staging,
-    send,
-    recv,
+    *refs,
 ):
+    owns, refs = refs[: 3 * plane], refs[3 * plane :]
+    grad_q_ref, grad_kv_ref, grad_residual_ref, grad_attn_ref, grad_router_ref, grad_gain_ref = refs[:6]
+    wholes, refs = refs[6 : 6 + 3 * plane], refs[6 + 3 * plane :]
+    bias_ref, grad_ref, terms_ref, landing, staging, send, recv = refs[:7]
     step, pairs = pl.program_id(0), pl.num_programs(0) - 1
+    partners = []
+    if plane:
+        gather = PlaneGather(owns, wholes, 0, *refs[7:])
+        partners = [(None, device) for device in gather.partners]
 
     def line(j):
         return LineSum(
@@ -1521,7 +1598,9 @@
 
     @pl.when(step == 0)
     def _():
-        greet(line(0).neighbours())
+        greet(line(0).neighbours() + partners)
+        if plane:
+            gather.begin()
         mask_bias(bias_ref, length_ref, q_ref.shape[1])
         routes = routes_ref[...]
         expert_id = lax.broadcasted_iota(jnp.int32, (routes.shape[0], EXPERTS), 1)
@@ -1552,6 +1631,11 @@
         for j in range(grad_ref.shape[0]):
             grad_ref[j] = grad_mixed[:, j * width : (j + 1) * width]
 
+    @pl.when(step == 2)
+    def _():
+        if plane:
+            gather.second()
+
     @pl.when(step < pairs)
     def _():
         attention_back_pair(
@@ -1564,6 +1648,12 @@
         for hop in range(1, n - 1):
             line(step - 1).forward(hop)
         line(step - 1).finish(grad_kv_ref)
+
+    @pl.when(step == pairs)
+    def _():
+        if plane:
+            gather.third()
+            gather.finish()
 
 
 def attention_back_pair(q_ref, kv_ref, grad_ref, log_total_ref, grad_q_ref, grad_kv_ref, bias_ref):
@@ -1589,13 +1679,14 @@
         put_heads(grad_q_ref, head, dot_tn(key, grad_scores) * scale)
 
 
-def attention_back(length, query, kv_all, log_total, sources, n, collective_id):
+def attention_back(length, query, kv_all, log_total, sources, sums, n, collective_id):
+    plane = len(sums) > 0
     rows, keys = query.shape[1], kv_all.shape[0]
     pairs, width = KEY_VALUE_HEADS // 2, 2 * LANES
     now = lambda j: jnp.minimum(j, pairs - 1)
     row_spec = pl.BlockSpec((rows, width), lambda j: (0, now(j)))
     return pl.pallas_call(
-        functools.partial(attention_back_kernel, n),
+        functools.partial(attention_back_kernel, n, plane),
         grid=(pairs + 1,),
         out_shape=(
             jax.ShapeDtypeStruct((rows, pairs * width), F32),
@@ -1604,19 +1695,21 @@
             jax.ShapeDtypeStruct((rows, D), BF),
             jax.ShapeDtypeStruct((D, LANES), F32),
             jax.ShapeDtypeStruct((1, D), F32),
-        ),
+        )
+        + (tuple(plane_gather_shapes(sums)) if plane else ()),
         in_specs=[
             pl.BlockSpec(memory_space=pltpu.SMEM),
             pl.BlockSpec((1, rows, width), lambda j: (now(j), 0, 0)),
             pl.BlockSpec((keys, width), lambda j: (0, now(j))),
             pl.BlockSpec((1, 2, 2 * rows), lambda j: (now(j), 0, 0)),
         ]
-        + [IN_VMEM] * len(sources),
+        + [IN_VMEM] * (len(sources) + len(sums)),
         out_specs=(
             row_spec,
             pl.BlockSpec((rows, width), lambda j: (0, jnp.maximum(j - 1, 0))),
         )
-        + (IN_VMEM,) * 4,
+        + (IN_VMEM,) * 4
+        + (ANY,) * len(sums),
         scratch_shapes=[
             pltpu.VMEM((keys, rows), F32),
             pltpu.VMEM((pairs, rows, width), BF),
@@ -1625,7 +1718,8 @@
             pltpu.VMEM((pairs, 2, n - 2, rows, width), BF),
             pltpu.SemaphoreType.DMA((pairs, 2, n - 1)),
             pltpu.SemaphoreType.DMA((pairs, 2, n - 1)),
-        ],
+        ]
+        + (plane_gather_sems() if plane else []),
         compiler_params=pltpu.CompilerParams(
             dimension_semantics=("arbitrary",),
             vmem_limit_bytes=60 * 1024 * 1024,
@@ -1636,26 +1730,37 @@
             flops=40 * rows * keys * D, bytes_accessed=100000000, transcendentals=0
         ),
         name="attention_back",
-    )(length, query, kv_all, log_total, *sources)
-
-
-def widen_kernel(value_ref, out_ref):
-    out_ref[...] = value_ref[...].astype(F32)
-
-
-def widen(value):
-    block = (1,) + value.shape[1:]
-    spec = pl.BlockSpec(block, lambda e: (e, 0, 0))
+    )(length, query, kv_all, log_total, *sources, *sums)
+
+
+def widen_kernel(count, *refs):
+    step = pl.program_id(0)
+    for i, ref in enumerate(refs[:-1]):
+
+        @pl.when((step >= i * count) & (step < (i + 1) * count))
+        def _():
+            refs[-1][...] = ref[...].astype(F32)
+
+
+def widen(values):
+    count = values[0].shape[0]
+    block = (1,) + values[0].shape[1:]
+
+    def spec(i):
+        return pl.BlockSpec(block, lambda e: (jnp.clip(e - i * count, 0, count - 1), 0, 0))
+
+    total = count * len(values)
+    size = total * block[1] * block[2]
     return pl.pallas_call(
-        widen_kernel,
-        grid=(value.shape[0],),
-        out_shape=jax.ShapeDtypeStruct(value.shape, F32),
-        in_specs=[spec],
-        out_specs=spec,
+        functools.partial(widen_kernel, count),
+        grid=(total,),
+        out_shape=jax.ShapeDtypeStruct((total,) + block[1:], F32),
+        in_specs=[spec(i) for i in range(len(values))],
+        out_specs=pl.BlockSpec(block, lambda e: (e, 0, 0)),
         compiler_params=pltpu.CompilerParams(dimension_semantics=("arbitrary",)),
-        cost_estimate=pl.CostEstimate(flops=0, bytes_accessed=6 * value.size, transcendentals=0),
+        cost_estimate=pl.CostEstimate(flops=0, bytes_accessed=6 * size, transcendentals=0),
         name="widen",
-    )(value)
+    )(*values)
 
 
 def unpair_columns(value):
@@ -1747,11 +1852,12 @@
         router,
         out_weight,
     )
-    grad_query_acc, kv_gradient, grad_residual, grad_attn, grad_router, gain_two_row = (
-        attention_back(lengths, query_pairs, kv_all, log_total, sources, n, 5)
+    sums = (grad_gate, grad_up, grad_down) if plane else ()
+    grad_query_acc, kv_gradient, grad_residual, grad_attn, grad_router, gain_two_row, *low = (
+        attention_back(lengths, query_pairs, kv_all, log_total, sources, sums, n, 5)
     )
     if plane:
-        *shares, expert_sum, grad_rest = reduce_weights(
+        *shares, expert_sum, grad_rest, high = reduce_weights(
             grad_query_acc,
             kv_gradient,
             tokens,
@@ -1764,6 +1870,7 @@
             grad_router,
             gain_two_row,
             y_part,
+            sums,
             n,
             6,
         )
@@ -1800,10 +1907,15 @@
     shares = [share.astype(F32) for share in shares]
     share_query, share_key, share_value, share_out, share_small = shares
 
-    def sum_over_groups(value):
-        if not plane:
+    if plane:
+        widths = (FF, FF, D)
+        halves = [[h.reshape(h.shape[0], -1, w) for h in p] for *p, w in zip(low, high, widths)]
+        grad_experts = [widen(pair) for pair in halves]
+    else:
+        grad_experts = []
+        for value in (grad_gate, grad_up, grad_down):
             value = lax.psum_scatter(value, "group", scatter_dimension=1, tiled=True)
-        return widen(lax.all_gather(value, "group", axis=1, tiled=True))
+            grad_experts.append(widen([lax.all_gather(value, "group", axis=1, tiled=True)]))
 
     return (
         mixed,
@@ -1815,9 +1927,7 @@
         share_out,
         share_small[:, EXPERTS + 1],
         share_small[:, :EXPERTS],
-        sum_over_groups(grad_gate),
-        sum_over_groups(grad_up),
-        sum_over_groups(grad_down),
+        *grad_experts,
     )
 
 

time: 494 us -> 511 us (1.034)
  Pallas kernels: 459 us -> 491 us
  between operations: 14.6 us -> 1.46 us
    pallas_call x1, Pallas kernels: 104 us -> 123 us  [reduce_weights(): pl.pallas_call(functools.partial(reduce_kernel, n, pieces), out_shape=[ja...]
    pallas_call x4, Pallas kernels: 87.7 us -> 101 us  [the longest x1 68.5 us: attention_back(): pl.pallas_call(functools.partial(attention_back_kernel, n, plane), grid=(...]
  transfers between devices with their start and end apart: 3 -> 0, of which waited for: 0 -> 0; matrix products, arithmetic and copies ran while one was open for 2% -> 0% of each run, Pallas kernels for 37% -> 0%
where the time goes in v4:
time: 511 us; the launch traced here: 510 us
  Pallas kernels  491 us (96%)
  other arithmetic  11.1 us (2%)
  local copies, waits for them, and re-layouts  6.44 us (1%)
    pallas_call x1, Pallas kernels, run_experts(): pl.pallas_call(functools.partial(expert_kernel, sizes, plane), grid=(loca...  158 us
    pallas_call x1, Pallas kernels, reduce_weights(): pl.pallas_call(functools.partial(reduce_kernel, n, pieces), out_shape=[ja...  123 us
    pallas_call x1, Pallas kernels, attention_back(): pl.pallas_call(functools.partial(attention_back_kernel, n, plane), grid=(...  68.5 us
    pallas_call x1, Pallas kernels, gather_weights(): pl.pallas_call(functools.partial(weights_kernel, n, pieces, widths), out_...  64.2 us
    pallas_call x1, Pallas kernels, attention(): pl.pallas_call(functools.partial(attention_kernel, n), grid=(pairs,), out...  44 us
    pallas_call x3, Pallas kernels, widen(): pl.pallas_call(functools.partial(widen_kernel, count), grid=(total,), out...  32.8 us

profile of v4, /device:TPU:0, one launch (start us, length us, event | category | flops | bytes accessed | tf_op | source)
XLA Modules:
  0.0 510.2 jit_solution(1893653879159061080)
XLA Ops:
  1.3 0.7 fusion.3
  2.0 0.8 copy.31
  2.9 0.7 pad.8.refs_4_
  3.7 0.8 copy.34.sine_ref.refs_6_
  4.5 1.5 copy.35.routes_ref
  6.0 0.8 copy.33.cosine_ref.refs_5_
  6.8 1.1 broadcast_select_fusion.ct_ref
  7.9 0.9 pad_maximum_fusion.refs_5_
  8.8 64.2 %gather_weights.1 = (bf16[4,2,2,2,32,2048]{5,4,3,2,1,0:T(8,128)(2,1)}, bf16[4,2,2,2,32,1024]{5,4,3,2,1,0:T(8,128)(2,1)}, bf16[4,2,2,2,32,128]{5,4,3,2,1,0:T(8,128)(2,1)}, bf16[4,272,1024]{2,1,0:T(8,128)(2,1)}) custom-call(bf16[256,1024]{1,0:T(8,128)(2,1)} %refs_0_.1, bf16[256,512]{1,0:T(8,128)(2,1)} %refs_1_.2, bf16[256,512]{1,0:T(8,128)(2,1)} %refs_2_.2, ...), custom_call_target="tpu_custom_call" | custom-call | bytes 100000000 | tf_op jit(solution)/shard_map/gather_weights/pallas_call | solution.py:560
  73.0 0.8 convert_reduce_fusion
  73.8 0.6 copy.41
  74.4 44.0 %attention.1 = (bf16[256,1024]{1,0:T(8,128)(2,1)}, f32[4,2,512]{2,1,0:T(2,128)}, bf16[1024,1024]{1,0:T(8,128)(2,1)}, bf16[4,256,256]{2,1,0:T(8,128)(2,1)}, bf16[4,32,256]{2,1,0:T(8,128)(2,1)}) custom-call(s32[1]{0:T(128)} %copy.42.length_ref, bf16[256,1024]{1,0:T(8,128)(2,1)} %refs_2_.3, f32[2,1024]{1,0:T(2,128)} %bitcast.41, bf16[1024,2048]{1,0:T(8,128)(2,1)} %bitcast.24, ...), custom_call_target="tpu_custom_call" | custom-call | flops 4294967296 | bytes 100000000 | tf_op jit(solution)/shard_map/attention/pallas_call | solution.py:1525
  118.5 158.4 %experts.1 = (bf16[1024,1024]{1,0:T(8,128)(2,1)}, f32[256,1152]{1,0:T(8,128)}, bf16[8,128,512]{2,1,0:T(8,128)(2,1)}, bf16[8,128,512]{2,1,0:T(8,128)(2,1)}, bf16[...) custom-call(bf16[256,1024]{1,0:T(8,128)(2,1)} %get-tuple-element.46.refs_0_.refs_7_, ...), custom_call_target="tpu_custom_call" | custom-call | flops 30601641984 | bytes 58720256 | tf_op jit(solution)/shard_map/experts/pallas_call | solution.py:1295
  276.9 68.5 %attention_back.1 = (f32[256,1024]{1,0:T(8,128)}, bf16[256,1024]{1,0:T(8,128)(2,1)}, f32[256,1024]{1,0:T(8,128)}, bf16[256,1024]{1,0:T(8,128)(2,1)}, f32[1024,12...) custom-call(s32[1]{0:T(128)} %copy.42.length_ref, ...), custom_call_target="tpu_custom_call" | custom-call | flops 10737418240 | bytes 100000000 | tf_op jit(solution)/shard_map/attention_back/pallas_call | solution.py:1688
  345.4 123.3 %reduce_weights.1 = (bf16[2,2,2,32,1664]{4,3,2,1,0:T(8,128)(2,1)}, bf16[2,2,2,32,1536]{4,3,2,1,0:T(8,128)(2,1)}, f32[256,1024]{1,0:T(8,128)}, f32[256,1024]{1,0:...) custom-call(f32[256,1024]{1,0:T(8,128)} %get-tuple-element.59.refs_0, ...), custom_call_target="tpu_custom_call" | custom-call | bytes 100000000 | tf_op jit(solution)/shard_map/reduce_weights/pallas_call | solution.py:859
  468.7 2.3 add_convert_fusion
  471.0 2.4 add.26
  473.5 0.6 fusion.6
  474.1 0.6 slice.18
  474.7 1.1 slice_convert_fusion.2
  475.8 1.6 slice_convert_fusion
  477.4 10.9 %widen.3 = f32[8,1024,512]{2,1,0:T(8,128)} custom-call(bf16[4,1024,512]{2,1,0:T(8,128)(2,1)} %bitcast.28, bf16[4,1024,512]{2,1,0:T(8,128)(2,1)} %bitcast.31), custom_call_target="tpu_custom_call" | custom-call | bytes 25165824 | tf_op jit(solution)/shard_map/widen/pallas_call | solution.py:1754
  488.3 10.9 %widen.4 = f32[8,1024,512]{2,1,0:T(8,128)} custom-call(bf16[4,1024,512]{2,1,0:T(8,128)(2,1)} %bitcast.27, bf16[4,1024,512]{2,1,0:T(8,128)(2,1)} %bitcast.30), custom_call_target="tpu_custom_call" | custom-call | bytes 25165824 | tf_op jit(solution)/shard_map/widen/pallas_call | solution.py:1754
  499.3 10.9 %widen.5 = f32[8,512,1024]{2,1,0:T(8,128)} custom-call(bf16[4,512,1024]{2,1,0:T(8,128)(2,1)} %bitcast.26, bf16[4,512,1024]{2,1,0:T(8,128)(2,1)} %bitcast.29), custom_call_target="tpu_custom_call" | custom-call | bytes 25165824 | tf_op jit(solution)/shard_map/widen/pallas_call | solution.py:1754
  (20 shorter events, 0.4 us)
Async XLA Ops:
  7.9 110.6 %copy-start = (bf16[256,1024]{1,0:T(8,128)(2,1)}, bf16[256,1024]{1,0:T(8,128)(2,1)S(1)}, u32[]{:S(2)}) copy-start(bf16[256,1024]{1,0:T(8,128)(2,1)S(1)} %broadcast_select_fusion.ct_ref) | copy-start | bytes 1572868
  345.4 123.3 %copy-start.2 = (f32[256,1024]{1,0:T(8,128)S(1)}, f32[256,1024]{1,0:T(8,128)}, u32[]{:S(2)}) copy-start(f32[256,1024]{1,0:T(8,128)} %get-tuple-element.50.residual_ref) | copy-start | bytes 3145732
  345.4 125.6 %copy-start.1 = (f32[256,1024]{1,0:T(8,128)S(1)}, f32[256,1024]{1,0:T(8,128)}, u32[]{:S(2)}) copy-start(f32[256,1024]{1,0:T(8,128)} %get-tuple-element.66) | copy-start | bytes 3145732
  468.7 4.7 copy-start.3
  468.7 6.0 %copy-start.4 = (bf16[2,2,2,32,1536]{4,3,2,1,0:T(8,128)(2,1)S(1)}, bf16[2,2,2,32,1536]{4,3,2,1,0:T(8,128)(2,1)}, u32[]{:S(2)}) copy-start(bf16[2,2,2,32,1536]{4,3,2,1,0:T(8,128)(2,1)} %get-tuple-element.69) | copy-start | bytes 2359300

commit v5 on v3

--- a/solution.py
+++ b/solution.py
@@ -346,14 +346,16 @@
     def sends(step, side):
         return (me - step >= 0) & (me < n - 1) if side == 0 else (me + step < n) & (me > 0)
 
-    def extra_hop(step, side):
+    def extra_hop(part, step, side):
         block = me - step if side == 0 else me + step
-        source = extra if step == 0 else extra_out.at[block]
+        middle = extra.shape[1] // 2
+        columns = slice(part * middle, (part + 1) * middle)
+        source = extra.at[:, columns] if step == 0 else extra_out.at[block, :, columns]
         return remote(
             source,
-            extra_out.at[block],
-            xsend.at[side, step],
-            xrecv.at[side, step],
+            extra_out.at[block, :, columns],
+            xsend.at[part, side, step],
+            xrecv.at[part, side, step],
             right if side == 0 else left,
         )
 
@@ -384,20 +386,20 @@
             return [(0, me, me >= 0)]
         return [(step, me - step, me - step >= 0), (n - 1 + step, me + step, me + step < n)]
 
-    def extra_step(far):
+    def extra_step(part, far):
         for side in (0, 1):
             if far > 0:
 
                 @pl.when(me - far >= 0 if side == 0 else me + far < n)
                 def _():
-                    extra_hop(far - 1, side).wait_recv()
+                    extra_hop(part, far - 1, side).wait_recv()
 
         for side in (0, 1):
             if far < n - 1:
 
                 @pl.when(sends(far, side))
                 def _():
-                    extra_hop(far, side).start()
+                    extra_hop(part, far, side).start()
 
     count = len(pieces)
     for step in range(n + 2):
@@ -444,12 +446,9 @@
                     for i in range(3):
                         third(slot, block, i).start()
 
-        if step == 1:
-            extra_step(0)
-        elif step >= n:
-            extra_step(step - n + 1)
-    for far in range(3, n):
-        extra_step(far)
+        for part in (0, 1):
+            if 0 <= step - 1 - part < n:
+                extra_step(part, step - 1 - part)
 
     for step in range(n):
         for slot, block, there in held(step):
@@ -469,7 +468,8 @@
                 def _():
                     for i in range(3):
                         hop(i, step, side).wait_send()
-                    extra_hop(step, side).wait_send()
+                    for part in (0, 1):
+                        extra_hop(part, step, side).wait_send()
 
 
 def path_pieces(query_width, key_width, out_width, small_width):
@@ -503,8 +503,8 @@
             pltpu.SemaphoreType.DMA((2, 2 * n - 1, 4)),
             pltpu.SemaphoreType.DMA((2 * n - 1, 3)),
             pltpu.SemaphoreType.DMA((2 * n - 1, 3)),
-            pltpu.SemaphoreType.DMA((2, n - 1)),
-            pltpu.SemaphoreType.DMA((2, n - 1)),
+            pltpu.SemaphoreType.DMA((2, 2, n - 1)),
+            pltpu.SemaphoreType.DMA((2, 2, n - 1)),
         ],
         compiler_params=pltpu.CompilerParams(collective_id=collective_id, has_side_effects=True),
         cost_estimate=pl.CostEstimate(flops=0, bytes_accessed=100000000, transcendentals=0),

time: 494 us -> 492 us (level)
  no operation moved by 1% of the time
where the time goes in v5:
time: 492 us; the launch traced here: 491 us
  Pallas kernels  456 us (93%)
  between operations  14.6 us (3%)
  other arithmetic  11.3 us (2%)
  local copies, waits for them, and re-layouts  7.46 us (2%)
    pallas_call x1, Pallas kernels, run_experts(): pl.pallas_call(functools.partial(expert_kernel, sizes, plane), grid=(loca...  160 us
    pallas_call x1, Pallas kernels, reduce_weights(): pl.pallas_call(functools.partial(reduce_kernel, n, pieces), out_shape=[ja...  102 us
    pallas_call x1, Pallas kernels, gather_weights(): pl.pallas_call(functools.partial(weights_kernel, n, pieces, widths), out_...  60 us
    pallas_call x1, Pallas kernels, attention_back(): pl.pallas_call(functools.partial(attention_back_kernel, n), grid=(pairs +...  58.3 us
    pallas_call x1, Pallas kernels, attention(): pl.pallas_call(functools.partial(attention_kernel, n), grid=(pairs,), out...  44.9 us
    pallas_call x3, Pallas kernels, widen(): pl.pallas_call(widen_kernel, grid=(value.shape[0],), out_shape=jax.ShapeD...  31.2 us
  transfers between devices with their start and end apart: 3, of which 0 were waited for; matrix products, arithmetic and copies ran while one was open for 2% of the time, Pallas kernels for 37%

profile of v5, /device:TPU:0, one launch (start us, length us, event | category | flops | bytes accessed | tf_op | source)
XLA Modules:
  0.0 491.2 jit_solution(14897101777096365935)
XLA Ops:
  7.9 0.8 copy.31
  9.0 0.8 copy.34.sine_ref.refs_6_
  9.7 1.5 copy.35.routes_ref
  11.2 0.8 copy.33.cosine_ref.refs_5_
  12.0 0.7 fusion.3
  12.7 0.6 pad.8.refs_4_
  13.3 1.1 broadcast_select_fusion.ct_ref
  14.5 0.9 pad_maximum_fusion.refs_5_
  15.4 60.0 %gather_weights.1 = (bf16[4,2,2,2,32,2048]{5,4,3,2,1,0:T(8,128)(2,1)}, bf16[4,2,2,2,32,1024]{5,4,3,2,1,0:T(8,128)(2,1)}, bf16[4,2,2,2,32,128]{5,4,3,2,1,0:T(8,128)(2,1)}, bf16[4,272,1024]{2,1,0:T(8,128)(2,1)}) custom-call(bf16[256,1024]{1,0:T(8,128)(2,1)} %refs_0_.1, bf16[256,512]{1,0:T(8,128)(2,1)} %refs_1_.2, bf16[256,512]{1,0:T(8,128)(2,1)} %refs_2_.2, ...), custom_call_target="tpu_custom_call" | custom-call | bytes 100000000 | tf_op jit(solution)/shard_map/gather_weights/pallas_call | solution.py:490
  75.4 0.8 convert_reduce_fusion
  76.8 44.9 %attention.1 = (bf16[256,1024]{1,0:T(8,128)(2,1)}, f32[4,2,512]{2,1,0:T(2,128)}, bf16[1024,1024]{1,0:T(8,128)(2,1)}, bf16[4,256,256]{2,1,0:T(8,128)(2,1)}, bf16[4,32,256]{2,1,0:T(8,128)(2,1)}) custom-call(s32[1]{0:T(128)} %copy.42.length_ref, bf16[256,1024]{1,0:T(8,128)(2,1)} %refs_2_.3, f32[2,1024]{1,0:T(2,128)} %bitcast.29, bf16[1024,2048]{1,0:T(8,128)(2,1)} %bitcast.18, ...), custom_call_target="tpu_custom_call" | custom-call | flops 4294967296 | bytes 100000000 | tf_op jit(solution)/shard_map/attention/pallas_call | solution.py:1445
  121.7 159.5 %experts.1 = (bf16[1024,1024]{1,0:T(8,128)(2,1)}, f32[256,1152]{1,0:T(8,128)}, bf16[8,128,512]{2,1,0:T(8,128)(2,1)}, bf16[8,128,512]{2,1,0:T(8,128)(2,1)}, bf16[...) custom-call(bf16[256,1024]{1,0:T(8,128)(2,1)} %get-tuple-element.40.refs_0_.refs_7_, ...), custom_call_target="tpu_custom_call" | custom-call | flops 30601641984 | bytes 58720256 | tf_op jit(solution)/shard_map/experts/pallas_call | solution.py:1215
  281.3 0.7 all-gather.6.cloned.1.call-update
  282.0 0.7 all-gather.4.cloned.1.call-update
  282.7 58.3 %attention_back.1 = (f32[256,1024]{1,0:T(8,128)}, bf16[256,1024]{1,0:T(8,128)(2,1)}, f32[256,1024]{1,0:T(8,128)}, bf16[256,1024]{1,0:T(8,128)(2,1)}, f32[1024,128]{1,0:T(8,128)}, /*index=5*/f32[1,1024]{1,0:T(1,128)}) custom-call(s32[1]{0:T(128)} %copy.42.length_ref, bf16[4,256,256]{2,1,0:T(8,128)(2,1)} %get-tuple-element.45.q_ref, ...), custom_call_target="tpu_custom_call" | custom-call | flops 10737418240 | bytes 100000000 | tf_op jit(solution)/shard_map/attention_back/pallas_call | solution.py:1597
  341.0 102.5 %reduce_weights.1 = (bf16[2,2,2,32,1664]{4,3,2,1,0:T(8,128)(2,1)}, bf16[2,2,2,32,1536]{4,3,2,1,0:T(8,128)(2,1)}, f32[256,1024]{1,0:T(8,128)}, f32[256,1024]{1,0:T(8,128)}) custom-call(f32[256,1024]{1,0:T(8,128)} %get-tuple-element.50.refs_0_, bf16[256,1024]{1,0:T(8,128)(2,1)} %get-tuple-element.51.refs_1_, bf16[256,1024]{1,0:T(8,128)(2,1)} %refs_2_.3, ...), custom_call_target="tpu_custom_call" | custom-call | bytes 100000000 | tf_op jit(solution)/shard_map/reduce_weights/pallas_call | solution.py:781
  443.5 1.0 split.20
  445.3 2.9 add.26
  448.8 2.1 slice_convert_fusion.2
  450.9 0.9 add_convert_fusion
  451.9 1.6 slice_convert_fusion
  453.5 10.6 %widen.5 = f32[8,512,1024]{2,1,0:T(8,128)} custom-call(bf16[8,512,1024]{2,1,0:T(8,128)(2,1)} %all-gather.8.cloned.1.call-done.value_ref), custom_call_target="tpu_custom_call" | custom-call | bytes 25165824 | tf_op jit(solution)/shard_map/widen/pallas_call | solution.py:1649
  464.0 10.3 %widen.4 = f32[8,1024,512]{2,1,0:T(8,128)} custom-call(bf16[8,1024,512]{2,1,0:T(8,128)(2,1)} %all-gather.6.cloned.1.call-done.value_ref), custom_call_target="tpu_custom_call" | custom-call | bytes 25165824 | tf_op jit(solution)/shard_map/widen/pallas_call | solution.py:1649
  474.4 10.3 %widen.3 = f32[8,1024,512]{2,1,0:T(8,128)} custom-call(bf16[8,1024,512]{2,1,0:T(8,128)(2,1)} %all-gather.4.cloned.1.call-done.value_ref), custom_call_target="tpu_custom_call" | custom-call | bytes 25165824 | tf_op jit(solution)/shard_map/widen/pallas_call | solution.py:1649
  (31 shorter events, 2.3 us)
Async XLA Ops:
  7.2 446.3 %all-gather.8.cloned.1.call-start = ((), (), s32[]{:S(2)}) async-start(), calls=%async_computation.2 | async-start | bytes 9437184 | tf_op jit(solution)/shard_map/all_gather | solution.py:1806
  14.5 107.2 %copy-start = (bf16[256,1024]{1,0:T(8,128)(2,1)}, bf16[256,1024]{1,0:T(8,128)(2,1)S(1)}, u32[]{:S(2)}) copy-start(bf16[256,1024]{1,0:T(8,128)(2,1)S(1)} %broadcast_select_fusion.ct_ref) | copy-start | bytes 1572868
  281.2 182.8 %all-gather.6.cloned.1.call-start = ((), (), s32[]{:S(2)}) async-start(), calls=%async_computation.1 | async-start | bytes 9437184 | tf_op jit(solution)/shard_map/all_gather | solution.py:1806
  282.0 192.4 %all-gather.4.cloned.1.call-start = ((), (), s32[]{:S(2)}) async-start(), calls=%async_computation | async-start | bytes 9437184 | tf_op jit(solution)/shard_map/all_gather | solution.py:1806
  341.0 104.3 %copy-start.1 = (f32[256,1024]{1,0:T(8,128)S(1)}, f32[256,1024]{1,0:T(8,128)}, u32[]{:S(2)}) copy-start(f32[256,1024]{1,0:T(8,128)} %get-tuple-element.57) | copy-start | bytes 3145732
  443.5 7.4 %copy-start.2 = (f32[256,1024]{1,0:T(8,128)S(1)}, f32[256,1024]{1,0:T(8,128)}, u32[]{:S(2)}) copy-start(f32[256,1024]{1,0:T(8,128)} %get-tuple-element.44.residual_ref) | copy-start | bytes 3145732
  443.5 7.4 %copy-start.3 = (f32[256,1024]{1,0:T(8,128)S(1)}, f32[256,1024]{1,0:T(8,128)}, u32[]{:S(2)}) copy-start(f32[256,1024]{1,0:T(8,128)} %get-tuple-element.56) | copy-start | bytes 3145732
  444.7 7.2 %copy-start.4 = (bf16[2,2,2,32,1664]{4,3,2,1,0:T(8,128)(2,1)S(1)}, bf16[2,2,2,32,1664]{4,3,2,1,0:T(8,128)(2,1)}, u32[]{:S(2)}) copy-start(bf16[2,2,2,32,1664]{4,3,2,1,0:T(8,128)(2,1)} %get-tuple-element.59) | copy-start | bytes 2555908
  444.7 7.2 %copy-start.5 = (bf16[2,2,2,32,1536]{4,3,2,1,0:T(8,128)(2,1)S(1)}, bf16[2,2,2,32,1536]{4,3,2,1,0:T(8,128)(2,1)}, u32[]{:S(2)}) copy-start(bf16[2,2,2,32,1536]{4,3,2,1,0:T(8,128)(2,1)} %get-tuple-element.60) | copy-start | bytes 2359300
Sparse Core Ops, SparseCore 0:
  281.3 52.3 all-gather.7
  335.6 72.8 all-gather.5
  410.3 60.2 all-gather.3
